TPU v7x, 512 devices: a whole 4x8x8 slice. The times are simulated.
512 devices in a mesh: frame: 32 (over x, z), patch: 16 (over y, core).
Axes of the slice: x: 4, y: 8, z: 8, core: 2. Of those that a mesh axis runs over, the one named last changes fastest.
Arguments:
- coeffs: float32 [16, 16, 32, 36], P('patch', None, 'frame'), may hold values from -1.8 to 1.8
- shifts: int32 [16, 16, 32, 2], P('patch', None, 'frame'), may hold values from -4 to 4
- pixels: bfloat16 [16, 16, 32, 128, 128], P('patch', None, 'frame'), may hold values from -6 to 6
- pupil_mask: int32 [64, 64], replicated, may hold values from 0 to 1, as said below
- chan_map: int32 [16], replicated, may hold values from 0 to 1, as said below
- intersection: int32 [16, 32], P('patch', 'frame'), may hold values from 4 to 16
Outputs:
- blended: float32 [2, 1536, 3072], P(None, 'patch', 'frame')
- coeff_grad: float32 [16, 16, 32, 36], P('patch', None, 'frame')
Inputs may be any that keep to these rules, and one draw needn't show every extreme that they name: pupil_mask is 1 exactly on the cells whose centres lie in the disc of diameter 64 about the grid's centre, outside a central disc whose radius in cells is drawn from 8 to 21, and off one row and one column of cells (support vanes) whose positions are drawn from 0 to 63. `chan_map`: every channel is named by exactly 8 slots.
All inputs are finite; a program needn't handle non-finite values.
Results may differ from a plain program's by a relative error of at most 0.0003.
Values may be sent and summed in bfloat16 or wider, within the bound.
No kernel may reach another device: no remote copies, remote signals or barrier semaphores. Data moves between devices by JAX's collectives and lax.ppermute only.
A program may use at most 64 MiB of HBM per device.

v0:
```python
import math

import jax
import jax.numpy as jnp
from jax import lax
from jax.sharding import PartitionSpec as P

CHANNELS = 2
MARGIN = 16


highest = lax.Precision.HIGHEST
regular_gamma = 0.1
wave_ratio = 0.35


def padded(cells, sides, width):
    for axis, dim in sides:
        count = lax.axis_size(axis)
        ends = count - 1
        head = lax.slice_in_dim(cells, 0, width, axis=dim)
        tail = lax.slice_in_dim(cells, cells.shape[dim] - width, cells.shape[dim], axis=dim)
        cells = jnp.concatenate(
            [
                lax.ppermute(tail, axis, [(i, (i + 1) % count) for i in range(ends)]),
                cells,
                lax.ppermute(head, axis, [((i + 1) % count, i) for i in range(ends)]),
            ],
            axis=dim,
        )
    return cells


def product(form, left, right):
    return jnp.einsum(form, left, right, precision=highest)


def noll_order(noll_index):
    radial = 0
    remain = noll_index - 1
    while remain > radial:
        radial += 1
        remain -= radial
    azimuth = radial % 2 + 2 * ((remain + (radial + 1) % 2) // 2)
    if noll_index % 2 == 1:
        azimuth = -azimuth
    return (radial, azimuth)


def zernike_basis(mode_count, pupil_side):
    position = (
        jnp.arange(pupil_side, dtype=jnp.int32).astype(jnp.float32) - (pupil_side - 1) / 2.0
    ) / (pupil_side / 2.0)
    grid_y = position[:, None] + jnp.zeros((1, pupil_side), jnp.float32)
    grid_x = jnp.zeros((pupil_side, 1), jnp.float32) + position[None, :]
    radius = jnp.sqrt(grid_x * grid_x + grid_y * grid_y)
    angle_map = jnp.arctan2(grid_y, grid_x)
    collected = []
    for noll_index in range(2, mode_count + 2):
        radial, azimuth = noll_order(noll_index)
        order_abs = abs(azimuth)
        radial_sum = jnp.zeros_like(radius)
        for power_step in range((radial - order_abs) // 2 + 1):
            factor = math.factorial(radial - power_step) / (
                math.factorial(power_step)
                * math.factorial((radial + order_abs) // 2 - power_step)
                * math.factorial((radial - order_abs) // 2 - power_step)
            )
            if power_step % 2 == 1:
                factor = -factor
            radial_sum = radial_sum + factor * radius ** (radial - 2 * power_step)
        if azimuth == 0:
            shaped = radial_sum * math.sqrt(radial + 1.0)
        elif azimuth > 0:
            shaped = radial_sum * math.sqrt(2.0 * (radial + 1.0)) * jnp.cos(order_abs * angle_map)
        else:
            shaped = radial_sum * math.sqrt(2.0 * (radial + 1.0)) * jnp.sin(order_abs * angle_map)
        collected.append(shaped.reshape(-1))
    return jnp.stack(collected)


def dft_tables(length, width):
    frequency = jnp.arange(length, dtype=jnp.int32)[:, None]
    position = jnp.arange(width, dtype=jnp.int32)[None, :]
    turns = (frequency * position % length).astype(jnp.float32) * (2.0 * math.pi / length)
    return (jnp.cos(turns), -jnp.sin(turns))


def complex_tables(length, width):
    table_re, table_im = dft_tables(length, width)
    right_table = jnp.stack([jnp.stack([table_re, table_im]), jnp.stack([-table_im, table_re])])
    left_table = jnp.stack([jnp.stack([table_re, -table_im]), jnp.stack([table_im, table_re])])
    return (right_table, left_table)


def real_transform(image, length):
    right_table, left_table = complex_tables(length, length)
    inner = product("bxy,tvy->tbxv", image, right_table[0])
    return product("tsux,sbxv->tbuv", left_table, inner)


def build_otf(coeff_in, scale_in, shift_in, zernike, mask_flat, length):
    pupil_side = length // 2
    batch_size = coeff_in.shape[0]
    phase_map = jnp.dot(coeff_in, zernike, precision=highest) * scale_in[:, None]
    pupil = jnp.stack([mask_flat * jnp.cos(phase_map), mask_flat * jnp.sin(phase_map)]).reshape(
        2, batch_size, pupil_side, pupil_side
    )
    right_table, left_table = complex_tables(length, pupil_side)
    half = product("sbxy,stvy->tbxv", pupil, right_table)
    field = product("tsux,sbxv->tbuv", left_table, half)
    intensity = field[0] * field[0] + field[1] * field[1]
    point_spread = intensity / jnp.sum(intensity, axis=(1, 2), keepdims=True)
    otf = real_transform(point_spread, length)
    frequency = jnp.arange(length, dtype=jnp.int32).astype(jnp.float32)
    angle_y = 2.0 * math.pi / length * shift_in[:, 0:1] * frequency[None, :]
    angle_x = 2.0 * math.pi / length * shift_in[:, 1:2] * frequency[None, :]
    total_angle = angle_y[:, :, None] + angle_x[:, None, :]
    tilt_re = jnp.cos(total_angle)
    tilt_im = -jnp.sin(total_angle)
    return jnp.stack([otf[0] * tilt_re - otf[1] * tilt_im, otf[0] * tilt_im + otf[1] * tilt_re])


def data_spectrum(pixel_in, length, margin):
    position = jnp.arange(length, dtype=jnp.int32)
    distance = jnp.minimum(position, length - 1 - position).astype(jnp.float32)
    taper_row = jnp.where(
        distance < margin, 0.5 - 0.5 * jnp.cos(math.pi * (distance + 0.5) / margin), 1.0
    )
    image = pixel_in.astype(jnp.float32) * taper_row[:, None] * taper_row[None, :]
    return real_transform(image, length)


def wiener_terms(otf, spec, onehot, length):
    otf_re, otf_im = (otf[0], otf[1])
    spec_re, spec_im = (spec[0], spec[1])
    cross_re = otf_re * spec_re + otf_im * spec_im
    cross_im = otf_re * spec_im - otf_im * spec_re
    intensity = otf_re * otf_re + otf_im * otf_im
    num_re = product("kc,kbuv->cbuv", onehot, cross_re)
    num_im = product("kc,kbuv->cbuv", onehot, cross_im)
    denominator = product("kc,kbuv->cbuv", onehot, intensity) + regular_gamma
    obj_re = num_re / denominator
    obj_im = num_im / denominator
    per_re = product("kc,cbuv->kbuv", onehot, obj_re)
    per_im = product("kc,cbuv->kbuv", onehot, obj_im)
    res_re = spec_re - (per_re * otf_re - per_im * otf_im)
    res_im = spec_im - (per_re * otf_im + per_im * otf_re)
    loss_scale = 1.0 / float(length * length * length)
    grad_re = -2.0 * loss_scale * (res_re * per_re + res_im * per_im)
    grad_im = 2.0 * loss_scale * (res_re * per_im - res_im * per_re)
    return (obj_re, obj_im, jnp.stack([grad_re, grad_im]))


def object_image(obj_re, obj_im, length):
    full_re, full_im = dft_tables(length, length)
    back_re = product("ux,bxv->buv", full_re, obj_re) + product("ux,bxv->buv", full_im, obj_im)
    back_im = product("ux,bxv->buv", full_re, obj_im) - product("ux,bxv->buv", full_im, obj_re)
    return (product("bux,vx->buv", back_re, full_re) + product("bux,vx->buv", back_im, full_im)) / (
        length * length
    )


def window_weight(width_in, length):
    position = jnp.arange(length, dtype=jnp.int32)
    distance = (jnp.minimum(position, length - 1 - position) + 1).astype(jnp.float32)
    ramp_row = jnp.minimum(1.0, distance / (width_in.astype(jnp.float32) + 1.0))
    return ramp_row[:, None] * ramp_row[None, :]


def fold_margins(extended, axis_num, margin):
    span = extended.shape[axis_num] - 4 * margin
    upper_part = lax.slice_in_dim(extended, 0, margin, axis=axis_num)
    middle = lax.slice_in_dim(extended, 2 * margin, 2 * margin + span, axis=axis_num)
    lower_part = lax.slice_in_dim(extended, span + 3 * margin, span + 4 * margin, axis=axis_num)
    pad_upper = [(0, 0)] * extended.ndim
    pad_lower = [(0, 0)] * extended.ndim
    pad_upper[axis_num] = (0, span - margin)
    pad_lower[axis_num] = (span - margin, 0)
    return middle + jnp.pad(upper_part, pad_upper) + jnp.pad(lower_part, pad_lower)


def per_device(coeffs, shifts, pixels, pupil_mask, chan_map, intersection):
    mode_count = coeffs.shape[3]
    length = pixels.shape[3]
    margin = MARGIN
    channels = CHANNELS
    small = jnp.concatenate([coeffs, shifts.astype(jnp.float32)], axis=3)
    small = lax.all_to_all(small, "patch", split_axis=1, concat_axis=0, tiled=True)
    slots = small.shape[0]
    small = small.reshape(slots, mode_count + 2)
    coeff_all = small[:, :mode_count]
    shift_all = small[:, mode_count:]
    frames = lax.all_to_all(pixels, "patch", split_axis=1, concat_axis=0, tiled=True)
    frames = frames.reshape(slots, length, length)
    zernike = zernike_basis(mode_count, length // 2)
    mask_flat = pupil_mask.reshape(-1).astype(jnp.float32)
    scale_all = 1.0 / (1.0 + wave_ratio * chan_map.astype(jnp.float32))
    onehot = (chan_map[:, None] == jnp.arange(channels, dtype=jnp.int32)[None, :]).astype(
        jnp.float32
    )

    def forward(coeff_in):
        return build_otf(coeff_in, scale_all, shift_all, zernike, mask_flat, length)

    otf, pullback = jax.vjp(forward, coeff_all)
    spectra = data_spectrum(frames, length, margin)
    shape = (2, slots, 1, length, length)
    obj_re, obj_im, otf_grad = wiener_terms(otf.reshape(shape), spectra.reshape(shape), onehot, length)
    images = object_image(
        obj_re.reshape(-1, length, length), obj_im.reshape(-1, length, length), length
    )
    grad_all = pullback(otf_grad.reshape(2, slots, length, length))[0]
    coeff_grad = lax.all_to_all(
        grad_all.reshape(slots, 1, 1, mode_count), "patch", split_axis=0, concat_axis=1, tiled=True
    )
    weight = window_weight(intersection[0, 0], length)
    numerator = images * weight[None]
    canvas = jnp.concatenate([numerator, weight[None]], axis=0)
    extended = padded(canvas, (("frame", 2), ("patch", 1)), margin)
    folded = fold_margins(fold_margins(extended, 1, margin), 2, margin)
    blended = folded[:channels] / folded[channels][None]
    return (blended, coeff_grad)


def solution(mesh):
    in_specs = (
        P("patch", None, "frame", None),
        P("patch", None, "frame", None),
        P("patch", None, "frame", None, None),
        P(),
        P(),
        P("patch", "frame"),
    )
    out_specs = (P(None, "patch", "frame"), P("patch", None, "frame", None))
    return jax.shard_map(
        per_device, mesh=mesh, in_specs=in_specs, out_specs=out_specs, check_vma=False
    )
```

profile of v0, /device:TPU:7, one launch (start us, length us, event | category | flops | bytes accessed | tf_op | source)
XLA Modules:
  0.0 144.8 jit_solution(2346695278505412335)
XLA Ops:
  2.8 7.8 %all-to-all-start = ((f32[1,16,1,38]{3,2,0,1:T(1,128)}), f32[1,16,1,38]{3,2,0,1:T(1,128)S(1)}, u32[]{:S(2)}, u32[]{:S(2)}) async-start(f32[1,16,1,38]{3,2,0,1:T(1,128)} %pad_maximum_fusion.12), calls=%async_computation | async-start | bytes 16384 | tf_op jit(solution)/shard_map/all_to_all | solution.py:189
  20.4 7.2 %all-to-all-start.1 = ((bf16[1,16,1,128,128]{4,3,2,0,1:T(8,128)(2,1)}), bf16[1,16,1,128,128]{4,3,2,0,1:T(8,128)(2,1)S(1)}, u32[]{:S(2)}, u32[]{:S(2)}) async-start(bf16[1,16,1,128,128]{4,3,2,0,1:T(8,128)(2,1)} %bitcast.39), calls=%async_computation.1 | async-start | bytes 1048576 | tf_op jit(solution)/shard_map/all_to_all | solution.py:194
  30.7 1.8 %convolution_bitcast_fusion = f32[2,16,128,128]{2,3,0,1:T(8,128)S(1)} fusion(f32[2,16,64,128,1]{3,2,0,4,1:T(8,128)S(1)} %convolution_bitcast_fusion.2, f32[1,2,128,64]{2,3,1,0:T(8,128)S(1)} %copy-done.26, f32[1,2,128,64]{2,3,1,0:T(8,128)S(1)} %copy-done.24), kind=kOutput, calls=%fused_computation.14 | convolution fusion | flops 805339136 | bytes 3276800 | tf_op jit(solution)/shard_map/jvp(tsux,sbxv->tbuv)/dot_general | solution.py:35
  33.0 1.9 %fusion.43 = f32[2,128,16,128]{3,1,0,2:T(8,128)S(1)} fusion(f32[16]{0:T(128)S(1)} %fusion.192, f32[1,128,128]{2,1,0:T(8,128)S(1)} %get-tuple-element.123, f32[1,128,128]{2,1,0:T(8,128)S(1)} %get-tuple-element.124, f32[2,16,128,128]{2,3,0,1:T(8,128)S(1)} %convolution_bitcast_fusion), kind=kOutput, calls=%fused_computation.56 | convolution fusion | flops 806387712 | bytes 4325440 | tf_op jit(solution)/shard_map/jvp(bxy,tvy->tbxv)/dot_general | solution.py:35
  34.9 3.2 %fusion.11 = f32[2,16,128,128]{2,3,0,1:T(8,128)} fusion(f32[2,128,16,128]{3,1,0,2:T(8,128)S(1)} %fusion.43, f32[1,2,128,128]{3,2,1,0:T(8,128)S(1)} %get-tuple-element.44, f32[1,2,128,128]{3,2,1,0:T(8,128)S(1)} %get-tuple-element.43), kind=kOutput, calls=%fused_computation.15 | convolution fusion | flops 1610678272 | bytes 4456448 | tf_op jit(solution)/shard_map/jvp(tsux,sbxv->tbuv)/dot_general | solution.py:35
  39.3 5.6 %all-to-all-done.1 = bf16[1,16,1,128,128]{4,3,2,0,1:T(8,128)(2,1)S(1)} async-done(((bf16[1,16,1,128,128]{4,3,2,0,1:T(8,128)(2,1)}), bf16[1,16,1,128,128]{4,3,2,0,1:T(8,128)(2,1)S(1)}, u32[]{:S(2)}, u32[]{:S(2)}) %all-to-all-start.1) | async-done | bytes 524320 | tf_op jit(solution)/shard_map/all_to_all | solution.py:194
  44.9 1.9 %fusion.45 = f32[2,128,16,128]{3,1,0,2:T(8,128)S(1)} fusion(bf16[1,16,1,128,128]{4,3,2,0,1:T(8,128)(2,1)S(1)} %all-to-all-done.1, f32[128]{0:T(128)S(1)} %copy-done.35, f32[1,128,128]{2,1,0:T(8,128)S(1)} %get-tuple-element.123, f32[1,128,128]{2,1,0:T(8,128)S(1)} %get-tuple-element.124), kind=kOutput, calls=%fused_computation.58 | convolution fusion | flops 806125568 | bytes 2753024 | tf_op jit(solution)/shard_map/bxy,tvy->tbxv/dot_general | solution.py:35
  46.9 2.1 %fusion.14 = f32[2,16,128,128]{2,3,1,0:T(8,128)S(1)} fusion(f32[2,128,16,128]{3,1,0,2:T(8,128)S(1)} %fusion.45, f32[1,2,128,128]{3,2,1,0:T(8,128)S(1)} %get-tuple-element.44, f32[1,2,128,128]{3,2,1,0:T(8,128)S(1)} %get-tuple-element.43), kind=kOutput, calls=%fused_computation.16 | convolution fusion | flops 1610678272 | bytes 4456448 | tf_op jit(solution)/shard_map/tsux,sbxv->tbuv/dot_general | solution.py:35
  49.0 5.6 %multiply_subtract_fusion = (f32[16,128,128]{1,2,0:T(8,128)}, f32[16,128,128]{1,2,0:T(8,128)S(1)}, f32[16,128,128]{1,2,0:T(8,128)S(1)}) fusion(f32[2,16,128,128]{2,3,1,0:T(8,128)S(1)} %fusion.14, f32[2,16,128,128]{2,3,0,1:T(8,128)S(1)} %copy-done.3, f32[16,128]{1,0:T(8,128)S(1)} %copy-done.30, f32[16,128]{1,0:T(8,128)S(1)} %copy-done.28), kind=kLoop, calls=%fused_computation.70 | loop fusion | flops 2883584 | bytes 7356416 | tf_op jit(solution)/shard_map/sub | solution.py:138
  54.5 1.7 %multiply_add_fusion.1 = (f32[16,128,128]{1,2,0:T(8,128)}, f32[16,128,128]{1,2,0:T(8,128)}) fusion(f32[16,128,128]{1,2,0:T(8,128)S(1)} %get-tuple-element.16, f32[16,128,128]{1,2,0:T(8,128)S(1)} %get-tuple-element.15, f32[2,16,128,128]{2,3,1,0:T(8,128)S(1)} %fusion.14), kind=kLoop, calls=%fused_computation.72 | loop fusion | flops 1572864 | bytes 6291456 | tf_op jit(solution)/shard_map/add | solution.py:137
  56.2 2.6 %copy.57 = f32[16,128,128]{2,0,1:T(8,128)} copy(f32[16,128,128]{1,2,0:T(8,128)} %get-tuple-element.30) | data formatting | bytes 2097152 | tf_op jit(solution)/shard_map/add | solution.py:139
  58.8 2.3 %convolution_add_fusion.2 = f32[2,128,128]{2,0,1:T(2,128)} fusion(f32[16,128,128]{2,0,1:T(8,128)} %copy.57, s32[16]{0:T(128)} %param.10), kind=kOutput, calls=%fused_computation.39 | convolution fusion | flops 6324256 | bytes 1179712 | tf_op jit(solution)/shard_map/kc,kbuv->cbuv/dot_general | solution.py:35
  61.2 2.6 %copy.56 = f32[16,128,128]{2,0,1:T(8,128)} copy(f32[16,128,128]{1,2,0:T(8,128)} %get-tuple-element.29) | data formatting | bytes 2097152 | tf_op jit(solution)/shard_map/add | solution.py:137
  63.8 2.3 %convolution_divide_fusion.1 = f32[2,128,128]{2,0,1:T(2,128)} fusion(f32[2,128,128]{2,0,1:T(2,128)} %convolution_add_fusion.2, f32[16,128,128]{2,0,1:T(8,128)} %copy.56, s32[16]{0:T(128)} %param.10), kind=kOutput, calls=%fused_computation.40 | convolution fusion | flops 6324256 | bytes 1310784 | tf_op jit(solution)/shard_map/kc,kbuv->cbuv/dot_general | solution.py:35
  66.1 1.7 %copy.58 = f32[2,128,128]{1,2,0:T(8,128)} copy(f32[2,128,128]{2,0,1:T(2,128)} %convolution_divide_fusion.1) | data formatting | bytes 262144 | tf_op jit(solution)/shard_map/div | solution.py:143
  67.8 2.5 %fusion.143 = f32[16,128,128]{2,0,1:T(8,128)} fusion(f32[2,128,128]{2,0,1:T(2,128)} %convolution_divide_fusion.1, s32[16]{0:T(128)} %param.10), kind=kOutput, calls=%fused_computation.231 | convolution fusion | flops 6291488 | bytes 1179712 | tf_op jit(solution)/shard_map/kc,cbuv->kbuv/dot_general | solution.py:35
  70.3 2.6 %copy.59 = f32[16,128,128]{2,0,1:T(8,128)} copy(f32[16,128,128]{1,2,0:T(8,128)} %get-tuple-element.14) | data formatting | bytes 2097152 | tf_op jit(solution)/shard_map/sub | solution.py:138
  73.0 2.3 %convolution_divide_fusion = f32[2,128,128]{2,0,1:T(2,128)} fusion(f32[2,128,128]{2,0,1:T(2,128)} %convolution_add_fusion.2, f32[16,128,128]{2,0,1:T(8,128)} %copy.59, s32[16]{0:T(128)} %param.10), kind=kOutput, calls=%fused_computation.38 | convolution fusion | flops 6324256 | bytes 1310784 | tf_op jit(solution)/shard_map/kc,kbuv->cbuv/dot_general | solution.py:35
  75.3 1.6 %copy.60 = f32[2,128,128]{1,2,0:T(8,128)} copy(f32[2,128,128]{2,0,1:T(2,128)} %convolution_divide_fusion) | data formatting | bytes 262144 | tf_op jit(solution)/shard_map/div | solution.py:144
  77.0 2.6 %fusion.141 = f32[16,128,128]{2,0,1:T(8,128)} fusion(f32[2,128,128]{2,0,1:T(2,128)} %convolution_divide_fusion, s32[16]{0:T(128)} %param.10), kind=kOutput, calls=%fused_computation.229 | convolution fusion | flops 6291488 | bytes 1179712 | tf_op jit(solution)/shard_map/kc,cbuv->kbuv/dot_general | solution.py:35
  86.7 10.9 %collective-permute-start.1 = (f32[3,128,16]{1,2,0:T(8,128)}, f32[3,128,16]{1,2,0:T(8,128)}, u32[]{:S(2)}, u32[]{:S(2)}) collective-permute-start(f32[3,128,16]{1,2,0:T(8,128)} %get-tuple-element.38), channel_id=1, source_target_pairs={{16,0},{32,16},{48,32},{64,48},{80,64},{96,80},{112,96},{128,112},... | collective-permute-start | bytes 73736 | tf_op jit(solution)/shard_map/ppermute | solution.py:27
  97.6 1.9 %collective-permute-start = (f32[3,128,16]{1,2,0:T(8,128)}, f32[3,128,16]{1,2,0:T(8,128)}, u32[]{:S(2)}, u32[]{:S(2)}) collective-permute-start(f32[3,128,16]{1,2,0:T(8,128)} %get-tuple-element.37), channel_id=1, source_target_pairs={{0,16},{16,32},{32,48},{48,64},{64,80},{80,96},{96,112},{112,128},... | collective-permute-start | bytes 73736 | tf_op jit(solution)/shard_map/ppermute | solution.py:25
  99.6 2.6 %copy.65 = f32[16,128,128]{1,2,0:T(8,128)} copy(f32[16,128,128]{2,0,1:T(8,128)} %fusion.143) | data formatting | bytes 2097152 | tf_op jit(solution)/shard_map/kc,cbuv->kbuv/dot_general | solution.py:35
  102.1 2.5 %copy.66 = f32[16,128,128]{1,2,0:T(8,128)} copy(f32[16,128,128]{2,0,1:T(8,128)} %fusion.141) | data formatting | bytes 2097152 | tf_op jit(solution)/shard_map/kc,cbuv->kbuv/dot_general | solution.py:35
  104.7 7.6 %fusion.39 = (f32[1,16,128,128]{2,3,1,0:T(8,128)S(1)}, f32[16,128,128]{1,2,0:T(8,128)S(1)}, f32[1,16,128,128]{2,3,1,0:T(8,128)S(1)}, f32[16,128,128]{1,2,0:T(8,128)S(1)}) fusion(f32[16,128]{1,0:T(8,128)} %get-tuple-element.105, f32[16,128]{1,0:T(8,128)} %get-tuple-element.104, f32[16,128,128]{1,2,0:T(8,128)} %copy.65, f32[16,128,128]{1,2,0:T(8,128)} %copy.66, ...), kind=kLoop, calls=%fused_computation.45 | loop fusion | flops 4980736 | bytes 10502144 | tf_op jit(solution)/shard_map/transpose(jvp())/mul | solution.py:121
  112.4 4.1 %fusion.37 = (f32[1,16,128,128]{2,3,1,0:T(8,128)S(1)}, f32[1,16,128,128]{2,3,1,0:T(8,128)S(1)}) fusion(f32[16,128,128]{1,2,0:T(8,128)S(1)} %get-tuple-element.11, f32[16,128]{1,0:T(8,128)S(1)} %copy-done.31, f32[16,128]{1,0:T(8,128)S(1)} %copy-done.29, f32[16,128,128]{1,2,0:T(8,128)S(1)} %get-tuple-element.26), kind=kLoop, calls=%fused_computation.43 | loop fusion | flops 1048576 | bytes 4210688 | tf_op jit(solution)/shard_map/transpose(jvp())/mul | solution.py:121
  116.5 1.9 %fusion.9 = f32[16,128,2,128,1]{3,1,4,2,0:T(8,128)S(1)} fusion(f32[1,16,128,128]{2,3,1,0:T(8,128)S(1)} %get-tuple-element.68, f32[1,16,128,128]{2,3,1,0:T(8,128)S(1)} %get-tuple-element.25, f32[1,16,128,128]{2,3,1,0:T(8,128)S(1)} %get-tuple-element.67, f32[1,16,128,128]{2,3,1,0:T(8,128)S(1)} %get-tuple-element.10, f32[1,2,128,128]{3,2,1,0:T(8,128)S(1)} %copy-done.9, ...), kind=kOutput, calls=%fused_computation.11 | convolution fusion | flops 1612251136 | bytes 6553600 | tf_op jit(solution)/shard_map/transpose(jvp(tsux,sbxv->tbuv))/dot_general | solution.py:35
  118.4 1.6 %multiply_reduce_fusion = (f32[16]{0:T(128)S(1)}, f32[16,128,128]{1,2,0:T(8,128)S(1)}) fusion(f32[16]{0:T(128)S(1)} %copy-done.40, f32[2,16,128,128]{2,3,0,1:T(8,128)S(1)} %copy-done.1, f32[1,128,128]{2,1,0:T(8,128)S(1)} %copy-done.13, f32[1,128,128]{2,1,0:T(8,128)S(1)} %copy-done.15, f32[16,128,2,128,1]{3,1,4,2,0:T(8,128)S(1)} %fusion.9), kind=kOutput, calls=%fused_computation.64 | convolution fusion | flops 806912000 | bytes 5374080 | tf_op jit(solution)/shard_map/transpose(jvp(bxy,tvy->tbxv))/dot_general | solution.py:35
  121.0 2.3 %fusion.26 = f32[2,128,16,64,1]{1,3,0,4,2:T(8,128)S(1)} fusion(f32[1,16,128,128]{2,3,1,0:T(8,128)S(1)} %get-tuple-element.28, f32[1,16,128,128]{2,3,1,0:T(8,128)S(1)} %get-tuple-element.27, f32[1,2,128,64]{2,3,1,0:T(8,128)S(1)} %copy-done.27, f32[1,2,128,64]{2,3,1,0:T(8,128)S(1)} %copy-done.25), kind=kOutput, calls=%fused_computation.28 | convolution fusion | flops 806912000 | bytes 3276800 | tf_op jit(solution)/shard_map/transpose(jvp(tsux,sbxv->tbuv))/dot_general | solution.py:35
  126.2 1.9 %collective-permute-start.3 = (f32[3,16,160]{1,2,0:T(8,128)S(1)}, f32[3,16,160]{1,2,0:T(8,128)S(1)}, u32[]{:S(2)}, u32[]{:S(2)}) collective-permute-start(f32[3,16,160]{1,2,0:T(8,128)S(1)} %get-tuple-element.36), channel_id=1, source_target_pairs={{1,0},{2,1},{3,2},{4,3},{5,4},{6,5},{7,6},{8,7},{9,8},{10,9},{11,1... | collective-permute-start | bytes 92168 | tf_op jit(solution)/shard_map/ppermute | solution.py:27
  128.1 3.6 %collective-permute-start.2 = (f32[3,16,160]{1,2,0:T(8,128)S(1)}, f32[3,16,160]{1,2,0:T(8,128)S(1)}, u32[]{:S(2)}, u32[]{:S(2)}) collective-permute-start(f32[3,16,160]{1,2,0:T(8,128)S(1)} %get-tuple-element.35), channel_id=1, source_target_pairs={{0,1},{1,2},{2,3},{3,4},{4,5},{5,6},{6,7},{7,8},{8,9},{9,10},{10,1... | collective-permute-start | bytes 92168 | tf_op jit(solution)/shard_map/ppermute | solution.py:25
  132.5 10.7 %all_to_all.30 = f32[16,1,1,36]{3,2,1,0:T(1,128)S(1)} all-to-all(f32[16,1,1,36]{3,2,1,0:T(1,128)S(1)} %bitcast.295), channel_id=1, replica_groups=mesh['frame'=32,'patch'=16] {'patch'}, dimensions={0} | all-to-all | bytes 4608 | tf_op jit(solution)/shard_map/all_to_all | solution.py:214
  (165 shorter events, 28.7 us)
Async XLA Ops:
  0.6 18.8 %copy-start.34 = (s32[64,64]{1,0:T(8,128)S(1)}, s32[64,64]{1,0:T(8,128)}, u32[]{:S(2)}) copy-start(s32[64,64]{1,0:T(8,128)} %param.9) | copy-start | bytes 49156
  2.8 17.6 %all-to-all-start = ((f32[1,16,1,38]{3,2,0,1:T(1,128)}), f32[1,16,1,38]{3,2,0,1:T(1,128)S(1)}, u32[]{:S(2)}, u32[]{:S(2)}) async-start(f32[1,16,1,38]{3,2,0,1:T(1,128)} %pad_maximum_fusion.12), calls=%async_computation | async-start | bytes 16384 | tf_op jit(solution)/shard_map/all_to_all | solution.py:189
  11.5 33.4 %copy-start.12 = (f32[1,128,128]{2,1,0:T(8,128)}, f32[1,128,128]{2,1,0:T(8,128)S(1)}, u32[]{:S(2)}) copy-start(f32[1,128,128]{2,1,0:T(8,128)S(1)} %get-tuple-element.123) | copy-start | bytes 196612
  11.5 33.4 %copy-start.14 = (f32[1,128,128]{2,1,0:T(8,128)}, f32[1,128,128]{2,1,0:T(8,128)S(1)}, u32[]{:S(2)}) copy-start(f32[1,128,128]{2,1,0:T(8,128)S(1)} %get-tuple-element.124) | copy-start | bytes 196612
  14.8 12.8 %copy-start.36 = (f32[16]{0:T(128)}, f32[16]{0:T(128)S(1)}, u32[]{:S(2)}) copy-start(f32[16]{0:T(128)S(1)} %add_divide_fusion) | copy-start | bytes 196
  17.4 29.4 %copy-start.8 = (f32[1,2,128,128]{3,2,1,0:T(8,128)}, f32[1,2,128,128]{3,2,1,0:T(8,128)S(1)}, u32[]{:S(2)}) copy-start(f32[1,2,128,128]{3,2,1,0:T(8,128)S(1)} %get-tuple-element.44) | copy-start | bytes 393220
  18.1 11.5 %copy-start.16 = (f32[1,2,128,64]{2,3,0,1:T(8,128)}, f32[1,2,128,64]{2,3,0,1:T(8,128)S(1)}, u32[]{:S(2)}) copy-start(f32[1,2,128,64]{2,3,0,1:T(8,128)S(1)} %get-tuple-element.40) | copy-start | bytes 196612
  18.1 11.5 %copy-start.18 = (f32[1,2,128,64]{2,3,0,1:T(8,128)}, f32[1,2,128,64]{2,3,0,1:T(8,128)S(1)}, u32[]{:S(2)}) copy-start(f32[1,2,128,64]{2,3,0,1:T(8,128)S(1)} %get-tuple-element.45) | copy-start | bytes 196612
  20.4 9.1 %copy-start.4 = (f32[36,4096]{1,0:T(8,128)}, f32[36,4096]{1,0:T(8,128)S(1)}, u32[]{:S(2)}) copy-start(f32[36,4096]{1,0:T(8,128)S(1)} %stack.46) | copy-start | bytes 1769476
  20.4 8.6 %copy-start.32 = (f32[1,16,1,38]{3,2,0,1:T(1,128)}, f32[1,16,1,38]{3,2,0,1:T(1,128)S(1)}, u32[]{:S(2)}) copy-start(f32[1,16,1,38]{3,2,0,1:T(1,128)S(1)} %all-to-all-done) | copy-start | bytes 7300
  20.4 24.4 %all-to-all-start.1 = ((bf16[1,16,1,128,128]{4,3,2,0,1:T(8,128)(2,1)}), bf16[1,16,1,128,128]{4,3,2,0,1:T(8,128)(2,1)S(1)}, u32[]{:S(2)}, u32[]{:S(2)}) async-start(bf16[1,16,1,128,128]{4,3,2,0,1:T(8,128)(2,1)} %bitcast.39), calls=%async_computation.1 | async-start | bytes 1048576 | tf_op jit(solution)/shard_map/all_to_all | solution.py:194
  30.7 2.1 %copy-start.33 = (f32[1,16,1,38]{3,2,0,1:T(1,128)S(1)}, f32[1,16,1,38]{3,2,0,1:T(1,128)}, u32[]{:S(2)}) copy-start(f32[1,16,1,38]{3,2,0,1:T(1,128)} %copy-done.32) | copy-start | bytes 7300
  32.5 2.3 %copy-start = (f32[2,16,128,128]{2,3,0,1:T(8,128)}, f32[2,16,128,128]{2,3,0,1:T(8,128)S(1)}, u32[]{:S(2)}) copy-start(f32[2,16,128,128]{2,3,0,1:T(8,128)S(1)} %convolution_bitcast_fusion) | copy-start | bytes 6291460
  32.8 5.3 %copy-start.38 = (f32[16]{0:T(128)}, f32[16]{0:T(128)S(1)}, u32[]{:S(2)}) copy-start(f32[16]{0:T(128)S(1)} %fusion.192) | copy-start | bytes 196
  34.9 3.7 %copy-start.41 = (f32[128]{0:T(128)S(1)}, f32[128]{0:T(128)}, u32[]{:S(2)}) copy-start(f32[128]{0:T(128)} %iota_convert_fusion) | copy-start | bytes 1540
  34.9 10.0 %copy-start.35 = (f32[128]{0:T(128)S(1)}, f32[128]{0:T(128)}, u32[]{:S(2)}) copy-start(f32[128]{0:T(128)} %compare_select_fusion) | copy-start | bytes 1540
  77.0 7.4 %copy-start.22 = (f32[2,128,128]{1,2,0:T(8,128)S(1)}, f32[2,128,128]{1,2,0:T(8,128)}, u32[]{:S(2)}) copy-start(f32[2,128,128]{1,2,0:T(8,128)} %copy.58) | copy-start | bytes 393220
  77.0 7.9 %copy-start.23 = (f32[128,128]{0,1:T(8,128)S(1)}, f32[128,128]{0,1:T(8,128)}, u32[]{:S(2)}) copy-start(f32[128,128]{0,1:T(8,128)} %multiply_multiply_fusion) | copy-start | bytes 196612
  77.0 9.1 %copy-start.20 = (f32[1,128,128]{1,2,0:T(8,128)S(1)}, f32[1,128,128]{1,2,0:T(8,128)}, u32[]{:S(2)}) copy-start(f32[1,128,128]{1,2,0:T(8,128)} %broadcast_multiply_fusion.2) | copy-start | bytes 196612
  86.7 38.2 %collective-permute-start.1 = (f32[3,128,16]{1,2,0:T(8,128)}, f32[3,128,16]{1,2,0:T(8,128)}, u32[]{:S(2)}, u32[]{:S(2)}) collective-permute-start(f32[3,128,16]{1,2,0:T(8,128)} %get-tuple-element.38), channel_id=1, source_target_pairs={{16,0},{32,16},{48,32},{64,48},{80,64},{96,80},{112,96},{128,112},... | collective-permute-start | bytes 73736 | tf_op jit(solution)/shard_map/ppermute | solution.py:27
  97.6 27.2 %collective-permute-start = (f32[3,128,16]{1,2,0:T(8,128)}, f32[3,128,16]{1,2,0:T(8,128)}, u32[]{:S(2)}, u32[]{:S(2)}) collective-permute-start(f32[3,128,16]{1,2,0:T(8,128)} %get-tuple-element.37), channel_id=1, source_target_pairs={{0,16},{16,32},{32,48},{48,64},{64,80},{80,96},{96,112},{112,128},... | collective-permute-start | bytes 73736 | tf_op jit(solution)/shard_map/ppermute | solution.py:25
  104.7 7.7 %copy-start.29 = (f32[16,128]{1,0:T(8,128)S(1)}, f32[16,128]{1,0:T(8,128)}, u32[]{:S(2)}) copy-start(f32[16,128]{1,0:T(8,128)} %get-tuple-element.104) | copy-start | bytes 24580
  104.7 7.7 %copy-start.31 = (f32[16,128]{1,0:T(8,128)S(1)}, f32[16,128]{1,0:T(8,128)}, u32[]{:S(2)}) copy-start(f32[16,128]{1,0:T(8,128)} %get-tuple-element.105) | copy-start | bytes 24580
  112.3 4.1 %copy-start.9 = (f32[1,2,128,128]{3,2,1,0:T(8,128)S(1)}, f32[1,2,128,128]{3,2,1,0:T(8,128)}, u32[]{:S(2)}) copy-start(f32[1,2,128,128]{3,2,1,0:T(8,128)} %copy-done.8) | copy-start | bytes 393220
  120.4 2.9 %copy-start.17 = (f32[1,2,128,64]{2,3,0,1:T(8,128)S(1)}, f32[1,2,128,64]{2,3,0,1:T(8,128)}, u32[]{:S(2)}) copy-start(f32[1,2,128,64]{2,3,0,1:T(8,128)} %copy-done.16) | copy-start | bytes 196612
  120.4 2.9 %copy-start.19 = (f32[1,2,128,64]{2,3,0,1:T(8,128)S(1)}, f32[1,2,128,64]{2,3,0,1:T(8,128)}, u32[]{:S(2)}) copy-start(f32[1,2,128,64]{2,3,0,1:T(8,128)} %copy-done.18) | copy-start | bytes 196612
  124.4 7.4 %copy-start.5 = (f32[36,4096]{1,0:T(8,128)S(1)}, f32[36,4096]{1,0:T(8,128)}, u32[]{:S(2)}) copy-start(f32[36,4096]{1,0:T(8,128)} %copy-done.4) | copy-start | bytes 1769476
  124.4 7.4 %copy-start.7 = (f32[16,4096]{1,0:T(8,128)S(1)}, f32[16,4096]{1,0:T(8,128)}, u32[]{:S(2)}) copy-start(f32[16,4096]{1,0:T(8,128)} %copy-done.6) | copy-start | bytes 786436
  124.4 7.4 %copy-start.37 = (f32[16]{0:T(128)S(1)}, f32[16]{0:T(128)}, u32[]{:S(2)}) copy-start(f32[16]{0:T(128)} %copy-done.36) | copy-start | bytes 196
  124.9 18.5 %copy-start.42 = (pred[96]{0:T(512)(128)(4,1)S(1)}, pred[96]{0:T(512)(128)(4,1)}, u32[]{:S(2)}) copy-start(pred[96]{0:T(512)(128)(4,1)} %constant.143.clone.1) | copy-start | bytes 292
  126.2 17.0 %collective-permute-start.3 = (f32[3,16,160]{1,2,0:T(8,128)S(1)}, f32[3,16,160]{1,2,0:T(8,128)S(1)}, u32[]{:S(2)}, u32[]{:S(2)}) collective-permute-start(f32[3,16,160]{1,2,0:T(8,128)S(1)} %get-tuple-element.36), channel_id=1, source_target_pairs={{1,0},{2,1},{3,2},{4,3},{5,4},{6,5},{7,6},{8,7},{9,8},{10,9},{11,1... | collective-permute-start | bytes 92168 | tf_op jit(solution)/shard_map/ppermute | solution.py:27
  128.1 15.0 %collective-permute-start.2 = (f32[3,16,160]{1,2,0:T(8,128)S(1)}, f32[3,16,160]{1,2,0:T(8,128)S(1)}, u32[]{:S(2)}, u32[]{:S(2)}) collective-permute-start(f32[3,16,160]{1,2,0:T(8,128)S(1)} %get-tuple-element.35), channel_id=1, source_target_pairs={{0,1},{1,2},{2,3},{3,4},{4,5},{5,6},{6,7},{7,8},{8,9},{9,10},{10,1... | collective-permute-start | bytes 92168 | tf_op jit(solution)/shard_map/ppermute | solution.py:25
  (17 other events, 25.4 us)
where the time goes:
time: 146 us; the launch traced here: 145 us
  matrix products  38.8 us (27%)
  starting transfers between devices  33.4 us (23%)
  other arithmetic  31.4 us (22%)
  local copies, waits for them, and re-layouts  22.7 us (16%)
  blocking collectives  10.7 us (7%)
  waiting for transfers between devices  5.61 us (4%)
  between operations  2.23 us (2%)
    dot_general x21, matrix products, product(): return jnp.einsum(form, left, right, precision=highest)  36.8 us
    ppermute x2, starting transfers between devices, padded(): lax.ppermute(head, axis, [((i + 1) % count, i) for i in range(ends)])  12.8 us
    all_to_all x1, blocking collectives, per_device(): lax.all_to_all(grad_all.reshape(slots, 1, 1, mode_count), 'patch', split_...  10.7 us
    all_to_all x1, starting transfers between devices, per_device(): lax.all_to_all(small, 'patch', split_axis=1, concat_axis=0, tiled=True)  7.79 us
    mul x1, other arithmetic, build_otf(): otf[1] * tilt_re  7.64 us
    all_to_all x1, starting transfers between devices, per_device(): lax.all_to_all(pixels, 'patch', split_axis=1, concat_axis=0, tiled=True)  7.24 us
    all_to_all x1, waiting for transfers between devices, per_device(): lax.all_to_all(pixels, 'patch', split_axis=1, concat_axis=0, tiled=True)  5.6 us
    sub x1, other arithmetic, wiener_terms(): cross_im = otf_re * spec_im - otf_im * spec_re  5.56 us
  transfers between devices with their start and end apart: 6, of which 1 were waited for; matrix products, arithmetic and copies ran while one was open for 31% of the time, Pallas kernels for 0%

commit v1 on v0

v1 whole, which is shorter than its diff:
```python
import functools
import math

import jax
import jax.numpy as jnp
import ml_dtypes
import numpy as np
from jax import lax
from jax.experimental import pallas as pl
from jax.experimental.pallas import tpu as pltpu
from jax.sharding import PartitionSpec as P

N = 128
PUP = 64
ZERN = 36
SLOTS = 16
PAIRS = SLOTS // 2
CHANNELS = 2
PER = SLOTS // CHANNELS
MARGIN = 16
HALF = 72
TWO = 2 * HALF
DEG = 9
COEF = 40
regular_gamma = 0.1
wave_ratio = 0.35
f32 = jnp.float32
bf16 = jnp.bfloat16
VM = pl.BlockSpec(memory_space=pltpu.VMEM)
SM = pl.BlockSpec(memory_space=pltpu.SMEM)


def noll_order(noll_index):
    radial = 0
    remain = noll_index - 1
    while remain > radial:
        radial += 1
        remain -= radial
    azimuth = radial % 2 + 2 * ((remain + (radial + 1) % 2) // 2)
    if noll_index % 2 == 1:
        azimuth = -azimuth
    return (radial, azimuth)


def zernike_modes():
    position = (np.arange(PUP) - (PUP - 1) / 2.0) / (PUP / 2.0)
    grid_y, grid_x = np.meshgrid(position, position, indexing="ij")
    radius = np.sqrt(grid_x * grid_x + grid_y * grid_y)
    theta = np.arctan2(grid_y, grid_x)
    modes = []
    for noll_index in range(2, ZERN + 2):
        radial, azimuth = noll_order(noll_index)
        order = abs(azimuth)
        total = np.zeros_like(radius)
        for step in range((radial - order) // 2 + 1):
            factor = math.factorial(radial - step) / (
                math.factorial(step)
                * math.factorial((radial + order) // 2 - step)
                * math.factorial((radial - order) // 2 - step)
            )
            total = total + (-1) ** step * factor * radius ** (radial - 2 * step)
        if azimuth == 0:
            modes.append(total * math.sqrt(radial + 1.0))
        elif azimuth > 0:
            modes.append(total * math.sqrt(2.0 * (radial + 1.0)) * np.cos(order * theta))
        else:
            modes.append(total * math.sqrt(2.0 * (radial + 1.0)) * np.sin(order * theta))
    return position, np.stack(modes)


def halves(table):
    high = table.astype(ml_dtypes.bfloat16)
    low = (table - high.astype(np.float64)).astype(ml_dtypes.bfloat16)
    return high, low


def pair_table(table):
    return np.stack(halves(table))


@functools.cache
def tables():
    index = np.arange(N)
    turns = 2.0 * np.pi / N * (np.outer(index, index) % N)
    c, s = np.cos(turns), np.sin(turns)
    cp, sp = c[:, :PUP], s[:, :PUP]
    ch, sh = c[:HALF], s[:HALF]
    distance = np.minimum(index, N - 1 - index)
    taper = np.where(distance < MARGIN, 0.5 - 0.5 * np.cos(np.pi * (distance + 0.5) / MARGIN), 1.0)
    weight = np.where(np.arange(HALF) < 1, 1.0, 2.0)
    weight[N // 2] = 1.0
    weight[N // 2 + 1 :] = 0.0
    out = {}
    out["right_pupil"] = pair_table(np.block([[cp.T, -sp.T], [sp.T, cp.T]]))
    out["left_pupil"] = pair_table(np.block([[cp, sp], [-sp, cp]]))
    out["left_half"] = pair_table(np.block([[ch], [-sh]]))
    out["right_full"] = pair_table(np.block([[c, -s], [s, c]]))
    out["right_back"] = pair_table(np.block([[c, s], [-s, c]]))
    high, low = halves(np.block([[ch], [-sh]]) * taper[None, :])
    out["left_taper"] = np.concatenate([high, low], axis=1)
    high, low = halves(np.concatenate([weight[None] * ch.T, -weight[None] * sh.T], axis=1))
    out["left_back"] = np.concatenate([high, high, low], axis=1)
    out["taper"] = np.tile(taper, 2)[None].astype(np.float32)
    out["weight"] = np.broadcast_to(weight[:, None], (HALF, N)).astype(np.float32)
    position, modes = zernike_modes()
    cheb = np.polynomial.chebyshev.chebvander(position, DEG - 1)
    fit = np.linalg.lstsq(cheb, modes.transpose(1, 0, 2).reshape(PUP, -1), rcond=None)[0]
    fit = fit.reshape(DEG, ZERN, PUP).transpose(1, 0, 2)
    phase = np.zeros((COEF, DEG, PUP))
    phase[:ZERN] = fit
    step = 2.0 * np.pi / N * (PUP / 2.0)
    phase[ZERN, 1] = step
    phase[ZERN + 1, 0] = step * position
    phase = np.concatenate([phase, phase], axis=2)
    out["phase"] = phase.reshape(COEF, DEG * N).astype(np.float32)
    return out, cheb


def split(x):
    high = x.astype(bf16)
    return high, (x - high.astype(f32)).astype(bf16)


def dot(left, right):
    return lax.dot_general(left, right, (((1,), (0,)), ((), ())), preferred_element_type=f32)


def rows3(x):
    high, low = split(x)
    return jnp.concatenate([high, low, high], axis=0)


def table_rows(ref):
    return jnp.concatenate([ref[0], ref[0], ref[1]], axis=0)


def table_lanes(ref):
    return jnp.concatenate([ref[0], ref[0], ref[1]], axis=1)


def swap_halves(y, count):
    top = jnp.concatenate([y[:count, :N], y[count:, :N]], axis=1)
    low = jnp.concatenate([y[:count, N:], y[count:, N:]], axis=1)
    return jnp.concatenate([top, low], axis=0)


def chebyshev_sums(parts, cheb, row):
    even = parts[0]
    for i in range(2, DEG, 2):
        even = even + float(cheb[row, i]) * parts[i]
    odd = float(cheb[row, 1]) * parts[1]
    for i in range(3, DEG, 2):
        odd = odd + float(cheb[row, i]) * parts[i]
    return even, odd


def turn(phase, lane_turns):
    count = jnp.floor(phase * (2.0 / math.pi) + 0.5)
    rest = phase - count * 1.5703125
    rest = rest - count * 4.837512969970703125e-4
    rest = rest - count * 7.549789954891882e-8
    quarter = count.astype(jnp.int32) + lane_turns
    sq = rest * rest
    sine = rest + rest * sq * (
        -1.6666654611e-1 + sq * (8.3321608736e-3 + sq * -1.9515295891e-4)
    )
    cosine = (1.0 - 0.5 * sq) + sq * sq * (
        4.166664568298827e-2 + sq * (-1.388731625493765e-3 + sq * 2.443315711809948e-5)
    )
    odd = (quarter & 1) == 1
    value = jnp.where(odd, sine, cosine)
    value = jnp.where(((quarter + 1) & 2) == 2, -value, value)
    slope = jnp.where(odd, cosine, sine)
    slope = jnp.where((quarter & 2) == 2, slope, -slope)
    return value, slope


def slot_scales(chan_ref, width):
    row = lax.broadcasted_iota(jnp.int32, (SLOTS, width), 0)
    channel = jnp.zeros((SLOTS, width), jnp.int32)
    for slot in range(SLOTS):
        channel = jnp.where(row == slot, chan_ref[slot], channel)
    return 1.0 / (1.0 + wave_ratio * channel.astype(f32))


def transfer_kernel(
    coef_ref, chan_ref, mask_ref, phase_ref, rp_ref, lp_ref, lh_ref, rf_ref,
    otf_ref, field_ref, slope_ref, inv_ref,
    wide_ref, ph_ref, pl_ref, half_re_ref, half_im_ref, yh_ref, yl_ref,
):
    cheb = tables()[1]
    lane = lax.broadcasted_iota(jnp.int32, (SLOTS, COEF), 1)
    coef = coef_ref[...] * jnp.where(lane < ZERN, slot_scales(chan_ref, COEF), 1.0)
    mask = mask_ref[...].astype(f32)
    wide_ref[...] = jnp.concatenate([mask, mask], axis=1)
    parts_all = lax.dot_general(
        coef, phase_ref[...], (((1,), (0,)), ((), ())),
        precision=lax.Precision.HIGHEST, preferred_element_type=f32,
    )
    parts = [parts_all[:, i * N : (i + 1) * N] for i in range(DEG)]
    lane_turns = jnp.where(lax.broadcasted_iota(jnp.int32, (SLOTS, N), 1) < PUP, 0, 3)
    for row in range(PUP // 2):
        even, odd = chebyshev_sums(parts, cheb, row)
        for at, phase in ((row, even + odd), (PUP - 1 - row, even - odd)):
            value, slope = turn(phase, lane_turns)
            mask = wide_ref[at : at + 1, :]
            value = value * mask
            here = slice(at * SLOTS, (at + 1) * SLOTS)
            slope_ref[here, :] = slope * mask
            high, low = split(value)
            ph_ref[here, :] = high
            pl_ref[here, :] = low
    right = table_rows(rp_ref)
    for chunk in range(4):
        here = slice(chunk * 256, (chunk + 1) * 256)
        high = ph_ref[here, :]
        half = dot(jnp.concatenate([high, pl_ref[here, :], high], axis=1), right)
        half_re_ref[here, :] = half[:, :N]
        half_im_ref[here, :] = half[:, N:]
    left = table_lanes(lp_ref)
    left_h = table_lanes(lh_ref)
    for pair in range(PAIRS):
        columns = []
        for part_ref in (half_re_ref, half_im_ref):
            columns.append(
                jnp.concatenate(
                    [
                        part_ref[pl.ds(2 * pair + which, PUP, stride=SLOTS), :]
                        for which in range(2)
                    ],
                    axis=1,
                )
            )
        field = dot(left, rows3(jnp.concatenate(columns, axis=0)))
        field_ref[pair] = field
        power = field[:N] * field[:N] + field[N:] * field[N:]
        y = dot(left_h, rows3(power))
        high, low = split(swap_halves(y, HALF))
        here = slice(pair * TWO, (pair + 1) * TWO)
        yh_ref[here, :] = high
        yl_ref[here, :] = low
    right = table_rows(rf_ref)
    for pair in range(PAIRS):
        here = slice(pair * TWO, (pair + 1) * TWO)
        high = yh_ref[here, :]
        out = dot(jnp.concatenate([high, yl_ref[here, :], high], axis=1), right)
        for which in range(2):
            slot = 2 * pair + which
            block = out[which * HALF : (which + 1) * HALF]
            inverse = 1.0 / block[0:1, 0:1]
            otf_ref[slot * HALF : (slot + 1) * HALF, :] = block * inverse
            inv_ref[slot : slot + 1, :] = jnp.broadcast_to(inverse, (1, N))


def object_kernel(
    width_ref, chan_ref, pix_ref, otf_ref, lt_ref, taper_ref, weight_ref, rf_ref, rb_ref, lb_ref,
    grad_ref, canvas_ref,
    order_ref, yh_ref, yl_ref, spec_ref, object_ref,
):
    at = [jnp.int32(0), jnp.int32(PER)]
    for slot in range(SLOTS):
        first = chan_ref[slot] == 0
        order_ref[jnp.where(first, at[0], at[1])] = slot
        at = [jnp.where(first, at[0] + 1, at[0]), jnp.where(first, at[1], at[1] + 1)]
    left = lt_ref[...]
    taper = taper_ref[...]
    for pair in range(PAIRS):
        image = jnp.concatenate([pix_ref[2 * pair], pix_ref[2 * pair + 1]], axis=1)
        y = dot(left, jnp.concatenate([image, image], axis=0)) * taper
        high, low = split(swap_halves(y, HALF))
        here = slice(pair * TWO, (pair + 1) * TWO)
        yh_ref[here, :] = high
        yl_ref[here, :] = low
    right = table_rows(rf_ref)
    for pair in range(PAIRS):
        here = slice(pair * TWO, (pair + 1) * TWO)
        high = yh_ref[here, :]
        spec_ref[here, :] = dot(jnp.concatenate([high, yl_ref[here, :], high], axis=1), right)
    for channel in range(CHANNELS):
        slots = [order_ref[channel * PER + i] for i in range(PER)]
        inner = [jnp.zeros((8, N), f32) for _ in range(PER)]
        for block in range(HALF // 8):
            where = [pl.ds(pl.multiple_of(slot * HALF + block * 8, 8), 8) for slot in slots]
            h_re = [otf_ref[w, :N] for w in where]
            h_im = [otf_ref[w, N:] for w in where]
            s_re = [spec_ref[w, :N] for w in where]
            s_im = [spec_ref[w, N:] for w in where]
            num_re = num_im = 0.0
            den = regular_gamma
            for i in range(PER):
                num_re = num_re + (h_re[i] * s_re[i] + h_im[i] * s_im[i])
                num_im = num_im + (h_re[i] * s_im[i] - h_im[i] * s_re[i])
                den = den + (h_re[i] * h_re[i] + h_im[i] * h_im[i])
            inverse = 1.0 / den
            o_re = num_re * inverse
            o_im = num_im * inverse
            rows = slice(channel * HALF + block * 8, channel * HALF + block * 8 + 8)
            object_ref[rows, :N] = o_re
            object_ref[rows, N:] = o_im
            weight = weight_ref[block * 8 : block * 8 + 8, :]
            for i in range(PER):
                r_re = s_re[i] - (o_re * h_re[i] - o_im * h_im[i])
                r_im = s_im[i] - (o_re * h_im[i] + o_im * h_re[i])
                g_re = -(r_re * o_re + r_im * o_im)
                g_im = r_re * o_im - r_im * o_re
                inner[i] = inner[i] + weight * (g_re * h_re[i] + g_im * h_im[i])
                grad_ref[where[i], :N] = g_re
                grad_ref[where[i], N:] = g_im
        origin = (lax.broadcasted_iota(jnp.int32, (8, N), 0) == 0) & (
            lax.broadcasted_iota(jnp.int32, (8, N), 1) == 0
        )
        for i in range(PER):
            total = jnp.sum(jnp.sum(inner[i], axis=0, keepdims=True), axis=1, keepdims=True)
            w = pl.ds(pl.multiple_of(slots[i] * HALF, 8), 8)
            grad_ref[w, :N] = grad_ref[w, :N] - jnp.where(origin, total, 0.0)
    high, low = split(object_ref[...] * (1.0 / (N * N)))
    z = dot(jnp.concatenate([high, low, high], axis=1), table_rows(rb_ref))
    image = dot(lb_ref[...], rows3(swap_halves(z, HALF)))
    width = width_ref[0].astype(f32) + 1.0
    row = lax.broadcasted_iota(jnp.int32, (N, N), 0)
    col = lax.broadcasted_iota(jnp.int32, (N, N), 1)

    def ramp(index):
        distance = (jnp.minimum(index, N - 1 - index) + 1).astype(f32)
        return jnp.minimum(1.0, distance / width)

    weight = ramp(row) * ramp(col)
    canvas_ref[0] = image[:, :N] * weight
    canvas_ref[1] = image[:, N:] * weight
    canvas_ref[2] = weight


def gradient_kernel(
    chan_ref, grad_ref, field_ref, slope_ref, inv_ref, phase_ref, rb_ref, lb_ref, rp_ref, lp_ref,
    out_ref,
    z_ref, qh_ref, ql_ref, pupil_ref,
):
    cheb = tables()[1]
    right = table_rows(rb_ref)
    for pair in range(PAIRS):
        here = slice(pair * TWO, (pair + 1) * TWO)
        high, low = split(grad_ref[here, :])
        z_ref[here, :] = dot(jnp.concatenate([high, low, high], axis=1), right)
    left_b = lb_ref[...]
    left = table_lanes(rp_ref)
    for pair in range(PAIRS):
        here = slice(pair * TWO, (pair + 1) * TWO)
        power = dot(left_b, rows3(swap_halves(z_ref[here, :], HALF)))
        field = field_ref[pair]
        back = jnp.concatenate([field[:N] * power, field[N:] * power], axis=0)
        half = dot(left, rows3(back))
        high, low = split(swap_halves(half, PUP))
        here = slice(pair * N, (pair + 1) * N)
        qh_ref[here, :] = high
        ql_ref[here, :] = low
    right = table_rows(lp_ref)
    for pair in range(PAIRS):
        here = slice(pair * N, (pair + 1) * N)
        high = qh_ref[here, :]
        pupil_ref[here, :] = dot(jnp.concatenate([high, ql_ref[here, :], high], axis=1), right)
    sums = [None] * DEG
    for row in range(PUP // 2):
        both = []
        for at in (row, PUP - 1 - row):
            q = pupil_ref[pl.ds(at, SLOTS, stride=PUP), :]
            both.append(q * slope_ref[at * SLOTS : (at + 1) * SLOTS, :])
        parity = (both[0] + both[1], both[0] - both[1])
        for i in range(DEG):
            term = parity[i % 2] * float(cheb[row, i]) if i else parity[0]
            sums[i] = term if sums[i] is None else sums[i] + term
    total = lax.dot_general(
        jnp.concatenate(sums, axis=1), phase_ref[...], (((1,), (1,)), ((), ())),
        precision=lax.Precision.HIGHEST, preferred_element_type=f32,
    )
    factor = 4.0 / float(N * N * N)
    out_ref[...] = total * (slot_scales(chan_ref, COEF) * factor * inv_ref[:, :COEF])


def transfer(coef, chan, mask, tabs, interpret=False):
    rows = SLOTS * HALF
    return pl.pallas_call(
        transfer_kernel,
        out_shape=(
            jax.ShapeDtypeStruct((rows, 2 * N), f32),
            jax.ShapeDtypeStruct((PAIRS, 2 * N, 2 * N), f32),
            jax.ShapeDtypeStruct((PUP * SLOTS, N), f32),
            jax.ShapeDtypeStruct((SLOTS, N), f32),
        ),
        in_specs=[VM, SM] + [VM] * 6,
        out_specs=(VM,) * 4,
        scratch_shapes=[
            pltpu.VMEM((PUP, N), f32),
            pltpu.VMEM((PUP * SLOTS, N), bf16),
            pltpu.VMEM((PUP * SLOTS, N), bf16),
            pltpu.VMEM((PUP * SLOTS, N), f32),
            pltpu.VMEM((PUP * SLOTS, N), f32),
            pltpu.VMEM((rows, 2 * N), bf16),
            pltpu.VMEM((rows, 2 * N), bf16),
        ],
        interpret=interpret,
        name="transfer",
    )(
        coef, chan, mask, tabs["phase"], tabs["right_pupil"], tabs["left_pupil"],
        tabs["left_half"], tabs["right_full"],
    )


def objects(width, chan, pixels, otf, tabs, interpret=False):
    rows = SLOTS * HALF
    return pl.pallas_call(
        object_kernel,
        out_shape=(
            jax.ShapeDtypeStruct((rows, 2 * N), f32),
            jax.ShapeDtypeStruct((CHANNELS + 1, N, N), f32),
        ),
        in_specs=[SM, SM] + [VM] * 8,
        out_specs=(VM,) * 2,
        scratch_shapes=[
            pltpu.SMEM((SLOTS,), jnp.int32),
            pltpu.VMEM((rows, 2 * N), bf16),
            pltpu.VMEM((rows, 2 * N), bf16),
            pltpu.VMEM((rows, 2 * N), f32),
            pltpu.VMEM((TWO, 2 * N), f32),
        ],
        interpret=interpret,
        name="objects",
    )(
        width, chan, pixels, otf, tabs["left_taper"], tabs["taper"], tabs["weight"],
        tabs["right_full"], tabs["right_back"], tabs["left_back"],
    )


def gradient(chan, grad, field, slope, inverse, tabs, interpret=False):
    rows = SLOTS * HALF
    return pl.pallas_call(
        gradient_kernel,
        out_shape=jax.ShapeDtypeStruct((SLOTS, COEF), f32),
        in_specs=[SM] + [VM] * 9,
        out_specs=VM,
        scratch_shapes=[
            pltpu.VMEM((rows, 2 * N), f32),
            pltpu.VMEM((SLOTS * PUP, 2 * N), bf16),
            pltpu.VMEM((SLOTS * PUP, 2 * N), bf16),
            pltpu.VMEM((SLOTS * PUP, N), f32),
        ],
        interpret=interpret,
        name="gradient",
    )(
        chan, grad, field, slope, inverse, tabs["phase"], tabs["right_back"], tabs["left_back"],
        tabs["right_pupil"], tabs["left_pupil"],
    )


def padded(cells, sides, width):
    for axis, dim in sides:
        count = lax.axis_size(axis)
        ends = count - 1
        head = lax.slice_in_dim(cells, 0, width, axis=dim)
        tail = lax.slice_in_dim(cells, cells.shape[dim] - width, cells.shape[dim], axis=dim)
        cells = jnp.concatenate(
            [
                lax.ppermute(tail, axis, [(i, (i + 1) % count) for i in range(ends)]),
                cells,
                lax.ppermute(head, axis, [((i + 1) % count, i) for i in range(ends)]),
            ],
            axis=dim,
        )
    return cells


def fold_margins(extended, axis_num, margin):
    span = extended.shape[axis_num] - 4 * margin
    upper_part = lax.slice_in_dim(extended, 0, margin, axis=axis_num)
    middle = lax.slice_in_dim(extended, 2 * margin, 2 * margin + span, axis=axis_num)
    lower_part = lax.slice_in_dim(extended, span + 3 * margin, span + 4 * margin, axis=axis_num)
    pad_upper = [(0, 0)] * extended.ndim
    pad_lower = [(0, 0)] * extended.ndim
    pad_upper[axis_num] = (0, span - margin)
    pad_lower[axis_num] = (span - margin, 0)
    return middle + jnp.pad(upper_part, pad_upper) + jnp.pad(lower_part, pad_lower)


def per_device(coeffs, shifts, pixels, pupil_mask, chan_map, intersection):
    tabs = {name: jnp.asarray(table) for name, table in tables()[0].items()}
    spare = jnp.zeros(coeffs.shape[:3] + (COEF - ZERN - 2,), f32)
    small = jnp.concatenate([coeffs, shifts.astype(f32), spare], axis=3)
    small = lax.all_to_all(small, "patch", split_axis=1, concat_axis=0, tiled=True)
    frames = lax.all_to_all(pixels, "patch", split_axis=1, concat_axis=0, tiled=True)
    otf, field, slope, inverse = transfer(small.reshape(SLOTS, COEF), chan_map, pupil_mask, tabs)
    grad, canvas = objects(
        intersection.reshape(1), chan_map, frames.reshape(SLOTS, N, N), otf, tabs
    )
    grad = gradient(chan_map, grad, field, slope, inverse, tabs)
    grad = lax.all_to_all(
        grad.reshape(SLOTS, 1, 1, COEF), "patch", split_axis=0, concat_axis=1, tiled=True
    )
    extended = padded(canvas, (("frame", 2), ("patch", 1)), MARGIN)
    folded = fold_margins(fold_margins(extended, 1, MARGIN), 2, MARGIN)
    blended = folded[:CHANNELS] / folded[CHANNELS][None]
    return (blended, grad[..., :ZERN])


def solution(mesh):
    in_specs = (
        P("patch", None, "frame", None),
        P("patch", None, "frame", None),
        P("patch", None, "frame", None, None),
        P(),
        P(),
        P("patch", "frame"),
    )
    out_specs = (P(None, "patch", "frame"), P("patch", None, "frame", None))
    return jax.shard_map(
        per_device, mesh=mesh, in_specs=in_specs, out_specs=out_specs, check_vma=False
    )
```

time: 146 us -> 83.8 us (0.57)
  matrix products: 38.8 us -> 0 us
  other arithmetic: 31.4 us -> 2.61 us
  local copies, waits for them, and re-layouts: 22.7 us -> 2.79 us
  Pallas kernels: 0 us -> 17.6 us
  blocking collectives: 10.7 us -> 24.9 us
  starting transfers between devices: 33.4 us -> 21.4 us
  waiting for transfers between devices: 5.61 us -> 12.5 us
    dot_general x23 -> x0, matrix products: 38.8 us -> none  [the longest x21 36.8 us: product(): return jnp.einsum(form, left, right, precision=highest)]
    pallas_call x0 -> x3, Pallas kernels: none -> 17.6 us  [the longest x1 7.37 us: transfer(): pl.pallas_call(transfer_kernel, out_shape=(jax.ShapeDtypeStruct((rows, 2...]
    mul x13 -> x0, other arithmetic: 15 us -> none  [the longest x1 7.64 us: build_otf(): otf[1] * tilt_re]
    all_to_all x1 -> x2, blocking collectives: 10.7 us -> 24.9 us  [the longest x1 14.7 us: per_device(): lax.all_to_all(small, 'patch', split_axis=1, concat_axis=0, tiled=True)]
    all_to_all x1 -> x0, starting transfers between devices: 7.79 us -> none  [per_device(): lax.all_to_all(small, 'patch', split_axis=1, concat_axis=0, tiled=True)]
    sub x1 -> x0, other arithmetic: 5.56 us -> none  [wiener_terms(): cross_im = otf_re * spec_im - otf_im * spec_re]
    add x2 -> x0, local copies, waits for them, and re-layouts: 5.21 us -> none  [the longest x1 2.62 us: wiener_terms(): cross_re = otf_re * spec_re + otf_im * spec_im]
    dot_general x2 -> x0, local copies, waits for them, and re-layouts: 5.11 us -> none  [product(): return jnp.einsum(form, left, right, precision=highest)]
  transfers between devices with their start and end apart: 6 -> 5, of which waited for: 1 -> 2; matrix products, arithmetic and copies ran while one was open for 31% -> 0% of each run, Pallas kernels for 0% -> 16%
where the time goes in v1:
time: 83.8 us; the launch traced here: 83.3 us
  blocking collectives  24.9 us (30%)
  starting transfers between devices  21.4 us (26%)
  Pallas kernels  17.6 us (21%)
  waiting for transfers between devices  12.5 us (15%)
  local copies, waits for them, and re-layouts  2.79 us (3%)
  other arithmetic  2.61 us (3%)
  between operations  1.41 us (2%)
    all_to_all x1, blocking collectives, per_device(): lax.all_to_all(small, 'patch', split_axis=1, concat_axis=0, tiled=True)  14.7 us
    ppermute x2, starting transfers between devices, padded(): lax.ppermute(head, axis, [((i + 1) % count, i) for i in range(ends)])  10.8 us
    all_to_all x1, blocking collectives, per_device(): lax.all_to_all(grad.reshape(SLOTS, 1, 1, COEF), 'patch', split_axis=0, co...  10.2 us
    all_to_all x1, waiting for transfers between devices, per_device(): lax.all_to_all(pixels, 'patch', split_axis=1, concat_axis=0, tiled=True)  9.29 us
    pallas_call x1, Pallas kernels, transfer(): pl.pallas_call(transfer_kernel, out_shape=(jax.ShapeDtypeStruct((rows, 2...  7.37 us
    ppermute x2, starting transfers between devices, padded(): lax.ppermute(tail, axis, [(i, (i + 1) % count) for i in range(ends)])  6.72 us
    pallas_call x1, Pallas kernels, gradient(): pl.pallas_call(gradient_kernel, out_shape=jax.ShapeDtypeStruct((SLOTS, CO...  5.91 us
    pallas_call x1, Pallas kernels, objects(): pl.pallas_call(object_kernel, out_shape=(jax.ShapeDtypeStruct((rows, 2 *...  4.35 us
  transfers between devices with their start and end apart: 5, of which 2 were waited for; matrix products, arithmetic and copies ran while one was open for 0% of the time, Pallas kernels for 16%

profile of v1, /device:TPU:7, one launch (start us, length us, event | category | flops | bytes accessed | tf_op | source)
XLA Modules:
  0.0 83.3 jit_solution(15578626678697743000)
XLA Ops:
  0.6 0.7 convert_element_type.11
  1.3 0.1 copy.24
  1.4 0.1 pad.25.clone
  1.5 0.8 maximum_maximum_fusion
  2.3 14.7 %all_to_all.30 = f32[1,16,1,40]{3,2,0,1:T(1,128)} all-to-all(f32[1,16,1,40]{3,2,0,1:T(1,128)S(1)} %maximum_maximum_fusion), channel_id=1, replica_groups=mesh['frame'=32,'patch'=16] {'patch'}, dimensions={1} | all-to-all | bytes 5120 | tf_op jit(solution)/shard_map/all_to_all | solution.py:487
  17.0 3.9 %all-to-all-start = ((bf16[1,16,1,128,128]{4,3,2,0,1:T(8,128)(2,1)}), bf16[1,16,1,128,128]{4,3,2,0,1:T(8,128)(2,1)S(1)}, u32[]{:S(2)}, u32[]{:S(2)}) async-start(bf16[1,16,1,128,128]{4,3,2,0,1:T(8,128)(2,1)} %bitcast.15), calls=%async_computation | async-start | bytes 1048576 | tf_op jit(solution)/shard_map/all_to_all | solution.py:488
  21.5 7.4 %transfer.1 = (f32[1152,256]{1,0:T(8,128)}, f32[8,256,256]{2,1,0:T(8,128)}, f32[1024,128]{1,0:T(8,128)}, f32[16,128]{1,0:T(8,128)}) custom-call(f32[16,40]{1,0:T(8,128)} %bitcast.16, s32[16]{0:T(128)} %chan_ref.5, s32[64,64]{1,0:T(8,128)} %mask_ref.1, f32[40,1152]{1,0:T(8,128)} %constant.35.clone.phase_ref, bf16[2,128,256]{2,1,0:T(8,128)(2,1)} %constant.26.clone.rp_ref, ...), custom_call_target="tpu_custom_call" | custom-call | tf_op jit(solution)/shard_map/transfer/pallas_call | solution.py:381
  28.9 9.3 %all-to-all-done = bf16[1,16,1,128,128]{4,3,2,0,1:T(8,128)(2,1)S(1)} async-done(((bf16[1,16,1,128,128]{4,3,2,0,1:T(8,128)(2,1)}), bf16[1,16,1,128,128]{4,3,2,0,1:T(8,128)(2,1)S(1)}, u32[]{:S(2)}, u32[]{:S(2)}) %all-to-all-start) | async-done | bytes 524320 | tf_op jit(solution)/shard_map/all_to_all | solution.py:488
  38.2 0.0 copy-start.1
  38.2 0.8 copy-done.1
  39.0 4.3 %objects.1 = (f32[1152,256]{1,0:T(8,128)}, f32[3,128,128]{2,1,0:T(8,128)}) custom-call(s32[1]{0:T(128)} %bitcast.13.width_ref, s32[16]{0:T(128)} %chan_ref.5, bf16[16,128,128]{2,1,0:T(8,128)(2,1)} %bitcast.14, f32[1152,256]{1,0:T(8,128)} %get-tuple-element.8.otf_ref, bf16[144,256]{1,0:T(8,128)(2,1)} %constant.31.clone.lt_ref, ...), custom_call_target="tpu_custom_call" | custom-call | tf_op jit(solution)/shard_map/objects/pallas_call | solution.py:410
  43.3 1.1 %fusion.3 = (f32[3,128,16]{2,1,0:T(8,128)S(1)}, f32[3,128,16]{2,1,0:T(8,128)S(1)}) fusion(f32[3,128,128]{2,1,0:T(8,128)} %get-tuple-element.9), kind=kLoop, calls=%fused_computation.11 | loop fusion | bytes 98304 | tf_op jit(solution)/shard_map/slice | solution.py:459
  44.5 4.0 %collective-permute-start = (f32[3,128,16]{2,1,0:T(8,128)S(1)}, f32[3,128,16]{2,1,0:T(8,128)S(1)}, u32[]{:S(2)}, u32[]{:S(2)}) collective-permute-start(f32[3,128,16]{2,1,0:T(8,128)S(1)} %get-tuple-element.20), channel_id=1, source_target_pairs={{0,16},{16,32},{32,48},{48,64},{64,80},{80,96},{96,112},{112,128},... | collective-permute-start | bytes 73736 | tf_op jit(solution)/shard_map/ppermute | solution.py:462
  48.5 8.9 %collective-permute-start.1 = (f32[3,128,16]{2,1,0:T(8,128)S(1)}, f32[3,128,16]{2,1,0:T(8,128)S(1)}, u32[]{:S(2)}, u32[]{:S(2)}) collective-permute-start(f32[3,128,16]{2,1,0:T(8,128)S(1)} %get-tuple-element.21), channel_id=1, source_target_pairs={{16,0},{32,16},{48,32},{64,48},{80,64},{96,80},{112,96},{128,112},... | collective-permute-start | bytes 73736 | tf_op jit(solution)/shard_map/ppermute | solution.py:464
  57.3 0.0 copy-start
  57.3 5.9 %gradient.1 = f32[16,40]{1,0:T(8,128)} custom-call(s32[16]{0:T(128)} %chan_ref.5, f32[1152,256]{1,0:T(8,128)} %get-tuple-element.10.grad_ref, f32[8,256,256]{2,1,0:T(8,128)} %get-tuple-element.11.field_ref, f32[1024,128]{1,0:T(8,128)} %get-tuple-element.12.slope_ref, f32[16,128]{1,0:T(8,128)} %get-tuple-element.13.inv_ref, ...), custom_call_target="tpu_custom_call" | custom-call | tf_op jit(solution)/shard_map/gradient/pallas_call | solution.py:435
  63.3 10.2 %all_to_all.31 = f32[16,1,1,40]{3,2,1,0:T(1,128)S(1)} all-to-all(f32[16,1,1,40]{3,2,1,0:T(1,128)} %bitcast.17), channel_id=1, replica_groups=mesh['frame'=32,'patch'=16] {'patch'}, dimensions={0} | all-to-all | bytes 5120 | tf_op jit(solution)/shard_map/all_to_all | solution.py:494
  73.4 0.0 copy-start.2
  73.4 0.0 collective-permute-done
  73.4 0.0 collective-permute-done.1
  73.4 0.0 copy-done
  73.4 0.1 pad_maximum_fusion.2
  73.6 2.7 %collective-permute-start.2 = (f32[3,16,160]{2,1,0:T(8,128)S(1)}, f32[3,16,160]{2,1,0:T(8,128)S(1)}, u32[]{:S(2)}, u32[]{:S(2)}) collective-permute-start(f32[3,16,160]{2,1,0:T(8,128)S(1)} %get-tuple-element.18), channel_id=1, source_target_pairs={{0,1},{1,2},{2,3},{3,4},{4,5},{5,6},{6,7},{7,8},{8,9},{9,10},{10,1... | collective-permute-start | bytes 92168 | tf_op jit(solution)/shard_map/ppermute | solution.py:462
  76.3 1.9 %collective-permute-start.3 = (f32[3,16,160]{2,1,0:T(8,128)S(1)}, f32[3,16,160]{2,1,0:T(8,128)S(1)}, u32[]{:S(2)}, u32[]{:S(2)}) collective-permute-start(f32[3,16,160]{2,1,0:T(8,128)S(1)} %get-tuple-element.19), channel_id=1, source_target_pairs={{1,0},{2,1},{3,2},{4,3},{5,4},{6,5},{7,6},{8,7},{9,8},{10,9},{11,1... | collective-permute-start | bytes 92168 | tf_op jit(solution)/shard_map/ppermute | solution.py:464
  78.2 0.2 pad_maximum_fusion
  78.4 0.0 collective-permute-done.2
  78.4 3.2 %collective-permute-done.3 = f32[3,16,160]{2,1,0:T(8,128)S(1)} collective-permute-done((f32[3,16,160]{2,1,0:T(8,128)S(1)}, f32[3,16,160]{2,1,0:T(8,128)S(1)}, u32[]{:S(2)}, u32[]{:S(2)}) %collective-permute-start.3) | collective-permute-done | bytes 30752 | tf_op jit(solution)/shard_map/ppermute | solution.py:464
  81.7 0.1 slice.48
  81.8 0.0 copy-done.2
  81.8 0.1 fusion.2
  82.0 0.7 slice_divide_fusion
  82.7 0.6 copy.29
  (3 shorter events, 0.0 us)
Async XLA Ops:
  17.0 21.2 %all-to-all-start = ((bf16[1,16,1,128,128]{4,3,2,0,1:T(8,128)(2,1)}), bf16[1,16,1,128,128]{4,3,2,0,1:T(8,128)(2,1)S(1)}, u32[]{:S(2)}, u32[]{:S(2)}) async-start(bf16[1,16,1,128,128]{4,3,2,0,1:T(8,128)(2,1)} %bitcast.15), calls=%async_computation | async-start | bytes 1048576 | tf_op jit(solution)/shard_map/all_to_all | solution.py:488
  38.2 0.8 copy-start.1
  44.5 29.0 %collective-permute-start = (f32[3,128,16]{2,1,0:T(8,128)S(1)}, f32[3,128,16]{2,1,0:T(8,128)S(1)}, u32[]{:S(2)}, u32[]{:S(2)}) collective-permute-start(f32[3,128,16]{2,1,0:T(8,128)S(1)} %get-tuple-element.20), channel_id=1, source_target_pairs={{0,16},{16,32},{32,48},{48,64},{64,80},{80,96},{96,112},{112,128},... | collective-permute-start | bytes 73736 | tf_op jit(solution)/shard_map/ppermute | solution.py:462
  48.5 25.0 %collective-permute-start.1 = (f32[3,128,16]{2,1,0:T(8,128)S(1)}, f32[3,128,16]{2,1,0:T(8,128)S(1)}, u32[]{:S(2)}, u32[]{:S(2)}) collective-permute-start(f32[3,128,16]{2,1,0:T(8,128)S(1)} %get-tuple-element.21), channel_id=1, source_target_pairs={{16,0},{32,16},{48,32},{64,48},{80,64},{96,80},{112,96},{128,112},... | collective-permute-start | bytes 73736 | tf_op jit(solution)/shard_map/ppermute | solution.py:464
  57.3 16.1 %copy-start = (f32[3,128,128]{2,1,0:T(8,128)S(1)}, f32[3,128,128]{2,1,0:T(8,128)}, u32[]{:S(2)}) copy-start(f32[3,128,128]{2,1,0:T(8,128)} %get-tuple-element.9) | copy-start | bytes 589828
  73.4 8.4 %copy-start.2 = (pred[96]{0:T(512)(128)(4,1)S(1)}, pred[96]{0:T(512)(128)(4,1)}, u32[]{:S(2)}) copy-start(pred[96]{0:T(512)(128)(4,1)} %constant.25.clone.1) | copy-start | bytes 292
  73.6 4.9 %collective-permute-start.2 = (f32[3,16,160]{2,1,0:T(8,128)S(1)}, f32[3,16,160]{2,1,0:T(8,128)S(1)}, u32[]{:S(2)}, u32[]{:S(2)}) collective-permute-start(f32[3,16,160]{2,1,0:T(8,128)S(1)} %get-tuple-element.18), channel_id=1, source_target_pairs={{0,1},{1,2},{2,3},{3,4},{4,5},{5,6},{6,7},{7,8},{8,9},{9,10},{10,1... | collective-permute-start | bytes 92168 | tf_op jit(solution)/shard_map/ppermute | solution.py:462
  76.3 5.4 %collective-permute-start.3 = (f32[3,16,160]{2,1,0:T(8,128)S(1)}, f32[3,16,160]{2,1,0:T(8,128)S(1)}, u32[]{:S(2)}, u32[]{:S(2)}) collective-permute-start(f32[3,16,160]{2,1,0:T(8,128)S(1)} %get-tuple-element.19), channel_id=1, source_target_pairs={{1,0},{2,1},{3,2},{4,3},{5,4},{6,5},{7,6},{8,7},{9,8},{10,9},{11,1... | collective-permute-start | bytes 92168 | tf_op jit(solution)/shard_map/ppermute | solution.py:464

commit v2 on v1

--- a/solution.py
+++ b/solution.py
@@ -10,6 +10,7 @@
 from jax.experimental.pallas import tpu as pltpu
 from jax.sharding import PartitionSpec as P
 
+
 N = 128
 PUP = 64
 ZERN = 36
@@ -18,10 +19,12 @@
 CHANNELS = 2
 PER = SLOTS // CHANNELS
 MARGIN = 16
+TILE = N - 2 * MARGIN
 HALF = 72
 TWO = 2 * HALF
 DEG = 9
 COEF = 40
+ROWS = N + 8
 regular_gamma = 0.1
 wave_ratio = 0.35
 f32 = jnp.float32
@@ -183,14 +186,19 @@
     return 1.0 / (1.0 + wave_ratio * channel.astype(f32))
 
 
-def transfer_kernel(
-    coef_ref, chan_ref, mask_ref, phase_ref, rp_ref, lp_ref, lh_ref, rf_ref,
+def transfer_part(
+    data_ref, chan_ref, mask_ref, phase_ref, rp_ref, lp_ref, lh_ref, rf_ref, ready,
     otf_ref, field_ref, slope_ref, inv_ref,
-    wide_ref, ph_ref, pl_ref, half_re_ref, half_im_ref, yh_ref, yl_ref,
+    line_ref, wide_ref, ph_ref, pl_ref, half_re_ref, half_im_ref, yh_ref, yl_ref,
 ):
     cheb = tables()[1]
-    lane = lax.broadcasted_iota(jnp.int32, (SLOTS, COEF), 1)
-    coef = coef_ref[...] * jnp.where(lane < ZERN, slot_scales(chan_ref, COEF), 1.0)
+    for slot in range(SLOTS):
+        line_ref[slot * 8 : slot * 8 + 8, :] = data_ref[slot, N:, :].astype(f32)
+    line = line_ref[pl.ds(0, SLOTS, stride=8), :]
+    coef = line + (pltpu.roll(line, N - ZERN, 1) + pltpu.roll(line, N - 2 * ZERN, 1))
+    lane = lax.broadcasted_iota(jnp.int32, (SLOTS, N), 1)
+    shift = pltpu.roll(line, N - 2 * ZERN, 1)
+    coef = jnp.where(lane < ZERN, coef * slot_scales(chan_ref, N), shift)[:, :COEF]
     mask = mask_ref[...].astype(f32)
     wide_ref[...] = jnp.concatenate([mask, mask], axis=1)
     parts_all = lax.dot_general(
@@ -210,6 +218,7 @@
             high, low = split(value)
             ph_ref[here, :] = high
             pl_ref[here, :] = low
+    ready()
     right = table_rows(rp_ref)
     for chunk in range(4):
         here = slice(chunk * 256, (chunk + 1) * 256)
@@ -252,9 +261,9 @@
             inv_ref[slot : slot + 1, :] = jnp.broadcast_to(inverse, (1, N))
 
 
-def object_kernel(
+def object_part(
     width_ref, chan_ref, pix_ref, otf_ref, lt_ref, taper_ref, weight_ref, rf_ref, rb_ref, lb_ref,
-    grad_ref, canvas_ref,
+    grad_ref, canvas_ref, head_ref, tail_ref,
     order_ref, yh_ref, yl_ref, spec_ref, object_ref,
 ):
     at = [jnp.int32(0), jnp.int32(PER)]
@@ -265,7 +274,7 @@
     left = lt_ref[...]
     taper = taper_ref[...]
     for pair in range(PAIRS):
-        image = jnp.concatenate([pix_ref[2 * pair], pix_ref[2 * pair + 1]], axis=1)
+        image = jnp.concatenate([pix_ref[2 * pair, :N, :], pix_ref[2 * pair + 1, :N, :]], axis=1)
         y = dot(left, jnp.concatenate([image, image], axis=0)) * taper
         high, low = split(swap_halves(y, HALF))
         here = slice(pair * TWO, (pair + 1) * TWO)
@@ -325,9 +334,114 @@
         return jnp.minimum(1.0, distance / width)
 
     weight = ramp(row) * ramp(col)
-    canvas_ref[0] = image[:, :N] * weight
-    canvas_ref[1] = image[:, N:] * weight
-    canvas_ref[2] = weight
+    head_ref[CHANNELS] = weight[:MARGIN]
+    tail_ref[CHANNELS] = weight[N - MARGIN :]
+    canvas_ref[CHANNELS] = weight
+    for channel in range(CHANNELS):
+        shown = image[:, channel * N : (channel + 1) * N] * weight
+        canvas_ref[channel] = shown
+        turned = shown.T
+        head_ref[channel] = turned[:MARGIN]
+        tail_ref[channel] = turned[N - MARGIN :]
+
+
+TABLES = ("right_pupil", "left_pupil", "left_half", "right_full", "right_back", "left_back")
+
+
+def object_kernel(
+    width_ref, chan_ref, data_ref, mask_ref, phase_ref, lt_ref, taper_ref, weight_ref,
+    rp_hbm, lp_hbm, lh_hbm, rf_hbm, rb_hbm, lb_hbm,
+    grad_ref, field_ref, slope_ref, inv_ref, canvas_ref, head_ref, tail_ref,
+    rp_ref, lp_ref, lh_ref, rf_ref, rb_ref, lb_ref, sems,
+    otf_ref, line_ref, wide_ref, ph_ref, pl_ref, half_re_ref, half_im_ref, yh_ref, yl_ref,
+    order_ref, sh_ref, sl_ref, spec_ref, object_ref,
+):
+    moves = (
+        (rp_hbm, rp_ref), (lp_hbm, lp_ref), (lh_hbm, lh_ref),
+        (rf_hbm, rf_ref), (rb_hbm, rb_ref), (lb_hbm, lb_ref),
+    )
+    copies = [
+        pltpu.make_async_copy(source, target, sems.at[i])
+        for i, (source, target) in enumerate(moves)
+    ]
+    for copy in copies:
+        copy.start()
+
+    def ready():
+        for copy in copies:
+            copy.wait()
+
+    transfer_part(
+        data_ref, chan_ref, mask_ref, phase_ref, rp_ref, lp_ref, lh_ref, rf_ref, ready,
+        otf_ref, field_ref, slope_ref, inv_ref,
+        line_ref, wide_ref, ph_ref, pl_ref, half_re_ref, half_im_ref, yh_ref, yl_ref,
+    )
+    object_part(
+        width_ref, chan_ref, data_ref, otf_ref, lt_ref, taper_ref, weight_ref, rf_ref, rb_ref,
+        lb_ref, grad_ref, canvas_ref, head_ref, tail_ref,
+        order_ref, sh_ref, sl_ref, spec_ref, object_ref,
+    )
+
+
+def pack_kernel(coef_ref, shift_ref, pix_ref, out_ref, sem):
+    copy = pltpu.make_async_copy(pix_ref, out_ref.at[:, :N, :], sem)
+    copy.start()
+    coef = jnp.concatenate([coef_ref[...], jnp.zeros((SLOTS, N - ZERN), f32)], axis=1)
+    first = coef.astype(bf16).astype(f32)
+    rest = coef - first
+    second = rest.astype(bf16).astype(f32)
+    third = rest - second
+    shift = jnp.concatenate([shift_ref[...].astype(f32), jnp.zeros((6, SLOTS), f32)], axis=0)
+    shift = jnp.concatenate([shift, jnp.zeros((8, N - SLOTS), f32)], axis=1)
+    shift = jnp.concatenate([shift, jnp.zeros((N - 8, N), f32)], axis=0).T[:SLOTS]
+    line = first + pltpu.roll(second, ZERN, 1) + pltpu.roll(third, 2 * ZERN, 1)
+    line = line + pltpu.roll(shift, 3 * ZERN, 1)
+    for slot in range(SLOTS):
+        out_ref[slot, N:, :] = jnp.broadcast_to(line[slot : slot + 1], (8, N)).astype(bf16)
+    copy.wait()
+
+
+def pack(coef, shift, pixels):
+    return pl.pallas_call(
+        pack_kernel,
+        out_shape=jax.ShapeDtypeStruct((SLOTS, ROWS, N), bf16),
+        in_specs=[VM, VM, pl.BlockSpec(memory_space=pl.ANY)],
+        out_specs=VM,
+        scratch_shapes=[pltpu.SemaphoreType.DMA],
+        name="pack",
+        compiler_params=limit(4),
+    )(coef, shift, pixels)
+
+
+def fold_kernel(
+    canvas_ref, left_ref, right_ref, grad_ref,
+    middle_ref, head_ref, tail_ref, out_ref,
+):
+    out_ref[...] = grad_ref[...]
+    gap = jnp.zeros((TILE - 2 * MARGIN, N), f32)
+    rest = jnp.zeros((N - TILE, N), f32)
+    for layer in range(CHANNELS + 1):
+        sides = jnp.concatenate([left_ref[layer], gap, right_ref[layer], rest], axis=0).T
+        total = pltpu.roll(canvas_ref[layer], N - MARGIN, 1) + sides
+        head_ref[layer] = total[:MARGIN]
+        middle_ref[layer] = total[MARGIN : N - MARGIN]
+        tail_ref[layer] = total[N - MARGIN :]
+
+
+def blend_kernel(middle_ref, upper_ref, lower_ref, out_ref):
+    def folded(layer):
+        return jnp.concatenate(
+            [
+                middle_ref[layer, :MARGIN] + upper_ref[layer],
+                middle_ref[layer, MARGIN : TILE - MARGIN],
+                middle_ref[layer, TILE - MARGIN :] + lower_ref[layer],
+            ],
+            axis=0,
+        )
+
+    weight = folded(CHANNELS)
+    for channel in range(CHANNELS):
+        out_ref[channel] = (folded(channel) / weight)[:, :TILE]
 
 
 def gradient_kernel(
@@ -373,22 +487,36 @@
         precision=lax.Precision.HIGHEST, preferred_element_type=f32,
     )
     factor = 4.0 / float(N * N * N)
-    out_ref[...] = total * (slot_scales(chan_ref, COEF) * factor * inv_ref[:, :COEF])
-
-
-def transfer(coef, chan, mask, tabs, interpret=False):
+    total = total * (slot_scales(chan_ref, COEF) * factor * inv_ref[:, :COEF])
+    out_ref[...] = total[:, :ZERN]
+
+
+def limit(mib):
+    return pltpu.CompilerParams(vmem_limit_bytes=mib << 20)
+
+
+def objects(width, chan, data, mask, tabs, interpret=False):
     rows = SLOTS * HALF
+    margin = jax.ShapeDtypeStruct((CHANNELS + 1, MARGIN, N), f32)
+    fixed = [tabs[name] for name in TABLES]
     return pl.pallas_call(
-        transfer_kernel,
+        object_kernel,
         out_shape=(
             jax.ShapeDtypeStruct((rows, 2 * N), f32),
             jax.ShapeDtypeStruct((PAIRS, 2 * N, 2 * N), f32),
             jax.ShapeDtypeStruct((PUP * SLOTS, N), f32),
             jax.ShapeDtypeStruct((SLOTS, N), f32),
+            jax.ShapeDtypeStruct((CHANNELS + 1, N, N), f32),
+            margin,
+            margin,
         ),
-        in_specs=[VM, SM] + [VM] * 6,
-        out_specs=(VM,) * 4,
-        scratch_shapes=[
+        in_specs=[SM, SM] + [VM] * 6 + [pl.BlockSpec(memory_space=pltpu.HBM)] * len(TABLES),
+        out_specs=(VM,) * 7,
+        scratch_shapes=[pltpu.VMEM(table.shape, bf16) for table in fixed]
+        + [
+            pltpu.SemaphoreType.DMA((len(TABLES),)),
+            pltpu.VMEM((rows, 2 * N), f32),
+            pltpu.VMEM((SLOTS * 8, N), f32),
             pltpu.VMEM((PUP, N), f32),
             pltpu.VMEM((PUP * SLOTS, N), bf16),
             pltpu.VMEM((PUP * SLOTS, N), bf16),
@@ -396,26 +524,6 @@
             pltpu.VMEM((PUP * SLOTS, N), f32),
             pltpu.VMEM((rows, 2 * N), bf16),
             pltpu.VMEM((rows, 2 * N), bf16),
-        ],
-        interpret=interpret,
-        name="transfer",
-    )(
-        coef, chan, mask, tabs["phase"], tabs["right_pupil"], tabs["left_pupil"],
-        tabs["left_half"], tabs["right_full"],
-    )
-
-
-def objects(width, chan, pixels, otf, tabs, interpret=False):
-    rows = SLOTS * HALF
-    return pl.pallas_call(
-        object_kernel,
-        out_shape=(
-            jax.ShapeDtypeStruct((rows, 2 * N), f32),
-            jax.ShapeDtypeStruct((CHANNELS + 1, N, N), f32),
-        ),
-        in_specs=[SM, SM] + [VM] * 8,
-        out_specs=(VM,) * 2,
-        scratch_shapes=[
             pltpu.SMEM((SLOTS,), jnp.int32),
             pltpu.VMEM((rows, 2 * N), bf16),
             pltpu.VMEM((rows, 2 * N), bf16),
@@ -424,9 +532,10 @@
         ],
         interpret=interpret,
         name="objects",
+        compiler_params=limit(16),
     )(
-        width, chan, pixels, otf, tabs["left_taper"], tabs["taper"], tabs["weight"],
-        tabs["right_full"], tabs["right_back"], tabs["left_back"],
+        width, chan, data, mask, tabs["phase"], tabs["left_taper"], tabs["taper"], tabs["weight"],
+        *fixed,
     )
 
 
@@ -434,7 +543,7 @@
     rows = SLOTS * HALF
     return pl.pallas_call(
         gradient_kernel,
-        out_shape=jax.ShapeDtypeStruct((SLOTS, COEF), f32),
+        out_shape=jax.ShapeDtypeStruct((SLOTS, ZERN), f32),
         in_specs=[SM] + [VM] * 9,
         out_specs=VM,
         scratch_shapes=[
@@ -445,59 +554,68 @@
         ],
         interpret=interpret,
         name="gradient",
+        compiler_params=limit(16),
     )(
         chan, grad, field, slope, inverse, tabs["phase"], tabs["right_back"], tabs["left_back"],
         tabs["right_pupil"], tabs["left_pupil"],
     )
 
 
-def padded(cells, sides, width):
-    for axis, dim in sides:
-        count = lax.axis_size(axis)
-        ends = count - 1
-        head = lax.slice_in_dim(cells, 0, width, axis=dim)
-        tail = lax.slice_in_dim(cells, cells.shape[dim] - width, cells.shape[dim], axis=dim)
-        cells = jnp.concatenate(
-            [
-                lax.ppermute(tail, axis, [(i, (i + 1) % count) for i in range(ends)]),
-                cells,
-                lax.ppermute(head, axis, [((i + 1) % count, i) for i in range(ends)]),
-            ],
-            axis=dim,
-        )
-    return cells
-
-
-def fold_margins(extended, axis_num, margin):
-    span = extended.shape[axis_num] - 4 * margin
-    upper_part = lax.slice_in_dim(extended, 0, margin, axis=axis_num)
-    middle = lax.slice_in_dim(extended, 2 * margin, 2 * margin + span, axis=axis_num)
-    lower_part = lax.slice_in_dim(extended, span + 3 * margin, span + 4 * margin, axis=axis_num)
-    pad_upper = [(0, 0)] * extended.ndim
-    pad_lower = [(0, 0)] * extended.ndim
-    pad_upper[axis_num] = (0, span - margin)
-    pad_lower[axis_num] = (span - margin, 0)
-    return middle + jnp.pad(upper_part, pad_upper) + jnp.pad(lower_part, pad_lower)
+def fold(canvas, left, right, grad):
+    margin = jax.ShapeDtypeStruct((CHANNELS + 1, MARGIN, N), f32)
+    return pl.pallas_call(
+        fold_kernel,
+        out_shape=(
+            jax.ShapeDtypeStruct((CHANNELS + 1, TILE, N), f32),
+            margin,
+            margin,
+            jax.ShapeDtypeStruct((SLOTS, ZERN), f32),
+        ),
+        in_specs=[VM] * 4,
+        out_specs=(VM,) * 4,
+        name="fold",
+        compiler_params=limit(8),
+    )(canvas, left, right, grad)
+
+
+def blend(middle, upper, lower):
+    return pl.pallas_call(
+        blend_kernel,
+        out_shape=jax.ShapeDtypeStruct((CHANNELS, TILE, TILE), f32),
+        in_specs=[VM] * 3,
+        out_specs=VM,
+        name="blend",
+        compiler_params=limit(8),
+    )(middle, upper, lower)
+
+
+def shifted(cells, axis, forward):
+    ends = lax.axis_size(axis) - 1
+    if forward:
+        return lax.ppermute(cells, axis, [(i, i + 1) for i in range(ends)])
+    return lax.ppermute(cells, axis, [(i + 1, i) for i in range(ends)])
 
 
 def per_device(coeffs, shifts, pixels, pupil_mask, chan_map, intersection):
     tabs = {name: jnp.asarray(table) for name, table in tables()[0].items()}
-    spare = jnp.zeros(coeffs.shape[:3] + (COEF - ZERN - 2,), f32)
-    small = jnp.concatenate([coeffs, shifts.astype(f32), spare], axis=3)
-    small = lax.all_to_all(small, "patch", split_axis=1, concat_axis=0, tiled=True)
-    frames = lax.all_to_all(pixels, "patch", split_axis=1, concat_axis=0, tiled=True)
-    otf, field, slope, inverse = transfer(small.reshape(SLOTS, COEF), chan_map, pupil_mask, tabs)
-    grad, canvas = objects(
-        intersection.reshape(1), chan_map, frames.reshape(SLOTS, N, N), otf, tabs
-    )
+    coef = coeffs.reshape(SLOTS, ZERN)
+    shift = shifts.reshape(SLOTS, 2).T
+    data = pack(coef, shift, pixels.reshape(SLOTS, N, N)).reshape(1, SLOTS, 1, ROWS, N)
+    data = lax.all_to_all(data, "patch", split_axis=1, concat_axis=0, tiled=True)
+    grad, field, slope, inverse, canvas, head, tail = objects(
+        intersection.reshape(1), chan_map, data.reshape(SLOTS, ROWS, N), pupil_mask, tabs
+    )
+    left = shifted(tail, "frame", True)
+    right = shifted(head, "frame", False)
     grad = gradient(chan_map, grad, field, slope, inverse, tabs)
+    middle, head, tail, grad = fold(canvas, left, right, grad)
+    upper = shifted(tail, "patch", True)
+    lower = shifted(head, "patch", False)
     grad = lax.all_to_all(
-        grad.reshape(SLOTS, 1, 1, COEF), "patch", split_axis=0, concat_axis=1, tiled=True
-    )
-    extended = padded(canvas, (("frame", 2), ("patch", 1)), MARGIN)
-    folded = fold_margins(fold_margins(extended, 1, MARGIN), 2, MARGIN)
-    blended = folded[:CHANNELS] / folded[CHANNELS][None]
-    return (blended, grad[..., :ZERN])
+        grad.reshape(SLOTS, 1, 1, ZERN), "patch", split_axis=0, concat_axis=1, tiled=True
+    )
+    blended = blend(middle, upper, lower)
+    return (blended, grad)
 
 
 def solution(mesh):

time: 83.8 us -> 73.4 us (0.88)
  blocking collectives: 24.9 us -> 12.6 us
  waiting for transfers between devices: 12.5 us -> 17.2 us
  Pallas kernels: 17.6 us -> 13.6 us
  starting transfers between devices: 21.4 us -> 25 us
  other arithmetic: 2.61 us -> 0 us
    all_to_all x2 -> x1, blocking collectives: 24.9 us -> 12.6 us  [per_device(): lax.all_to_all(grad.reshape(SLOTS, 1, 1, ZERN), 'patch', split_axis=0, co...]
    all_to_all x1, waiting for transfers between devices: 9.29 us -> 17.2 us  [per_device(): lax.all_to_all(data, 'patch', split_axis=1, concat_axis=0, tiled=True)]
    pallas_call x2 -> x4, Pallas kernels: 13.3 us -> 5.48 us  [the longest x1 3.62 us: gradient(): pl.pallas_call(gradient_kernel, out_shape=jax.ShapeDtypeStruct((SLOTS, ZE...]
    all_to_all x1, starting transfers between devices: 3.87 us -> 7.8 us  [per_device(): lax.all_to_all(data, 'patch', split_axis=1, concat_axis=0, tiled=True)]
    pallas_call x1, Pallas kernels: 4.35 us -> 8.09 us  [objects(): pl.pallas_call(object_kernel, out_shape=(jax.ShapeDtypeStruct((rows, 2 *...]
    ppermute x4, waiting for transfers between devices: 3.25 us -> 0.01 us  [the longest x2 0.01 us: shifted(): return lax.ppermute(cells, axis, [(i, i + 1) for i in range(ends)])]
    unnamed x7 -> x31, local copies, waits for them, and re-layouts: 1.4 us -> 3.15 us
    slice x2 -> x0, local copies, waits for them, and re-layouts: 1.22 us -> none  [the longest x1 1.13 us: padded(): lax.slice_in_dim(cells, cells.shape[dim] - width, cells.shape[dim], axis=...]
  transfers between devices with their start and end apart: 5 -> 5, of which waited for: 2 -> 1; matrix products, arithmetic and copies ran while one was open for 0% -> 0% of each run, Pallas kernels for 16% -> 5%
where the time goes in v2:
time: 73.4 us; the launch traced here: 73 us
  starting transfers between devices  25 us (34%)
  waiting for transfers between devices  17.2 us (23%)
  Pallas kernels  13.6 us (19%)
  blocking collectives  12.6 us (17%)
  local copies, waits for them, and re-layouts  3.15 us (4%)
  between operations  1.51 us (2%)
    all_to_all x1, waiting for transfers between devices, per_device(): lax.all_to_all(data, 'patch', split_axis=1, concat_axis=0, tiled=True)  17.2 us
    all_to_all x1, blocking collectives, per_device(): lax.all_to_all(grad.reshape(SLOTS, 1, 1, ZERN), 'patch', split_axis=0, co...  12.6 us
    ppermute x2, starting transfers between devices, shifted(): return lax.ppermute(cells, axis, [(i + 1, i) for i in range(ends)])  11.3 us
    pallas_call x1, Pallas kernels, objects(): pl.pallas_call(object_kernel, out_shape=(jax.ShapeDtypeStruct((rows, 2 *...  8.09 us
    all_to_all x1, starting transfers between devices, per_device(): lax.all_to_all(data, 'patch', split_axis=1, concat_axis=0, tiled=True)  7.8 us
    ppermute x2, starting transfers between devices, shifted(): return lax.ppermute(cells, axis, [(i, i + 1) for i in range(ends)])  5.92 us
    pallas_call x1, Pallas kernels, gradient(): pl.pallas_call(gradient_kernel, out_shape=jax.ShapeDtypeStruct((SLOTS, ZE...  3.62 us
    unnamed x31, local copies, waits for them, and re-layouts  3.15 us
  transfers between devices with their start and end apart: 5, of which 1 were waited for; matrix products, arithmetic and copies ran while one was open for 0% of the time, Pallas kernels for 5%

profile of v2, /device:TPU:7, one launch (start us, length us, event | category | flops | bytes accessed | tf_op | source)
XLA Modules:
  0.0 73.0 jit_solution(2818369708351377183)
XLA Ops:
  0.6 0.0 copy-start.1
  0.6 0.0 copy-start.2
  0.7 0.0 copy-start
  0.7 0.0 copy-start.3
  0.7 0.0 copy-start.4
  0.7 1.1 %copy-done.5 = bf16[1,16,1,128,128]{4,3,2,1,0:T(8,128)(2,1)S(1)} copy-done((bf16[1,16,1,128,128]{4,3,2,1,0:T(8,128)(2,1)S(1)}, bf16[1,16,1,128,128]{4,3,2,1,0:T(8,128)(2,1)}, u32[]{:S(2)}) %copy-start.5) | copy-done | bytes 524312
  1.8 0.7 copy-done.11
  2.5 0.7 copy-done.13
  3.2 0.0 copy-start.10
  3.2 0.0 copy-start.12
  3.2 0.0 copy-start.14
  3.2 1.0 %pack.1 = bf16[16,136,128]{2,1,0:T(8,128)(2,1)} custom-call(f32[16,36]{1,0:T(8,128)S(1)} %bitcast.19, s32[2,16]{1,0:T(2,128)S(1)} %bitcast.21, bf16[16,128,128]{2,1,0:T(8,128)(2,1)S(1)} %bitcast.18), custom_call_target="tpu_custom_call" | custom-call | tf_op jit(solution)/shard_map/pack/pallas_call | solution.py:405
  4.3 7.8 %all-to-all-start = ((bf16[1,16,1,136,128]{4,3,2,0,1:T(8,128)(2,1)}), bf16[1,16,1,136,128]{4,3,2,0,1:T(8,128)(2,1)S(1)}, u32[]{:S(2)}, u32[]{:S(2)}) async-start(bf16[1,16,1,136,128]{4,3,2,0,1:T(8,128)(2,1)} %bitcast.6), calls=%async_computation | async-start | bytes 1114112 | tf_op jit(solution)/shard_map/all_to_all | solution.py:604
  12.7 17.2 %all-to-all-done = bf16[1,16,1,136,128]{4,3,2,0,1:T(8,128)(2,1)S(1)} async-done(((bf16[1,16,1,136,128]{4,3,2,0,1:T(8,128)(2,1)}), bf16[1,16,1,136,128]{4,3,2,0,1:T(8,128)(2,1)S(1)}, u32[]{:S(2)}, u32[]{:S(2)}) %all-to-all-start) | async-done | bytes 557088 | tf_op jit(solution)/shard_map/all_to_all | solution.py:604
  29.9 0.0 copy-done.3
  29.9 0.0 copy-done.4
  29.9 0.0 copy-done.6
  30.0 0.0 copy-done.7
  30.0 8.1 %objects.1 = (f32[1152,256]{1,0:T(8,128)S(1)}, f32[8,256,256]{2,1,0:T(8,128)S(1)}, f32[1024,128]{1,0:T(8,128)S(1)}, f32[16,128]{1,0:T(8,128)S(1)}, f32[3,128,128...) custom-call(s32[1]{0:T(128)} %bitcast.16.width_ref, s32[16]{0:T(128)S(1)} %copy-done.12, ...), custom_call_target="tpu_custom_call" | custom-call | tf_op jit(solution)/shard_map/objects/pallas_call | solution.py:502
  38.1 4.0 %collective-permute-start = (f32[3,16,128]{2,1,0:T(8,128)S(1)}, f32[3,16,128]{2,1,0:T(8,128)S(1)}, u32[]{:S(2)}, u32[]{:S(2)}) collective-permute-start(f32[3,16,128]{2,1,0:T(8,128)S(1)} %get-tuple-element.14), channel_id=1, source_target_pairs={{0,16},{16,32},{32,48},{48,64},{64,80},{80,96},{96,112},{112,128},... | collective-permute-start | bytes 73736 | tf_op jit(solution)/shard_map/ppermute | solution.py:595
  42.1 8.9 %collective-permute-start.1 = (f32[3,16,128]{2,1,0:T(8,128)S(1)}, f32[3,16,128]{2,1,0:T(8,128)S(1)}, u32[]{:S(2)}, u32[]{:S(2)}) collective-permute-start(f32[3,16,128]{2,1,0:T(8,128)S(1)} %get-tuple-element.15), channel_id=1, source_target_pairs={{16,0},{32,16},{48,32},{64,48},{80,64},{96,80},{112,96},{128,112},... | collective-permute-start | bytes 73736 | tf_op jit(solution)/shard_map/ppermute | solution.py:596
  51.0 3.6 %gradient.1.grad_ref = f32[16,36]{1,0:T(8,128)S(1)} custom-call(s32[16]{0:T(128)S(1)} %copy-done.12, f32[1152,256]{1,0:T(8,128)S(1)} %get-tuple-element.16.grad_ref, f32[8,256,256]{2,1,0:T(8,128)S(1)} %get-tuple-element.17.field_ref, f32[1024,128]{1,0:T(8,128)S(1)} %get-tuple-element.18.slope_ref, f32[16,128]{1,0:T(8,128)S(1)} %get-tuple-element.19.inv_ref, ...), custom_call_target="tpu_custom_call" | custom-call | tf_op jit(solution)/shard_map/gradient/pallas_call | solution.py:544
  54.6 0.0 collective-permute-done.left_ref
  54.6 0.0 collective-permute-done.1.right_ref
  54.6 0.2 fold.1
  54.8 1.9 %collective-permute-start.2 = (f32[3,16,128]{2,1,0:T(8,128)S(1)}, f32[3,16,128]{2,1,0:T(8,128)S(1)}, u32[]{:S(2)}, u32[]{:S(2)}) collective-permute-start(f32[3,16,128]{2,1,0:T(8,128)S(1)} %get-tuple-element.21), channel_id=1, source_target_pairs={{0,1},{1,2},{2,3},{3,4},{4,5},{5,6},{6,7},{7,8},{8,9},{9,10},{10,1... | collective-permute-start | bytes 73736 | tf_op jit(solution)/shard_map/ppermute | solution.py:595
  56.8 2.4 %collective-permute-start.3 = (f32[3,16,128]{2,1,0:T(8,128)S(1)}, f32[3,16,128]{2,1,0:T(8,128)S(1)}, u32[]{:S(2)}, u32[]{:S(2)}) collective-permute-start(f32[3,16,128]{2,1,0:T(8,128)S(1)} %get-tuple-element.22), channel_id=1, source_target_pairs={{1,0},{2,1},{3,2},{4,3},{5,4},{6,5},{7,6},{8,7},{9,8},{10,9},{11,1... | collective-permute-start | bytes 73736 | tf_op jit(solution)/shard_map/ppermute | solution.py:596
  59.2 12.6 %all_to_all.21 = f32[16,1,1,36]{3,2,1,0:T(1,128)S(1)} all-to-all(f32[16,1,1,36]{3,2,1,0:T(1,128)S(1)} %bitcast.20), channel_id=1, replica_groups=mesh['frame'=32,'patch'=16] {'patch'}, dimensions={0} | all-to-all | bytes 4608 | tf_op jit(solution)/shard_map/all_to_all | solution.py:614
  71.8 0.0 collective-permute-done.2.upper_ref
  71.8 0.0 collective-permute-done.3.lower_ref
  71.8 0.7 blend.1
  72.4 0.6 copy.24
  (15 shorter events, 0.0 us)
Async XLA Ops:
  0.6 29.3 %copy-start.1 = (f32[40,1152]{1,0:T(8,128)S(1)}, f32[40,1152]{1,0:T(8,128)}, u32[]{:S(2)}) copy-start(f32[40,1152]{1,0:T(8,128)} %constant.29.clone.phase_ref) | copy-start | bytes 552964
  0.6 29.3 %copy-start.2 = (bf16[128,432]{1,0:T(8,128)(2,1)S(1)}, bf16[128,432]{1,0:T(8,128)(2,1)}, u32[]{:S(2)}) copy-start(bf16[128,432]{1,0:T(8,128)(2,1)} %constant.26.clone.lb_hbm.lb_ref) | copy-start | bytes 331780
  0.7 29.3 %copy-start = (bf16[2,256,256]{2,1,0:T(8,128)(2,1)S(1)}, bf16[2,256,256]{2,1,0:T(8,128)(2,1)}, u32[]{:S(2)}) copy-start(bf16[2,256,256]{2,1,0:T(8,128)(2,1)} %constant.24.clone.rb_hbm.rb_ref) | copy-start | bytes 786436
  0.7 29.3 %copy-start.3 = (bf16[2,256,128]{2,1,0:T(8,128)(2,1)S(1)}, bf16[2,256,128]{2,1,0:T(8,128)(2,1)}, u32[]{:S(2)}) copy-start(bf16[2,256,128]{2,1,0:T(8,128)(2,1)} %constant.21.clone.lp_hbm.lp_ref) | copy-start | bytes 393220
  0.7 29.3 %copy-start.4 = (bf16[2,128,256]{2,1,0:T(8,128)(2,1)S(1)}, bf16[2,128,256]{2,1,0:T(8,128)(2,1)}, u32[]{:S(2)}) copy-start(bf16[2,128,256]{2,1,0:T(8,128)(2,1)} %constant.20.clone.rp_hbm.rp_ref) | copy-start | bytes 393220
  0.7 1.1 %copy-start.5 = (bf16[1,16,1,128,128]{4,3,2,1,0:T(8,128)(2,1)S(1)}, bf16[1,16,1,128,128]{4,3,2,1,0:T(8,128)(2,1)}, u32[]{:S(2)}) copy-start(bf16[1,16,1,128,128]{4,3,2,1,0:T(8,128)(2,1)} %param.18) | copy-start | bytes 1572868
  1.8 0.7 copy-start.11
  2.5 0.7 copy-start.13
  3.2 26.8 %copy-start.6 = (bf16[2,256,256]{2,1,0:T(8,128)(2,1)S(1)}, bf16[2,256,256]{2,1,0:T(8,128)(2,1)}, u32[]{:S(2)}) copy-start(bf16[2,256,256]{2,1,0:T(8,128)(2,1)} %constant.23.clone.rf_hbm) | copy-start | bytes 786436
  3.2 26.8 %copy-start.7 = (bf16[144,256]{1,0:T(8,128)(2,1)S(1)}, bf16[144,256]{1,0:T(8,128)(2,1)}, u32[]{:S(2)}) copy-start(bf16[144,256]{1,0:T(8,128)(2,1)} %constant.25.clone.lt_ref) | copy-start | bytes 221188
  3.2 26.8 %copy-start.8 = (bf16[2,144,128]{2,1,0:T(8,128)(2,1)S(1)}, bf16[2,144,128]{2,1,0:T(8,128)(2,1)}, u32[]{:S(2)}) copy-start(bf16[2,144,128]{2,1,0:T(8,128)(2,1)} %constant.22.clone.lh_hbm) | copy-start | bytes 221188
  3.2 26.8 %copy-start.9 = (f32[72,128]{1,0:T(8,128)S(1)}, f32[72,128]{1,0:T(8,128)}, u32[]{:S(2)}) copy-start(f32[72,128]{1,0:T(8,128)} %constant.28.clone.weight_ref) | copy-start | bytes 110596
  3.2 26.8 %copy-start.10 = (s32[64,64]{1,0:T(8,128)S(1)}, s32[64,64]{1,0:T(8,128)}, u32[]{:S(2)}) copy-start(s32[64,64]{1,0:T(8,128)} %mask_ref.1) | copy-start | bytes 49156
  3.2 26.8 %copy-start.12 = (s32[16]{0:T(128)S(1)}, s32[16]{0:T(128)}, u32[]{:S(2)}) copy-start(s32[16]{0:T(128)} %chan_ref.3) | copy-start | bytes 196
  3.2 26.8 %copy-start.14 = (f32[1,256]{1,0:T(1,128)S(1)}, f32[1,256]{1,0:T(1,128)}, u32[]{:S(2)}) copy-start(f32[1,256]{1,0:T(1,128)} %constant.27.clone.taper_ref) | copy-start | bytes 3076
  4.3 25.7 %all-to-all-start = ((bf16[1,16,1,136,128]{4,3,2,0,1:T(8,128)(2,1)}), bf16[1,16,1,136,128]{4,3,2,0,1:T(8,128)(2,1)S(1)}, u32[]{:S(2)}, u32[]{:S(2)}) async-start(bf16[1,16,1,136,128]{4,3,2,0,1:T(8,128)(2,1)} %bitcast.6), calls=%async_computation | async-start | bytes 1114112 | tf_op jit(solution)/shard_map/all_to_all | solution.py:604
  38.1 16.5 %collective-permute-start = (f32[3,16,128]{2,1,0:T(8,128)S(1)}, f32[3,16,128]{2,1,0:T(8,128)S(1)}, u32[]{:S(2)}, u32[]{:S(2)}) collective-permute-start(f32[3,16,128]{2,1,0:T(8,128)S(1)} %get-tuple-element.14), channel_id=1, source_target_pairs={{0,16},{16,32},{32,48},{48,64},{64,80},{80,96},{96,112},{112,128},... | collective-permute-start | bytes 73736 | tf_op jit(solution)/shard_map/ppermute | solution.py:595
  42.1 12.5 %collective-permute-start.1 = (f32[3,16,128]{2,1,0:T(8,128)S(1)}, f32[3,16,128]{2,1,0:T(8,128)S(1)}, u32[]{:S(2)}, u32[]{:S(2)}) collective-permute-start(f32[3,16,128]{2,1,0:T(8,128)S(1)} %get-tuple-element.15), channel_id=1, source_target_pairs={{16,0},{32,16},{48,32},{64,48},{80,64},{96,80},{112,96},{128,112},... | collective-permute-start | bytes 73736 | tf_op jit(solution)/shard_map/ppermute | solution.py:596
  54.8 16.9 %collective-permute-start.2 = (f32[3,16,128]{2,1,0:T(8,128)S(1)}, f32[3,16,128]{2,1,0:T(8,128)S(1)}, u32[]{:S(2)}, u32[]{:S(2)}) collective-permute-start(f32[3,16,128]{2,1,0:T(8,128)S(1)} %get-tuple-element.21), channel_id=1, source_target_pairs={{0,1},{1,2},{2,3},{3,4},{4,5},{5,6},{6,7},{7,8},{8,9},{9,10},{10,1... | collective-permute-start | bytes 73736 | tf_op jit(solution)/shard_map/ppermute | solution.py:595
  56.8 15.0 %collective-permute-start.3 = (f32[3,16,128]{2,1,0:T(8,128)S(1)}, f32[3,16,128]{2,1,0:T(8,128)S(1)}, u32[]{:S(2)}, u32[]{:S(2)}) collective-permute-start(f32[3,16,128]{2,1,0:T(8,128)S(1)} %get-tuple-element.22), channel_id=1, source_target_pairs={{1,0},{2,1},{3,2},{4,3},{5,4},{6,5},{7,6},{8,7},{9,8},{10,9},{11,1... | collective-permute-start | bytes 73736 | tf_op jit(solution)/shard_map/ppermute | solution.py:596

commit v3 on v2

--- a/solution.py
+++ b/solution.py
@@ -31,6 +31,7 @@
 bf16 = jnp.bfloat16
 VM = pl.BlockSpec(memory_space=pltpu.VMEM)
 SM = pl.BlockSpec(memory_space=pltpu.SMEM)
+HB = pl.BlockSpec(memory_space=pltpu.HBM)
 
 
 def noll_order(noll_index):
@@ -383,9 +384,15 @@
     )
 
 
-def pack_kernel(coef_ref, shift_ref, pix_ref, out_ref, sem):
-    copy = pltpu.make_async_copy(pix_ref, out_ref.at[:, :N, :], sem)
-    copy.start()
+def pack_kernel(coef_hbm, shift_hbm, pix_hbm, out_ref, coef_ref, shift_ref, sems):
+    coef_copy = pltpu.make_async_copy(coef_hbm, coef_ref, sems.at[0])
+    shift_copy = pltpu.make_async_copy(shift_hbm, shift_ref, sems.at[1])
+    pix_copy = pltpu.make_async_copy(pix_hbm, out_ref.at[:, :N, :], sems.at[2])
+    coef_copy.start()
+    shift_copy.start()
+    pix_copy.start()
+    coef_copy.wait()
+    shift_copy.wait()
     coef = jnp.concatenate([coef_ref[...], jnp.zeros((SLOTS, N - ZERN), f32)], axis=1)
     first = coef.astype(bf16).astype(f32)
     rest = coef - first
@@ -398,26 +405,29 @@
     line = line + pltpu.roll(shift, 3 * ZERN, 1)
     for slot in range(SLOTS):
         out_ref[slot, N:, :] = jnp.broadcast_to(line[slot : slot + 1], (8, N)).astype(bf16)
-    copy.wait()
+    pix_copy.wait()
 
 
 def pack(coef, shift, pixels):
     return pl.pallas_call(
         pack_kernel,
         out_shape=jax.ShapeDtypeStruct((SLOTS, ROWS, N), bf16),
-        in_specs=[VM, VM, pl.BlockSpec(memory_space=pl.ANY)],
+        in_specs=[HB] * 3,
         out_specs=VM,
-        scratch_shapes=[pltpu.SemaphoreType.DMA],
+        scratch_shapes=[
+            pltpu.VMEM((SLOTS, ZERN), f32),
+            pltpu.VMEM((2, SLOTS), jnp.int32),
+            pltpu.SemaphoreType.DMA((3,)),
+        ],
         name="pack",
         compiler_params=limit(4),
-    )(coef, shift, pixels)
+    )(*[pltpu.with_memory_space_constraint(x, pltpu.HBM) for x in (coef, shift, pixels)])
 
 
 def fold_kernel(
-    canvas_ref, left_ref, right_ref, grad_ref,
-    middle_ref, head_ref, tail_ref, out_ref,
+    canvas_ref, left_ref, right_ref,
+    middle_ref, head_ref, tail_ref,
 ):
-    out_ref[...] = grad_ref[...]
     gap = jnp.zeros((TILE - 2 * MARGIN, N), f32)
     rest = jnp.zeros((N - TILE, N), f32)
     for layer in range(CHANNELS + 1):
@@ -510,7 +520,7 @@
             margin,
             margin,
         ),
-        in_specs=[SM, SM] + [VM] * 6 + [pl.BlockSpec(memory_space=pltpu.HBM)] * len(TABLES),
+        in_specs=[SM, SM] + [VM] * 6 + [HB] * len(TABLES),
         out_specs=(VM,) * 7,
         scratch_shapes=[pltpu.VMEM(table.shape, bf16) for table in fixed]
         + [
@@ -561,7 +571,7 @@
     )
 
 
-def fold(canvas, left, right, grad):
+def fold(canvas, left, right):
     margin = jax.ShapeDtypeStruct((CHANNELS + 1, MARGIN, N), f32)
     return pl.pallas_call(
         fold_kernel,
@@ -569,13 +579,12 @@
             jax.ShapeDtypeStruct((CHANNELS + 1, TILE, N), f32),
             margin,
             margin,
-            jax.ShapeDtypeStruct((SLOTS, ZERN), f32),
         ),
-        in_specs=[VM] * 4,
-        out_specs=(VM,) * 4,
+        in_specs=[VM] * 3,
+        out_specs=(VM,) * 3,
         name="fold",
         compiler_params=limit(8),
-    )(canvas, left, right, grad)
+    )(canvas, left, right)
 
 
 def blend(middle, upper, lower):
@@ -608,12 +617,12 @@
     left = shifted(tail, "frame", True)
     right = shifted(head, "frame", False)
     grad = gradient(chan_map, grad, field, slope, inverse, tabs)
-    middle, head, tail, grad = fold(canvas, left, right, grad)
+    grad = lax.all_to_all(
+        grad.reshape(SLOTS, 1, 1, ZERN), "patch", split_axis=0, concat_axis=1, tiled=True
+    )
+    middle, head, tail = fold(canvas, left, right)
     upper = shifted(tail, "patch", True)
     lower = shifted(head, "patch", False)
-    grad = lax.all_to_all(
-        grad.reshape(SLOTS, 1, 1, ZERN), "patch", split_axis=0, concat_axis=1, tiled=True
-    )
     blended = blend(middle, upper, lower)
     return (blended, grad)
 

time: 73.4 us -> 73.4 us (level)
  local copies, waits for them, and re-layouts: 3.15 us -> 0.67 us
  Pallas kernels: 13.6 us -> 14.6 us
  waiting for transfers between devices: 17.2 us -> 18.1 us
    unnamed x31 -> x25, local copies, waits for them, and re-layouts: 3.15 us -> 0.67 us
    pallas_call x1, Pallas kernels: 1.01 us -> 2.02 us  [pack(): pl.pallas_call(pack_kernel, out_shape=jax.ShapeDtypeStruct((SLOTS, ROWS,...]
    ppermute x2, waiting for transfers between devices: 0.01 us -> 0.92 us  [shifted(): return lax.ppermute(cells, axis, [(i + 1, i) for i in range(ends)])]
  transfers between devices with their start and end apart: 5 -> 5, of which waited for: 1 -> 2; matrix products, arithmetic and copies ran while one was open for 0% -> 0% of each run, Pallas kernels for 5% -> 5%
where the time goes in v3:
time: 73.4 us; the launch traced here: 73.1 us
  starting transfers between devices  25 us (34%)
  waiting for transfers between devices  18.1 us (25%)
  Pallas kernels  14.6 us (20%)
  blocking collectives  13.2 us (18%)
  between operations  1.52 us (2%)
    all_to_all x1, waiting for transfers between devices, per_device(): lax.all_to_all(data, 'patch', split_axis=1, concat_axis=0, tiled=True)  17.2 us
    all_to_all x1, blocking collectives, per_device(): lax.all_to_all(grad.reshape(SLOTS, 1, 1, ZERN), 'patch', split_axis=0, co...  13.2 us
    ppermute x2, starting transfers between devices, shifted(): return lax.ppermute(cells, axis, [(i + 1, i) for i in range(ends)])  11.3 us
    pallas_call x1, Pallas kernels, objects(): pl.pallas_call(object_kernel, out_shape=(jax.ShapeDtypeStruct((rows, 2 *...  8.1 us
    all_to_all x1, starting transfers between devices, per_device(): lax.all_to_all(data, 'patch', split_axis=1, concat_axis=0, tiled=True)  7.8 us
    ppermute x2, starting transfers between devices, shifted(): return lax.ppermute(cells, axis, [(i, i + 1) for i in range(ends)])  5.91 us
    pallas_call x1, Pallas kernels, gradient(): pl.pallas_call(gradient_kernel, out_shape=jax.ShapeDtypeStruct((SLOTS, ZE...  3.63 us
    pallas_call x1, Pallas kernels, pack(): pl.pallas_call(pack_kernel, out_shape=jax.ShapeDtypeStruct((SLOTS, ROWS,...  2.02 us
  transfers between devices with their start and end apart: 5, of which 2 were waited for; matrix products, arithmetic and copies ran while one was open for 0% of the time, Pallas kernels for 5%

profile of v3, /device:TPU:7, one launch (start us, length us, event | category | flops | bytes accessed | tf_op | source)
XLA Modules:
  0.0 73.1 jit_solution(4597699123973882089)
XLA Ops:
  0.6 0.0 copy-start.1
  0.6 0.0 copy-start.2
  0.7 0.0 copy-start
  0.7 0.0 copy-start.3
  0.7 0.0 copy-start.4
  0.7 0.0 copy-start.8
  0.7 0.0 copy-start.11
  0.7 0.0 copy-start.6
  0.7 0.0 copy-start.5
  0.7 0.0 copy-start.7
  0.8 2.0 %pack.1 = bf16[16,136,128]{2,1,0:T(8,128)(2,1)} custom-call(f32[16,36]{1,0:T(8,128)} %bitcast.21, s32[2,16]{1,0:T(2,128)} %bitcast.22, bf16[16,128,128]{2,1,0:T(8,128)(2,1)} %bitcast.19), custom_call_target="tpu_custom_call" | custom-call | tf_op jit(solution)/shard_map/pack/pallas_call | solution.py:412
  2.8 7.8 %all-to-all-start = ((bf16[1,16,1,136,128]{4,3,2,0,1:T(8,128)(2,1)}), bf16[1,16,1,136,128]{4,3,2,0,1:T(8,128)(2,1)S(1)}, u32[]{:S(2)}, u32[]{:S(2)}) async-start(bf16[1,16,1,136,128]{4,3,2,0,1:T(8,128)(2,1)} %bitcast.6), calls=%async_computation | async-start | bytes 1114112 | tf_op jit(solution)/shard_map/all_to_all | solution.py:613
  11.3 17.2 %all-to-all-done = bf16[1,16,1,136,128]{4,3,2,0,1:T(8,128)(2,1)S(1)} async-done(((bf16[1,16,1,136,128]{4,3,2,0,1:T(8,128)(2,1)}), bf16[1,16,1,136,128]{4,3,2,0,1:T(8,128)(2,1)S(1)}, u32[]{:S(2)}, u32[]{:S(2)}) %all-to-all-start) | async-done | bytes 557088 | tf_op jit(solution)/shard_map/all_to_all | solution.py:613
  28.5 0.0 copy-done.3
  28.5 0.0 copy-done.4
  28.5 0.0 copy-done.8
  28.5 0.0 copy-done.11
  28.5 0.0 copy-done.6
  28.6 8.1 %objects.1 = (f32[1152,256]{1,0:T(8,128)S(1)}, f32[8,256,256]{2,1,0:T(8,128)S(1)}, f32[1024,128]{1,0:T(8,128)S(1)}, f32[16,128]{1,0:T(8,128)S(1)}, f32[3,128,128...) custom-call(s32[1]{0:T(128)} %bitcast.16.width_ref, s32[16]{0:T(128)S(1)} %copy-done.10, ...), custom_call_target="tpu_custom_call" | custom-call | tf_op jit(solution)/shard_map/objects/pallas_call | solution.py:512
  36.7 4.0 %collective-permute-start = (f32[3,16,128]{2,1,0:T(8,128)S(1)}, f32[3,16,128]{2,1,0:T(8,128)S(1)}, u32[]{:S(2)}, u32[]{:S(2)}) collective-permute-start(f32[3,16,128]{2,1,0:T(8,128)S(1)} %get-tuple-element.13), channel_id=1, source_target_pairs={{0,16},{16,32},{32,48},{48,64},{64,80},{80,96},{96,112},{112,128},... | collective-permute-start | bytes 73736 | tf_op jit(solution)/shard_map/ppermute | solution.py:604
  40.7 8.8 %collective-permute-start.1 = (f32[3,16,128]{2,1,0:T(8,128)S(1)}, f32[3,16,128]{2,1,0:T(8,128)S(1)}, u32[]{:S(2)}, u32[]{:S(2)}) collective-permute-start(f32[3,16,128]{2,1,0:T(8,128)S(1)} %get-tuple-element.14), channel_id=1, source_target_pairs={{16,0},{32,16},{48,32},{64,48},{80,64},{96,80},{112,96},{128,112},... | collective-permute-start | bytes 73736 | tf_op jit(solution)/shard_map/ppermute | solution.py:605
  49.5 0.0 collective-permute-done.left_ref
  49.5 0.9 %collective-permute-done.1.right_ref = f32[3,16,128]{2,1,0:T(8,128)S(1)} collective-permute-done((f32[3,16,128]{2,1,0:T(8,128)S(1)}, f32[3,16,128]{2,1,0:T(8,128)S(1)}, u32[]{:S(2)}, u32[]{:S(2)}) %collective-permute-start.1) | collective-permute-done | bytes 24608 | tf_op jit(solution)/shard_map/ppermute | solution.py:605
  50.4 0.2 fold.1
  50.6 1.9 %collective-permute-start.2 = (f32[3,16,128]{2,1,0:T(8,128)S(1)}, f32[3,16,128]{2,1,0:T(8,128)S(1)}, u32[]{:S(2)}, u32[]{:S(2)}) collective-permute-start(f32[3,16,128]{2,1,0:T(8,128)S(1)} %get-tuple-element.16), channel_id=1, source_target_pairs={{0,1},{1,2},{2,3},{3,4},{4,5},{5,6},{6,7},{7,8},{8,9},{9,10},{10,1... | collective-permute-start | bytes 73736 | tf_op jit(solution)/shard_map/ppermute | solution.py:604
  52.6 2.4 %collective-permute-start.3 = (f32[3,16,128]{2,1,0:T(8,128)S(1)}, f32[3,16,128]{2,1,0:T(8,128)S(1)}, u32[]{:S(2)}, u32[]{:S(2)}) collective-permute-start(f32[3,16,128]{2,1,0:T(8,128)S(1)} %get-tuple-element.17), channel_id=1, source_target_pairs={{1,0},{2,1},{3,2},{4,3},{5,4},{6,5},{7,6},{8,7},{9,8},{10,9},{11,1... | collective-permute-start | bytes 73736 | tf_op jit(solution)/shard_map/ppermute | solution.py:605
  55.0 3.6 %gradient.1 = f32[16,36]{1,0:T(8,128)S(1)} custom-call(s32[16]{0:T(128)S(1)} %copy-done.10, f32[1152,256]{1,0:T(8,128)S(1)} %get-tuple-element.18.grad_ref, f32[8,256,256]{2,1,0:T(8,128)S(1)} %get-tuple-element.19.field_ref, f32[1024,128]{1,0:T(8,128)S(1)} %get-tuple-element.20.slope_ref, f32[16,128]{1,0:T(8,128)S(1)} %get-tuple-element.21.inv_ref, ...), custom_call_target="tpu_custom_call" | custom-call | tf_op jit(solution)/shard_map/gradient/pallas_call | solution.py:554
  58.6 13.2 %all_to_all.21 = f32[16,1,1,36]{3,2,1,0:T(1,128)S(1)} all-to-all(f32[16,1,1,36]{3,2,1,0:T(1,128)S(1)} %bitcast.18), channel_id=1, replica_groups=mesh['frame'=32,'patch'=16] {'patch'}, dimensions={0} | all-to-all | bytes 4608 | tf_op jit(solution)/shard_map/all_to_all | solution.py:620
  71.8 0.0 collective-permute-done.2.upper_ref
  71.8 0.0 collective-permute-done.3.lower_ref
  71.8 0.7 blend.1
  72.5 0.6 copy.24
  (9 shorter events, 0.0 us)
Async XLA Ops:
  0.6 27.8 %copy-start.1 = (f32[40,1152]{1,0:T(8,128)S(1)}, f32[40,1152]{1,0:T(8,128)}, u32[]{:S(2)}) copy-start(f32[40,1152]{1,0:T(8,128)} %constant.29.clone.phase_ref) | copy-start | bytes 552964
  0.6 27.8 %copy-start.2 = (bf16[128,432]{1,0:T(8,128)(2,1)S(1)}, bf16[128,432]{1,0:T(8,128)(2,1)}, u32[]{:S(2)}) copy-start(bf16[128,432]{1,0:T(8,128)(2,1)} %constant.26.clone.lb_hbm.lb_ref) | copy-start | bytes 331780
  0.7 27.8 %copy-start = (bf16[2,256,256]{2,1,0:T(8,128)(2,1)S(1)}, bf16[2,256,256]{2,1,0:T(8,128)(2,1)}, u32[]{:S(2)}) copy-start(bf16[2,256,256]{2,1,0:T(8,128)(2,1)} %constant.24.clone.rb_hbm.rb_ref) | copy-start | bytes 786436
  0.7 27.8 %copy-start.3 = (bf16[2,256,128]{2,1,0:T(8,128)(2,1)S(1)}, bf16[2,256,128]{2,1,0:T(8,128)(2,1)}, u32[]{:S(2)}) copy-start(bf16[2,256,128]{2,1,0:T(8,128)(2,1)} %constant.21.clone.lp_hbm.lp_ref) | copy-start | bytes 393220
  0.7 27.8 %copy-start.4 = (bf16[2,128,256]{2,1,0:T(8,128)(2,1)S(1)}, bf16[2,128,256]{2,1,0:T(8,128)(2,1)}, u32[]{:S(2)}) copy-start(bf16[2,128,256]{2,1,0:T(8,128)(2,1)} %constant.20.clone.rp_hbm.rp_ref) | copy-start | bytes 393220
  0.7 27.8 %copy-start.8 = (f32[72,128]{1,0:T(8,128)S(1)}, f32[72,128]{1,0:T(8,128)}, u32[]{:S(2)}) copy-start(f32[72,128]{1,0:T(8,128)} %constant.28.clone.weight_ref) | copy-start | bytes 110596
  0.7 27.8 %copy-start.11 = (f32[1,256]{1,0:T(1,128)S(1)}, f32[1,256]{1,0:T(1,128)}, u32[]{:S(2)}) copy-start(f32[1,256]{1,0:T(1,128)} %constant.27.clone.taper_ref) | copy-start | bytes 3076
  0.7 27.8 %copy-start.6 = (bf16[144,256]{1,0:T(8,128)(2,1)S(1)}, bf16[144,256]{1,0:T(8,128)(2,1)}, u32[]{:S(2)}) copy-start(bf16[144,256]{1,0:T(8,128)(2,1)} %constant.25.clone.lt_ref) | copy-start | bytes 221188
  0.7 27.8 %copy-start.5 = (bf16[2,256,256]{2,1,0:T(8,128)(2,1)S(1)}, bf16[2,256,256]{2,1,0:T(8,128)(2,1)}, u32[]{:S(2)}) copy-start(bf16[2,256,256]{2,1,0:T(8,128)(2,1)} %constant.23.clone.rf_hbm) | copy-start | bytes 786436
  0.7 27.8 %copy-start.7 = (bf16[2,144,128]{2,1,0:T(8,128)(2,1)S(1)}, bf16[2,144,128]{2,1,0:T(8,128)(2,1)}, u32[]{:S(2)}) copy-start(bf16[2,144,128]{2,1,0:T(8,128)(2,1)} %constant.22.clone.lh_hbm) | copy-start | bytes 221188
  0.8 27.8 %copy-start.10 = (s32[16]{0:T(128)S(1)}, s32[16]{0:T(128)}, u32[]{:S(2)}) copy-start(s32[16]{0:T(128)} %chan_ref.3) | copy-start | bytes 196
  0.8 27.8 %copy-start.9 = (s32[64,64]{1,0:T(8,128)S(1)}, s32[64,64]{1,0:T(8,128)}, u32[]{:S(2)}) copy-start(s32[64,64]{1,0:T(8,128)} %mask_ref.1) | copy-start | bytes 49156
  2.8 25.7 %all-to-all-start = ((bf16[1,16,1,136,128]{4,3,2,0,1:T(8,128)(2,1)}), bf16[1,16,1,136,128]{4,3,2,0,1:T(8,128)(2,1)S(1)}, u32[]{:S(2)}, u32[]{:S(2)}) async-start(bf16[1,16,1,136,128]{4,3,2,0,1:T(8,128)(2,1)} %bitcast.6), calls=%async_computation | async-start | bytes 1114112 | tf_op jit(solution)/shard_map/all_to_all | solution.py:613
  36.7 12.9 %collective-permute-start = (f32[3,16,128]{2,1,0:T(8,128)S(1)}, f32[3,16,128]{2,1,0:T(8,128)S(1)}, u32[]{:S(2)}, u32[]{:S(2)}) collective-permute-start(f32[3,16,128]{2,1,0:T(8,128)S(1)} %get-tuple-element.13), channel_id=1, source_target_pairs={{0,16},{16,32},{32,48},{48,64},{64,80},{80,96},{96,112},{112,128},... | collective-permute-start | bytes 73736 | tf_op jit(solution)/shard_map/ppermute | solution.py:604
  40.7 9.8 %collective-permute-start.1 = (f32[3,16,128]{2,1,0:T(8,128)S(1)}, f32[3,16,128]{2,1,0:T(8,128)S(1)}, u32[]{:S(2)}, u32[]{:S(2)}) collective-permute-start(f32[3,16,128]{2,1,0:T(8,128)S(1)} %get-tuple-element.14), channel_id=1, source_target_pairs={{16,0},{32,16},{48,32},{64,48},{80,64},{96,80},{112,96},{128,112},... | collective-permute-start | bytes 73736 | tf_op jit(solution)/shard_map/ppermute | solution.py:605
  50.6 21.1 %collective-permute-start.2 = (f32[3,16,128]{2,1,0:T(8,128)S(1)}, f32[3,16,128]{2,1,0:T(8,128)S(1)}, u32[]{:S(2)}, u32[]{:S(2)}) collective-permute-start(f32[3,16,128]{2,1,0:T(8,128)S(1)} %get-tuple-element.16), channel_id=1, source_target_pairs={{0,1},{1,2},{2,3},{3,4},{4,5},{5,6},{6,7},{7,8},{8,9},{9,10},{10,1... | collective-permute-start | bytes 73736 | tf_op jit(solution)/shard_map/ppermute | solution.py:604
  52.6 19.2 %collective-permute-start.3 = (f32[3,16,128]{2,1,0:T(8,128)S(1)}, f32[3,16,128]{2,1,0:T(8,128)S(1)}, u32[]{:S(2)}, u32[]{:S(2)}) collective-permute-start(f32[3,16,128]{2,1,0:T(8,128)S(1)} %get-tuple-element.17), channel_id=1, source_target_pairs={{1,0},{2,1},{3,2},{4,3},{5,4},{6,5},{7,6},{8,7},{9,8},{10,9},{11,1... | collective-permute-start | bytes 73736 | tf_op jit(solution)/shard_map/ppermute | solution.py:605

commit v4 on v3

--- a/solution.py
+++ b/solution.py
@@ -23,6 +23,8 @@
 HALF = 72
 TWO = 2 * HALF
 DEG = 9
+DEG_ROWS = 16
+BLOCKS = HALF // 8
 COEF = 40
 ROWS = N + 8
 regular_gamma = 0.1
@@ -105,7 +107,7 @@
     high, low = halves(np.concatenate([weight[None] * ch.T, -weight[None] * sh.T], axis=1))
     out["left_back"] = np.concatenate([high, high, low], axis=1)
     out["taper"] = np.tile(taper, 2)[None].astype(np.float32)
-    out["weight"] = np.broadcast_to(weight[:, None], (HALF, N)).astype(np.float32)
+    out["weight"] = np.broadcast_to(weight[:, None] / 2.0, (HALF, N)).astype(np.float32)
     position, modes = zernike_modes()
     cheb = np.polynomial.chebyshev.chebvander(position, DEG - 1)
     fit = np.linalg.lstsq(cheb, modes.transpose(1, 0, 2).reshape(PUP, -1), rcond=None)[0]
@@ -116,7 +118,11 @@
     phase[ZERN, 1] = step
     phase[ZERN + 1, 0] = step * position
     phase = np.concatenate([phase, phase], axis=2)
-    out["phase"] = phase.reshape(COEF, DEG * N).astype(np.float32)
+    out["phase"] = (phase / (2.0 * np.pi)).reshape(COEF, DEG * N).astype(np.float32)
+    spread = np.zeros((DEG_ROWS, PUP))
+    spread[:DEG] = cheb.T
+    high, low = halves(spread)
+    out["sums"] = np.concatenate([high, high, low], axis=1)
     return out, cheb
 
 
@@ -148,35 +154,49 @@
     return jnp.concatenate([top, low], axis=0)
 
 
-def chebyshev_sums(parts, cheb, row):
-    even = parts[0]
-    for i in range(2, DEG, 2):
-        even = even + float(cheb[row, i]) * parts[i]
-    odd = float(cheb[row, 1]) * parts[1]
-    for i in range(3, DEG, 2):
-        odd = odd + float(cheb[row, i]) * parts[i]
-    return even, odd
-
-
-def turn(phase, lane_turns):
-    count = jnp.floor(phase * (2.0 / math.pi) + 0.5)
-    rest = phase - count * 1.5703125
-    rest = rest - count * 4.837512969970703125e-4
-    rest = rest - count * 7.549789954891882e-8
-    quarter = count.astype(jnp.int32) + lane_turns
-    sq = rest * rest
-    sine = rest + rest * sq * (
-        -1.6666654611e-1 + sq * (8.3321608736e-3 + sq * -1.9515295891e-4)
-    )
-    cosine = (1.0 - 0.5 * sq) + sq * sq * (
-        4.166664568298827e-2 + sq * (-1.388731625493765e-3 + sq * 2.443315711809948e-5)
-    )
-    odd = (quarter & 1) == 1
-    value = jnp.where(odd, sine, cosine)
-    value = jnp.where(((quarter + 1) & 2) == 2, -value, value)
-    slope = jnp.where(odd, cosine, sine)
-    slope = jnp.where((quarter & 2) == 2, slope, -slope)
-    return value, slope
+SINE = (3.141592616, -5.167708583, 2.55005456, -0.5981644139, 0.07742681132)
+COSINE = (0.9999999532, -4.934792831, 4.058411353, -1.331876568, 0.2196896111)
+
+
+def blocked(y):
+    pieces = []
+    for block in range(BLOCKS):
+        rows = slice(block * 8, block * 8 + 8)
+        im_rows = slice(HALF + block * 8, HALF + block * 8 + 8)
+        for which in range(2):
+            lanes = slice(which * N, (which + 1) * N)
+            pieces.append(jnp.concatenate([y[rows, lanes], y[im_rows, lanes]], axis=1))
+    return jnp.concatenate(pieces, axis=0)
+
+
+def store_blocked(y, pair, base, yh_ref, yl_ref):
+    high, low = split(blocked(y))
+    rows = slice(base + pair * 16, base + pair * 16 + 16)
+    for block in range(BLOCKS):
+        yh_ref[block, rows, :] = high[block * 16 : block * 16 + 16]
+        yl_ref[block, rows, :] = low[block * 16 : block * 16 + 16]
+
+
+def chebyshev_sum(parts, cheb, row):
+    total = parts[0]
+    for i in range(1, DEG):
+        total = total + float(cheb[row, i]) * parts[i]
+    return total
+
+
+def series(factors, square):
+    total = factors[-1] * square + factors[-2]
+    for factor in factors[-3::-1]:
+        total = total * square + factor
+    return total
+
+
+def turned(turns):
+    rest = turns - jnp.round(turns)
+    square = rest * rest
+    sine = rest * series(SINE, square)
+    twice = sine + sine
+    return 1.0 - twice * sine, twice * series(COSINE, square)
 
 
 def slot_scales(chan_ref, width):
@@ -188,9 +208,9 @@
 
 
 def transfer_part(
-    data_ref, chan_ref, mask_ref, phase_ref, rp_ref, lp_ref, lh_ref, rf_ref, ready,
-    otf_ref, field_ref, slope_ref, inv_ref,
-    line_ref, wide_ref, ph_ref, pl_ref, half_re_ref, half_im_ref, yh_ref, yl_ref,
+    data_ref, chan_ref, mask_ref, phase_ref, rp_ref, lp_ref, lh_ref, ready, spectra,
+    field_ref, slope_ref,
+    line_ref, wide_ref, ph_ref, pl_ref, half_re_ref, half_im_ref, power_ref, yh_ref, yl_ref,
 ):
     cheb = tables()[1]
     for slot in range(SLOTS):
@@ -206,123 +226,112 @@
         coef, phase_ref[...], (((1,), (0,)), ((), ())),
         precision=lax.Precision.HIGHEST, preferred_element_type=f32,
     )
+    first = lax.broadcasted_iota(jnp.int32, (SLOTS, N), 1) < PUP
+    sign = jnp.where(first, 1.0, -1.0)
     parts = [parts_all[:, i * N : (i + 1) * N] for i in range(DEG)]
-    lane_turns = jnp.where(lax.broadcasted_iota(jnp.int32, (SLOTS, N), 1) < PUP, 0, 3)
+    parts = [part * sign if i % 2 else part for i, part in enumerate(parts)]
     for row in range(PUP // 2):
-        even, odd = chebyshev_sums(parts, cheb, row)
-        for at, phase in ((row, even + odd), (PUP - 1 - row, even - odd)):
-            value, slope = turn(phase, lane_turns)
-            mask = wide_ref[at : at + 1, :]
-            value = value * mask
-            here = slice(at * SLOTS, (at + 1) * SLOTS)
-            slope_ref[here, :] = slope * mask
-            high, low = split(value)
-            ph_ref[here, :] = high
-            pl_ref[here, :] = low
+        if row % 4 == 0:
+            spectra(row // 4)
+        far = PUP - 1 - row
+        cosine, sine = turned(chebyshev_sum(parts, cheb, row))
+        mask = jnp.where(first, wide_ref[row : row + 1, :], wide_ref[far : far + 1, :])
+        cosine = cosine * mask
+        sine = sine * mask
+        far_cosine = pltpu.roll(cosine, PUP, 1)
+        far_sine = pltpu.roll(sine, PUP, 1)
+        here = slice(row * SLOTS, (row + 1) * SLOTS)
+        there = slice(far * SLOTS, (far + 1) * SLOTS)
+        slope_ref[here, :] = jnp.where(first, -sine, far_cosine)
+        slope_ref[there, :] = jnp.where(first, -far_sine, cosine)
+        high, low = split(jnp.where(first, cosine, far_sine))
+        ph_ref[here, :] = high
+        pl_ref[here, :] = low
+        high, low = split(jnp.where(first, far_cosine, sine))
+        ph_ref[there, :] = high
+        pl_ref[there, :] = low
     ready()
     right = table_rows(rp_ref)
-    for chunk in range(4):
-        here = slice(chunk * 256, (chunk + 1) * 256)
+    for chunk in range(2):
+        here = slice(chunk * 512, (chunk + 1) * 512)
         high = ph_ref[here, :]
         half = dot(jnp.concatenate([high, pl_ref[here, :], high], axis=1), right)
         half_re_ref[here, :] = half[:, :N]
         half_im_ref[here, :] = half[:, N:]
     left = table_lanes(lp_ref)
-    left_h = table_lanes(lh_ref)
     for pair in range(PAIRS):
         columns = []
         for part_ref in (half_re_ref, half_im_ref):
             columns.append(
                 jnp.concatenate(
-                    [
-                        part_ref[pl.ds(2 * pair + which, PUP, stride=SLOTS), :]
-                        for which in range(2)
-                    ],
+                    [part_ref[pl.ds(2 * pair + which, PUP, stride=SLOTS), :] for which in range(2)],
                     axis=1,
                 )
             )
         field = dot(left, rows3(jnp.concatenate(columns, axis=0)))
         field_ref[pair] = field
-        power = field[:N] * field[:N] + field[N:] * field[N:]
-        y = dot(left_h, rows3(power))
-        high, low = split(swap_halves(y, HALF))
-        here = slice(pair * TWO, (pair + 1) * TWO)
-        yh_ref[here, :] = high
-        yl_ref[here, :] = low
+        high, low = split(field[:N] * field[:N] + field[N:] * field[N:])
+        power_ref[pair, :N] = high
+        power_ref[pair, N:] = low
+    left = table_lanes(lh_ref)
+    for pair in range(PAIRS):
+        high = power_ref[pair, :N]
+        y = dot(left, jnp.concatenate([high, power_ref[pair, N:], high], axis=0))
+        store_blocked(y, pair, 0, yh_ref, yl_ref)
+
+
+def object_part(
+    width_ref, slots, weight_ref, rf_ref, rb_ref, lb_ref,
+    grad_ref, inv_ref, canvas_ref, head_ref, tail_ref,
+    yh_ref, yl_ref, plane_ref, object_ref, inner_ref,
+):
     right = table_rows(rf_ref)
-    for pair in range(PAIRS):
-        here = slice(pair * TWO, (pair + 1) * TWO)
-        high = yh_ref[here, :]
-        out = dot(jnp.concatenate([high, yl_ref[here, :], high], axis=1), right)
-        for which in range(2):
-            slot = 2 * pair + which
-            block = out[which * HALF : (which + 1) * HALF]
-            inverse = 1.0 / block[0:1, 0:1]
-            otf_ref[slot * HALF : (slot + 1) * HALF, :] = block * inverse
-            inv_ref[slot : slot + 1, :] = jnp.broadcast_to(inverse, (1, N))
-
-
-def object_part(
-    width_ref, chan_ref, pix_ref, otf_ref, lt_ref, taper_ref, weight_ref, rf_ref, rb_ref, lb_ref,
-    grad_ref, canvas_ref, head_ref, tail_ref,
-    order_ref, yh_ref, yl_ref, spec_ref, object_ref,
-):
-    at = [jnp.int32(0), jnp.int32(PER)]
-    for slot in range(SLOTS):
-        first = chan_ref[slot] == 0
-        order_ref[jnp.where(first, at[0], at[1])] = slot
-        at = [jnp.where(first, at[0] + 1, at[0]), jnp.where(first, at[1], at[1] + 1)]
-    left = lt_ref[...]
-    taper = taper_ref[...]
-    for pair in range(PAIRS):
-        image = jnp.concatenate([pix_ref[2 * pair, :N, :], pix_ref[2 * pair + 1, :N, :]], axis=1)
-        y = dot(left, jnp.concatenate([image, image], axis=0)) * taper
-        high, low = split(swap_halves(y, HALF))
-        here = slice(pair * TWO, (pair + 1) * TWO)
-        yh_ref[here, :] = high
-        yl_ref[here, :] = low
-    right = table_rows(rf_ref)
-    for pair in range(PAIRS):
-        here = slice(pair * TWO, (pair + 1) * TWO)
-        high = yh_ref[here, :]
-        spec_ref[here, :] = dot(jnp.concatenate([high, yl_ref[here, :], high], axis=1), right)
-    for channel in range(CHANNELS):
-        slots = [order_ref[channel * PER + i] for i in range(PER)]
-        inner = [jnp.zeros((8, N), f32) for _ in range(PER)]
-        for block in range(HALF // 8):
-            where = [pl.ds(pl.multiple_of(slot * HALF + block * 8, 8), 8) for slot in slots]
-            h_re = [otf_ref[w, :N] for w in where]
-            h_im = [otf_ref[w, N:] for w in where]
-            s_re = [spec_ref[w, :N] for w in where]
-            s_im = [spec_ref[w, N:] for w in where]
+    for block in range(BLOCKS):
+        high = yh_ref[block]
+        plane_ref[block] = dot(jnp.concatenate([high, yl_ref[block], high], axis=1), right)
+        if block == 0:
+            for slot in range(SLOTS):
+                inverse = 1.0 / plane_ref[0, slot * 8 : slot * 8 + 1, 0:1]
+                inv_ref[slot * 8 : slot * 8 + 8, :] = jnp.broadcast_to(inverse, (8, N))
+        for channel in range(CHANNELS):
+            mine = slots[channel * PER : (channel + 1) * PER]
+            where = [pl.ds(pl.multiple_of(slot * 8, 8), 8) for slot in mine]
+            there = [pl.ds(pl.multiple_of(SLOTS * 8 + slot * 8, 8), 8) for slot in mine]
+            inverse = [inv_ref[w, :] for w in where]
+            h_re = [plane_ref[block, where[i], :N] * inverse[i] for i in range(PER)]
+            h_im = [plane_ref[block, where[i], N:] * inverse[i] for i in range(PER)]
+            s_re = [plane_ref[block, w, :N] for w in there]
+            s_im = [plane_ref[block, w, N:] for w in there]
             num_re = num_im = 0.0
             den = regular_gamma
             for i in range(PER):
                 num_re = num_re + (h_re[i] * s_re[i] + h_im[i] * s_im[i])
                 num_im = num_im + (h_re[i] * s_im[i] - h_im[i] * s_re[i])
                 den = den + (h_re[i] * h_re[i] + h_im[i] * h_im[i])
-            inverse = 1.0 / den
-            o_re = num_re * inverse
-            o_im = num_im * inverse
+            recip = 1.0 / den
+            o_re = num_re * recip
+            o_im = num_im * recip
             rows = slice(channel * HALF + block * 8, channel * HALF + block * 8 + 8)
             object_ref[rows, :N] = o_re
             object_ref[rows, N:] = o_im
-            weight = weight_ref[block * 8 : block * 8 + 8, :]
+            scale = o_re * o_re + o_im * o_im
             for i in range(PER):
-                r_re = s_re[i] - (o_re * h_re[i] - o_im * h_im[i])
-                r_im = s_im[i] - (o_re * h_im[i] + o_im * h_re[i])
-                g_re = -(r_re * o_re + r_im * o_im)
-                g_im = r_re * o_im - r_im * o_re
-                inner[i] = inner[i] + weight * (g_re * h_re[i] + g_im * h_im[i])
-                grad_ref[where[i], :N] = g_re
-                grad_ref[where[i], N:] = g_im
-        origin = (lax.broadcasted_iota(jnp.int32, (8, N), 0) == 0) & (
-            lax.broadcasted_iota(jnp.int32, (8, N), 1) == 0
-        )
-        for i in range(PER):
-            total = jnp.sum(jnp.sum(inner[i], axis=0, keepdims=True), axis=1, keepdims=True)
-            w = pl.ds(pl.multiple_of(slots[i] * HALF, 8), 8)
-            grad_ref[w, :N] = grad_ref[w, :N] - jnp.where(origin, total, 0.0)
+                g_re = scale * h_re[i] - (s_re[i] * o_re + s_im[i] * o_im)
+                g_im = scale * h_im[i] - (s_im[i] * o_re - s_re[i] * o_im)
+                match = g_re * h_re[i] + g_im * h_im[i]
+                if block in (0, BLOCKS - 1):
+                    match = match * weight_ref[block * 8 : block * 8 + 8, :]
+                at = channel * PER + i
+                inner_ref[at] = match if block == 0 else inner_ref[at] + match
+                grad_ref[block, where[i], :N] = g_re
+                grad_ref[block, where[i], N:] = g_im
+    origin = (lax.broadcasted_iota(jnp.int32, (8, N), 0) == 0) & (
+        lax.broadcasted_iota(jnp.int32, (8, N), 1) == 0
+    )
+    for at in range(SLOTS):
+        total = jnp.sum(jnp.sum(inner_ref[at], axis=0, keepdims=True), axis=1, keepdims=True)
+        w = pl.ds(pl.multiple_of(slots[at] * 8, 8), 8)
+        grad_ref[0, w, :N] = grad_ref[0, w, :N] - jnp.where(origin, 2.0 * total, 0.0)
     high, low = split(object_ref[...] * (1.0 / (N * N)))
     z = dot(jnp.concatenate([high, low, high], axis=1), table_rows(rb_ref))
     image = dot(lb_ref[...], rows3(swap_halves(z, HALF)))
@@ -354,8 +363,8 @@
     rp_hbm, lp_hbm, lh_hbm, rf_hbm, rb_hbm, lb_hbm,
     grad_ref, field_ref, slope_ref, inv_ref, canvas_ref, head_ref, tail_ref,
     rp_ref, lp_ref, lh_ref, rf_ref, rb_ref, lb_ref, sems,
-    otf_ref, line_ref, wide_ref, ph_ref, pl_ref, half_re_ref, half_im_ref, yh_ref, yl_ref,
-    order_ref, sh_ref, sl_ref, spec_ref, object_ref,
+    line_ref, wide_ref, ph_ref, pl_ref, half_re_ref, half_im_ref, power_ref, yh_ref, yl_ref,
+    order_ref, plane_ref, object_ref, inner_ref,
 ):
     moves = (
         (rp_hbm, rp_ref), (lp_hbm, lp_ref), (lh_hbm, lh_ref),
@@ -372,15 +381,28 @@
         for copy in copies:
             copy.wait()
 
+    at = [jnp.int32(0), jnp.int32(PER)]
+    for slot in range(SLOTS):
+        first = chan_ref[slot] == 0
+        order_ref[jnp.where(first, at[0], at[1])] = slot
+        at = [jnp.where(first, at[0] + 1, at[0]), jnp.where(first, at[1], at[1] + 1)]
+    left = lt_ref[...]
+    taper = taper_ref[...]
+
+    def spectra(pair):
+        image = jnp.concatenate([data_ref[2 * pair, :N, :], data_ref[2 * pair + 1, :N, :]], axis=1)
+        y = dot(left, jnp.concatenate([image, image], axis=0)) * taper
+        store_blocked(y, pair, SLOTS * 8, yh_ref, yl_ref)
+
     transfer_part(
-        data_ref, chan_ref, mask_ref, phase_ref, rp_ref, lp_ref, lh_ref, rf_ref, ready,
-        otf_ref, field_ref, slope_ref, inv_ref,
-        line_ref, wide_ref, ph_ref, pl_ref, half_re_ref, half_im_ref, yh_ref, yl_ref,
+        data_ref, chan_ref, mask_ref, phase_ref, rp_ref, lp_ref, lh_ref, ready, spectra,
+        field_ref, slope_ref,
+        line_ref, wide_ref, ph_ref, pl_ref, half_re_ref, half_im_ref, power_ref, yh_ref, yl_ref,
     )
     object_part(
-        width_ref, chan_ref, data_ref, otf_ref, lt_ref, taper_ref, weight_ref, rf_ref, rb_ref,
-        lb_ref, grad_ref, canvas_ref, head_ref, tail_ref,
-        order_ref, sh_ref, sl_ref, spec_ref, object_ref,
+        width_ref, [order_ref[i] for i in range(SLOTS)], weight_ref, rf_ref, rb_ref, lb_ref,
+        grad_ref, inv_ref, canvas_ref, head_ref, tail_ref,
+        yh_ref, yl_ref, plane_ref, object_ref, inner_ref,
     )
 
 
@@ -456,48 +478,62 @@
 
 def gradient_kernel(
     chan_ref, grad_ref, field_ref, slope_ref, inv_ref, phase_ref, rb_ref, lb_ref, rp_ref, lp_ref,
+    sums_ref,
     out_ref,
-    z_ref, qh_ref, ql_ref, pupil_ref,
+    z_ref, back_ref, qh_ref, ql_ref, pupil_ref, total_ref,
 ):
-    cheb = tables()[1]
     right = table_rows(rb_ref)
+    for chunk in range(3):
+        here = slice(chunk * 3, (chunk + 1) * 3)
+        high, low = split(grad_ref[here].reshape(3 * SLOTS * 8, 2 * N))
+        z = dot(jnp.concatenate([high, low, high], axis=1), right)
+        z_ref[here] = z.reshape(3, SLOTS * 8, 2 * N)
+    left = lb_ref[...]
     for pair in range(PAIRS):
-        here = slice(pair * TWO, (pair + 1) * TWO)
-        high, low = split(grad_ref[here, :])
-        z_ref[here, :] = dot(jnp.concatenate([high, low, high], axis=1), right)
-    left_b = lb_ref[...]
+        rows = []
+        for part in range(2):
+            lanes = slice(part * N, (part + 1) * N)
+            for block in range(BLOCKS):
+                at = pair * 16
+                pieces = [z_ref[block, at + 8 * w : at + 8 * w + 8, lanes] for w in range(2)]
+                rows.append(jnp.concatenate(pieces, axis=1))
+        power = dot(left, rows3(jnp.concatenate(rows, axis=0)))
+        field = field_ref[pair]
+        high, low = split(jnp.concatenate([field[:N] * power, field[N:] * power], axis=0))
+        back_ref[pair, : 2 * N] = high
+        back_ref[pair, 2 * N :] = low
     left = table_lanes(rp_ref)
     for pair in range(PAIRS):
-        here = slice(pair * TWO, (pair + 1) * TWO)
-        power = dot(left_b, rows3(swap_halves(z_ref[here, :], HALF)))
-        field = field_ref[pair]
-        back = jnp.concatenate([field[:N] * power, field[N:] * power], axis=0)
-        half = dot(left, rows3(back))
+        high = back_ref[pair, : 2 * N]
+        half = dot(left, jnp.concatenate([high, back_ref[pair, 2 * N :], high], axis=0))
         high, low = split(swap_halves(half, PUP))
         here = slice(pair * N, (pair + 1) * N)
         qh_ref[here, :] = high
         ql_ref[here, :] = low
     right = table_rows(lp_ref)
-    for pair in range(PAIRS):
-        here = slice(pair * N, (pair + 1) * N)
+    for chunk in range(2):
+        here = slice(chunk * 4 * N, (chunk + 1) * 4 * N)
         high = qh_ref[here, :]
         pupil_ref[here, :] = dot(jnp.concatenate([high, ql_ref[here, :], high], axis=1), right)
-    sums = [None] * DEG
-    for row in range(PUP // 2):
+    left = sums_ref[...]
+    for pair in range(PAIRS):
         both = []
-        for at in (row, PUP - 1 - row):
-            q = pupil_ref[pl.ds(at, SLOTS, stride=PUP), :]
-            both.append(q * slope_ref[at * SLOTS : (at + 1) * SLOTS, :])
-        parity = (both[0] + both[1], both[0] - both[1])
-        for i in range(DEG):
-            term = parity[i % 2] * float(cheb[row, i]) if i else parity[0]
-            sums[i] = term if sums[i] is None else sums[i] + term
+        for which in range(2):
+            slot = 2 * pair + which
+            slope = slope_ref[pl.ds(slot, PUP, stride=SLOTS), :]
+            both.append(pupil_ref[slot * PUP : (slot + 1) * PUP, :] * slope)
+        out = dot(left, rows3(jnp.concatenate(both, axis=1)))
+        for which in range(2):
+            here = slice((2 * pair + which) * DEG_ROWS, (2 * pair + which + 1) * DEG_ROWS)
+            total_ref[here, :] = out[:, which * N : (which + 1) * N]
+    sums = [total_ref[pl.ds(i, SLOTS, stride=DEG_ROWS), :] for i in range(DEG)]
     total = lax.dot_general(
         jnp.concatenate(sums, axis=1), phase_ref[...], (((1,), (1,)), ((), ())),
         precision=lax.Precision.HIGHEST, preferred_element_type=f32,
     )
-    factor = 4.0 / float(N * N * N)
-    total = total * (slot_scales(chan_ref, COEF) * factor * inv_ref[:, :COEF])
+    factor = 8.0 * math.pi / float(N * N * N)
+    inverse = inv_ref[pl.ds(0, SLOTS, stride=8), :]
+    total = total * (slot_scales(chan_ref, COEF) * factor * inverse[:, :COEF])
     out_ref[...] = total[:, :ZERN]
 
 
@@ -506,16 +542,15 @@
 
 
 def objects(width, chan, data, mask, tabs, interpret=False):
-    rows = SLOTS * HALF
     margin = jax.ShapeDtypeStruct((CHANNELS + 1, MARGIN, N), f32)
     fixed = [tabs[name] for name in TABLES]
     return pl.pallas_call(
         object_kernel,
         out_shape=(
-            jax.ShapeDtypeStruct((rows, 2 * N), f32),
+            jax.ShapeDtypeStruct((BLOCKS, SLOTS * 8, 2 * N), f32),
             jax.ShapeDtypeStruct((PAIRS, 2 * N, 2 * N), f32),
             jax.ShapeDtypeStruct((PUP * SLOTS, N), f32),
-            jax.ShapeDtypeStruct((SLOTS, N), f32),
+            jax.ShapeDtypeStruct((SLOTS * 8, N), f32),
             jax.ShapeDtypeStruct((CHANNELS + 1, N, N), f32),
             margin,
             margin,
@@ -525,20 +560,19 @@
         scratch_shapes=[pltpu.VMEM(table.shape, bf16) for table in fixed]
         + [
             pltpu.SemaphoreType.DMA((len(TABLES),)),
-            pltpu.VMEM((rows, 2 * N), f32),
             pltpu.VMEM((SLOTS * 8, N), f32),
             pltpu.VMEM((PUP, N), f32),
             pltpu.VMEM((PUP * SLOTS, N), bf16),
             pltpu.VMEM((PUP * SLOTS, N), bf16),
             pltpu.VMEM((PUP * SLOTS, N), f32),
             pltpu.VMEM((PUP * SLOTS, N), f32),
-            pltpu.VMEM((rows, 2 * N), bf16),
-            pltpu.VMEM((rows, 2 * N), bf16),
+            pltpu.VMEM((PAIRS, 2 * N, 2 * N), bf16),
+            pltpu.VMEM((BLOCKS, SLOTS * 16, 2 * N), bf16),
+            pltpu.VMEM((BLOCKS, SLOTS * 16, 2 * N), bf16),
             pltpu.SMEM((SLOTS,), jnp.int32),
-            pltpu.VMEM((rows, 2 * N), bf16),
-            pltpu.VMEM((rows, 2 * N), bf16),
-            pltpu.VMEM((rows, 2 * N), f32),
+            pltpu.VMEM((BLOCKS, SLOTS * 16, 2 * N), f32),
             pltpu.VMEM((TWO, 2 * N), f32),
+            pltpu.VMEM((SLOTS, 8, N), f32),
         ],
         interpret=interpret,
         name="objects",
@@ -550,24 +584,25 @@
 
 
 def gradient(chan, grad, field, slope, inverse, tabs, interpret=False):
-    rows = SLOTS * HALF
     return pl.pallas_call(
         gradient_kernel,
         out_shape=jax.ShapeDtypeStruct((SLOTS, ZERN), f32),
-        in_specs=[SM] + [VM] * 9,
+        in_specs=[SM] + [VM] * 10,
         out_specs=VM,
         scratch_shapes=[
-            pltpu.VMEM((rows, 2 * N), f32),
+            pltpu.VMEM((BLOCKS, SLOTS * 8, 2 * N), f32),
+            pltpu.VMEM((PAIRS, 4 * N, 2 * N), bf16),
             pltpu.VMEM((SLOTS * PUP, 2 * N), bf16),
             pltpu.VMEM((SLOTS * PUP, 2 * N), bf16),
             pltpu.VMEM((SLOTS * PUP, N), f32),
+            pltpu.VMEM((SLOTS * DEG_ROWS, N), f32),
         ],
         interpret=interpret,
         name="gradient",
         compiler_params=limit(16),
     )(
         chan, grad, field, slope, inverse, tabs["phase"], tabs["right_back"], tabs["left_back"],
-        tabs["right_pupil"], tabs["left_pupil"],
+        tabs["right_pupil"], tabs["left_pupil"], tabs["sums"],
     )
 
 

time: 73.4 us -> 70.9 us (0.966)
  Pallas kernels: 14.6 us -> 12 us
    pallas_call x1, Pallas kernels: 8.1 us -> 5.8 us  [objects(): pl.pallas_call(object_kernel, out_shape=(jax.ShapeDtypeStruct((BLOCKS, SL...]
where the time goes in v4:
time: 70.9 us; the launch traced here: 70.5 us
  starting transfers between devices  25 us (35%)
  waiting for transfers between devices  18.1 us (26%)
  blocking collectives  13.2 us (19%)
  Pallas kernels  12 us (17%)
  between operations  1.54 us (2%)
    all_to_all x1, waiting for transfers between devices, per_device(): lax.all_to_all(data, 'patch', split_axis=1, concat_axis=0, tiled=True)  17.2 us
    all_to_all x1, blocking collectives, per_device(): lax.all_to_all(grad.reshape(SLOTS, 1, 1, ZERN), 'patch', split_axis=0, co...  13.2 us
    ppermute x2, starting transfers between devices, shifted(): return lax.ppermute(cells, axis, [(i + 1, i) for i in range(ends)])  11.3 us
    all_to_all x1, starting transfers between devices, per_device(): lax.all_to_all(data, 'patch', split_axis=1, concat_axis=0, tiled=True)  7.8 us
    ppermute x2, starting transfers between devices, shifted(): return lax.ppermute(cells, axis, [(i, i + 1) for i in range(ends)])  5.91 us
    pallas_call x1, Pallas kernels, objects(): pl.pallas_call(object_kernel, out_shape=(jax.ShapeDtypeStruct((BLOCKS, SL...  5.8 us
    pallas_call x1, Pallas kernels, gradient(): pl.pallas_call(gradient_kernel, out_shape=jax.ShapeDtypeStruct((SLOTS, ZE...  3.38 us
    pallas_call x1, Pallas kernels, pack(): pl.pallas_call(pack_kernel, out_shape=jax.ShapeDtypeStruct((SLOTS, ROWS,...  2.02 us
  transfers between devices with their start and end apart: 5, of which 2 were waited for; matrix products, arithmetic and copies ran while one was open for 0% of the time, Pallas kernels for 5%

profile of v4, /device:TPU:7, one launch (start us, length us, event | category | flops | bytes accessed | tf_op | source)
XLA Modules:
  0.0 70.5 jit_solution(2460800935178787370)
XLA Ops:
  0.6 0.0 copy-start.1
  0.6 0.0 copy-start.2
  0.7 0.0 copy-start
  0.7 0.0 copy-start.3
  0.7 0.0 copy-start.4
  0.7 0.0 copy-start.8
  0.7 0.0 copy-start.12
  0.7 0.0 copy-start.6
  0.7 0.0 copy-start.5
  0.7 0.0 copy-start.7
  0.8 0.0 copy-start.11
  0.8 0.0 copy-start.9
  0.8 0.0 copy-start.10
  0.8 2.0 %pack.1 = bf16[16,136,128]{2,1,0:T(8,128)(2,1)} custom-call(f32[16,36]{1,0:T(8,128)} %bitcast.21, s32[2,16]{1,0:T(2,128)} %bitcast.22, bf16[16,128,128]{2,1,0:T(8,128)(2,1)} %bitcast.19), custom_call_target="tpu_custom_call" | custom-call | tf_op jit(solution)/shard_map/pack/pallas_call | solution.py:434
  2.8 7.8 %all-to-all-start = ((bf16[1,16,1,136,128]{4,3,2,0,1:T(8,128)(2,1)}), bf16[1,16,1,136,128]{4,3,2,0,1:T(8,128)(2,1)S(1)}, u32[]{:S(2)}, u32[]{:S(2)}) async-start(bf16[1,16,1,136,128]{4,3,2,0,1:T(8,128)(2,1)} %bitcast.6), calls=%async_computation | async-start | bytes 1114112 | tf_op jit(solution)/shard_map/all_to_all | solution.py:648
  11.3 17.2 %all-to-all-done = bf16[1,16,1,136,128]{4,3,2,0,1:T(8,128)(2,1)S(1)} async-done(((bf16[1,16,1,136,128]{4,3,2,0,1:T(8,128)(2,1)}), bf16[1,16,1,136,128]{4,3,2,0,1:T(8,128)(2,1)S(1)}, u32[]{:S(2)}, u32[]{:S(2)}) %all-to-all-start) | async-done | bytes 557088 | tf_op jit(solution)/shard_map/all_to_all | solution.py:648
  28.5 0.0 copy-done.1
  28.5 0.0 copy-done.2
  28.6 5.8 %objects.1 = (f32[9,128,256]{2,1,0:T(8,128)S(1)}, f32[8,256,256]{2,1,0:T(8,128)S(1)}, f32[1024,128]{1,0:T(8,128)S(1)}, f32[128,128]{1,0:T(8,128)S(1)}, f32[3,128...) custom-call(s32[1]{0:T(128)} %bitcast.16.width_ref, s32[16]{0:T(128)S(1)} %copy-done.11, ...), custom_call_target="tpu_custom_call" | custom-call | tf_op jit(solution)/shard_map/objects/pallas_call | solution.py:547
  34.4 4.0 %collective-permute-start = (f32[3,16,128]{2,1,0:T(8,128)S(1)}, f32[3,16,128]{2,1,0:T(8,128)S(1)}, u32[]{:S(2)}, u32[]{:S(2)}) collective-permute-start(f32[3,16,128]{2,1,0:T(8,128)S(1)} %get-tuple-element.13), channel_id=1, source_target_pairs={{0,16},{16,32},{32,48},{48,64},{64,80},{80,96},{96,112},{112,128},... | collective-permute-start | bytes 73736 | tf_op jit(solution)/shard_map/ppermute | solution.py:639
  38.4 8.9 %collective-permute-start.1 = (f32[3,16,128]{2,1,0:T(8,128)S(1)}, f32[3,16,128]{2,1,0:T(8,128)S(1)}, u32[]{:S(2)}, u32[]{:S(2)}) collective-permute-start(f32[3,16,128]{2,1,0:T(8,128)S(1)} %get-tuple-element.14), channel_id=1, source_target_pairs={{16,0},{32,16},{48,32},{64,48},{80,64},{96,80},{112,96},{128,112},... | collective-permute-start | bytes 73736 | tf_op jit(solution)/shard_map/ppermute | solution.py:640
  47.2 0.0 collective-permute-done.left_ref
  47.3 0.9 %collective-permute-done.1.right_ref = f32[3,16,128]{2,1,0:T(8,128)S(1)} collective-permute-done((f32[3,16,128]{2,1,0:T(8,128)S(1)}, f32[3,16,128]{2,1,0:T(8,128)S(1)}, u32[]{:S(2)}, u32[]{:S(2)}) %collective-permute-start.1) | collective-permute-done | bytes 24608 | tf_op jit(solution)/shard_map/ppermute | solution.py:640
  48.2 0.2 fold.1
  48.4 1.9 %collective-permute-start.2 = (f32[3,16,128]{2,1,0:T(8,128)S(1)}, f32[3,16,128]{2,1,0:T(8,128)S(1)}, u32[]{:S(2)}, u32[]{:S(2)}) collective-permute-start(f32[3,16,128]{2,1,0:T(8,128)S(1)} %get-tuple-element.16), channel_id=1, source_target_pairs={{0,1},{1,2},{2,3},{3,4},{4,5},{5,6},{6,7},{7,8},{8,9},{9,10},{10,1... | collective-permute-start | bytes 73736 | tf_op jit(solution)/shard_map/ppermute | solution.py:639
  50.3 2.4 %collective-permute-start.3 = (f32[3,16,128]{2,1,0:T(8,128)S(1)}, f32[3,16,128]{2,1,0:T(8,128)S(1)}, u32[]{:S(2)}, u32[]{:S(2)}) collective-permute-start(f32[3,16,128]{2,1,0:T(8,128)S(1)} %get-tuple-element.17), channel_id=1, source_target_pairs={{1,0},{2,1},{3,2},{4,3},{5,4},{6,5},{7,6},{8,7},{9,8},{10,9},{11,1... | collective-permute-start | bytes 73736 | tf_op jit(solution)/shard_map/ppermute | solution.py:640
  52.7 3.4 %gradient.1 = f32[16,36]{1,0:T(8,128)S(1)} custom-call(s32[16]{0:T(128)S(1)} %copy-done.11, f32[9,128,256]{2,1,0:T(8,128)S(1)} %get-tuple-element.18.grad_ref, f32[8,256,256]{2,1,0:T(8,128)S(1)} %get-tuple-element.19.field_ref, f32[1024,128]{1,0:T(8,128)S(1)} %get-tuple-element.20.slope_ref, f32[128,128]{1,0:T(8,128)S(1)} %get-tuple-element.21.inv_ref, ...), custom_call_target="tpu_custom_call" | custom-call | tf_op jit(solution)/shard_map/gradient/pallas_call | solution.py:587
  56.1 13.2 %all_to_all.21 = f32[16,1,1,36]{3,2,1,0:T(1,128)S(1)} all-to-all(f32[16,1,1,36]{3,2,1,0:T(1,128)S(1)} %bitcast.18), channel_id=1, replica_groups=mesh['frame'=32,'patch'=16] {'patch'}, dimensions={0} | all-to-all | bytes 4608 | tf_op jit(solution)/shard_map/all_to_all | solution.py:655
  69.3 0.0 collective-permute-done.2.upper_ref
  69.3 0.0 collective-permute-done.3.lower_ref
  69.3 0.7 blend.1
  69.9 0.6 copy.25
  (11 shorter events, 0.0 us)
Async XLA Ops:
  0.6 27.8 %copy-start.1 = (f32[40,1152]{1,0:T(8,128)S(1)}, f32[40,1152]{1,0:T(8,128)}, u32[]{:S(2)}) copy-start(f32[40,1152]{1,0:T(8,128)} %constant.31.clone.phase_ref) | copy-start | bytes 552964
  0.6 27.8 %copy-start.2 = (bf16[128,432]{1,0:T(8,128)(2,1)S(1)}, bf16[128,432]{1,0:T(8,128)(2,1)}, u32[]{:S(2)}) copy-start(bf16[128,432]{1,0:T(8,128)(2,1)} %constant.28.clone.lb_hbm.lb_ref) | copy-start | bytes 331780
  0.7 27.8 %copy-start = (bf16[2,256,256]{2,1,0:T(8,128)(2,1)S(1)}, bf16[2,256,256]{2,1,0:T(8,128)(2,1)}, u32[]{:S(2)}) copy-start(bf16[2,256,256]{2,1,0:T(8,128)(2,1)} %constant.26.clone.rb_hbm.rb_ref) | copy-start | bytes 786436
  0.7 27.8 %copy-start.3 = (bf16[2,256,128]{2,1,0:T(8,128)(2,1)S(1)}, bf16[2,256,128]{2,1,0:T(8,128)(2,1)}, u32[]{:S(2)}) copy-start(bf16[2,256,128]{2,1,0:T(8,128)(2,1)} %constant.23.clone.lp_hbm.lp_ref) | copy-start | bytes 393220
  0.7 27.8 %copy-start.4 = (bf16[2,128,256]{2,1,0:T(8,128)(2,1)S(1)}, bf16[2,128,256]{2,1,0:T(8,128)(2,1)}, u32[]{:S(2)}) copy-start(bf16[2,128,256]{2,1,0:T(8,128)(2,1)} %constant.22.clone.rp_hbm.rp_ref) | copy-start | bytes 393220
  0.7 27.8 %copy-start.8 = (f32[72,128]{1,0:T(8,128)S(1)}, f32[72,128]{1,0:T(8,128)}, u32[]{:S(2)}) copy-start(f32[72,128]{1,0:T(8,128)} %constant.30.clone.weight_ref) | copy-start | bytes 110596
  0.7 27.8 %copy-start.12 = (f32[1,256]{1,0:T(1,128)S(1)}, f32[1,256]{1,0:T(1,128)}, u32[]{:S(2)}) copy-start(f32[1,256]{1,0:T(1,128)} %constant.29.clone.taper_ref) | copy-start | bytes 3076
  0.7 27.8 %copy-start.6 = (bf16[144,256]{1,0:T(8,128)(2,1)S(1)}, bf16[144,256]{1,0:T(8,128)(2,1)}, u32[]{:S(2)}) copy-start(bf16[144,256]{1,0:T(8,128)(2,1)} %constant.27.clone.lt_ref) | copy-start | bytes 221188
  0.7 27.8 %copy-start.5 = (bf16[2,256,256]{2,1,0:T(8,128)(2,1)S(1)}, bf16[2,256,256]{2,1,0:T(8,128)(2,1)}, u32[]{:S(2)}) copy-start(bf16[2,256,256]{2,1,0:T(8,128)(2,1)} %constant.25.clone.rf_hbm) | copy-start | bytes 786436
  0.7 27.8 %copy-start.7 = (bf16[2,144,128]{2,1,0:T(8,128)(2,1)S(1)}, bf16[2,144,128]{2,1,0:T(8,128)(2,1)}, u32[]{:S(2)}) copy-start(bf16[2,144,128]{2,1,0:T(8,128)(2,1)} %constant.24.clone.lh_hbm) | copy-start | bytes 221188
  0.8 27.8 %copy-start.11 = (s32[16]{0:T(128)S(1)}, s32[16]{0:T(128)}, u32[]{:S(2)}) copy-start(s32[16]{0:T(128)} %chan_ref.3) | copy-start | bytes 196
  0.8 27.8 %copy-start.9 = (s32[64,64]{1,0:T(8,128)S(1)}, s32[64,64]{1,0:T(8,128)}, u32[]{:S(2)}) copy-start(s32[64,64]{1,0:T(8,128)} %mask_ref.1) | copy-start | bytes 49156
  0.8 51.9 %copy-start.10 = (bf16[16,192]{1,0:T(8,128)(2,1)S(1)}, bf16[16,192]{1,0:T(8,128)(2,1)}, u32[]{:S(2)}) copy-start(bf16[16,192]{1,0:T(8,128)(2,1)} %constant.32.clone.sums_ref) | copy-start | bytes 18436
  2.8 25.7 %all-to-all-start = ((bf16[1,16,1,136,128]{4,3,2,0,1:T(8,128)(2,1)}), bf16[1,16,1,136,128]{4,3,2,0,1:T(8,128)(2,1)S(1)}, u32[]{:S(2)}, u32[]{:S(2)}) async-start(bf16[1,16,1,136,128]{4,3,2,0,1:T(8,128)(2,1)} %bitcast.6), calls=%async_computation | async-start | bytes 1114112 | tf_op jit(solution)/shard_map/all_to_all | solution.py:648
  34.4 12.9 %collective-permute-start = (f32[3,16,128]{2,1,0:T(8,128)S(1)}, f32[3,16,128]{2,1,0:T(8,128)S(1)}, u32[]{:S(2)}, u32[]{:S(2)}) collective-permute-start(f32[3,16,128]{2,1,0:T(8,128)S(1)} %get-tuple-element.13), channel_id=1, source_target_pairs={{0,16},{16,32},{32,48},{48,64},{64,80},{80,96},{96,112},{112,128},... | collective-permute-start | bytes 73736 | tf_op jit(solution)/shard_map/ppermute | solution.py:639
  38.4 9.8 %collective-permute-start.1 = (f32[3,16,128]{2,1,0:T(8,128)S(1)}, f32[3,16,128]{2,1,0:T(8,128)S(1)}, u32[]{:S(2)}, u32[]{:S(2)}) collective-permute-start(f32[3,16,128]{2,1,0:T(8,128)S(1)} %get-tuple-element.14), channel_id=1, source_target_pairs={{16,0},{32,16},{48,32},{64,48},{80,64},{96,80},{112,96},{128,112},... | collective-permute-start | bytes 73736 | tf_op jit(solution)/shard_map/ppermute | solution.py:640
  48.4 20.9 %collective-permute-start.2 = (f32[3,16,128]{2,1,0:T(8,128)S(1)}, f32[3,16,128]{2,1,0:T(8,128)S(1)}, u32[]{:S(2)}, u32[]{:S(2)}) collective-permute-start(f32[3,16,128]{2,1,0:T(8,128)S(1)} %get-tuple-element.16), channel_id=1, source_target_pairs={{0,1},{1,2},{2,3},{3,4},{4,5},{5,6},{6,7},{7,8},{8,9},{9,10},{10,1... | collective-permute-start | bytes 73736 | tf_op jit(solution)/shard_map/ppermute | solution.py:639
  50.3 19.0 %collective-permute-start.3 = (f32[3,16,128]{2,1,0:T(8,128)S(1)}, f32[3,16,128]{2,1,0:T(8,128)S(1)}, u32[]{:S(2)}, u32[]{:S(2)}) collective-permute-start(f32[3,16,128]{2,1,0:T(8,128)S(1)} %get-tuple-element.17), channel_id=1, source_target_pairs={{1,0},{2,1},{3,2},{4,3},{5,4},{6,5},{7,6},{8,7},{9,8},{10,9},{11,1... | collective-permute-start | bytes 73736 | tf_op jit(solution)/shard_map/ppermute | solution.py:640

commit v5 on v4

--- a/solution.py
+++ b/solution.py
@@ -19,6 +19,7 @@
 CHANNELS = 2
 PER = SLOTS // CHANNELS
 MARGIN = 16
+DEPTH = 8
 TILE = N - 2 * MARGIN
 HALF = 72
 TWO = 2 * HALF
@@ -359,12 +360,12 @@
 
 
 def object_kernel(
-    width_ref, chan_ref, data_ref, mask_ref, phase_ref, lt_ref, taper_ref, weight_ref,
-    rp_hbm, lp_hbm, lh_hbm, rf_hbm, rb_hbm, lb_hbm,
-    grad_ref, field_ref, slope_ref, inv_ref, canvas_ref, head_ref, tail_ref,
+    width_ref, early_ref, chan_ref, data_ref, mask_ref, phase_ref, lt_ref, taper_ref, weight_ref,
+    sums_ref, rp_hbm, lp_hbm, lh_hbm, rf_hbm, rb_hbm, lb_hbm,
+    grad_ref, field_ref, slope_ref, inv_ref, canvas_ref, head_ref, tail_ref, done_ref,
     rp_ref, lp_ref, lh_ref, rf_ref, rb_ref, lb_ref, sems,
     line_ref, wide_ref, ph_ref, pl_ref, half_re_ref, half_im_ref, power_ref, yh_ref, yl_ref,
-    order_ref, plane_ref, object_ref, inner_ref,
+    order_ref, plane_ref, object_ref, inner_ref, *scratch,
 ):
     moves = (
         (rp_hbm, rp_ref), (lp_hbm, lp_ref), (lh_hbm, lh_ref),
@@ -404,15 +405,32 @@
         grad_ref, inv_ref, canvas_ref, head_ref, tail_ref,
         yh_ref, yl_ref, plane_ref, object_ref, inner_ref,
     )
-
-
-def pack_kernel(coef_hbm, shift_hbm, pix_hbm, out_ref, coef_ref, shift_ref, sems):
+    done_ref[...] = jnp.zeros_like(done_ref)
+
+    @pl.when(early_ref[0] == 1)
+    def _():
+        gradient_part(
+            chan_ref, grad_ref, field_ref, slope_ref, inv_ref, phase_ref,
+            rb_ref, lb_ref, rp_ref, lp_ref, sums_ref, done_ref, *scratch,
+        )
+
+
+def pack_kernel(coef_hbm, shift_hbm, pix_hbm, out_hbm, coef_ref, shift_ref, data_ref, sems):
     coef_copy = pltpu.make_async_copy(coef_hbm, coef_ref, sems.at[0])
     shift_copy = pltpu.make_async_copy(shift_hbm, shift_ref, sems.at[1])
-    pix_copy = pltpu.make_async_copy(pix_hbm, out_ref.at[:, :N, :], sems.at[2])
+    chunks = [pl.ds(i * 4, 4) for i in range(4)]
+    loads = [
+        pltpu.make_async_copy(pix_hbm.at[c], data_ref.at[c, :N, :], sems.at[2 + i])
+        for i, c in enumerate(chunks)
+    ]
+    stores = [
+        pltpu.make_async_copy(data_ref.at[c], out_hbm.at[c], sems.at[6 + i])
+        for i, c in enumerate(chunks)
+    ]
     coef_copy.start()
     shift_copy.start()
-    pix_copy.start()
+    for load in loads:
+        load.start()
     coef_copy.wait()
     shift_copy.wait()
     coef = jnp.concatenate([coef_ref[...], jnp.zeros((SLOTS, N - ZERN), f32)], axis=1)
@@ -426,8 +444,12 @@
     line = first + pltpu.roll(second, ZERN, 1) + pltpu.roll(third, 2 * ZERN, 1)
     line = line + pltpu.roll(shift, 3 * ZERN, 1)
     for slot in range(SLOTS):
-        out_ref[slot, N:, :] = jnp.broadcast_to(line[slot : slot + 1], (8, N)).astype(bf16)
-    pix_copy.wait()
+        data_ref[slot, N:, :] = jnp.broadcast_to(line[slot : slot + 1], (8, N)).astype(bf16)
+    for load, store in zip(loads, stores):
+        load.wait()
+        store.start()
+    for store in stores:
+        store.wait()
 
 
 def pack(coef, shift, pixels):
@@ -435,11 +457,12 @@
         pack_kernel,
         out_shape=jax.ShapeDtypeStruct((SLOTS, ROWS, N), bf16),
         in_specs=[HB] * 3,
-        out_specs=VM,
+        out_specs=HB,
         scratch_shapes=[
             pltpu.VMEM((SLOTS, ZERN), f32),
             pltpu.VMEM((2, SLOTS), jnp.int32),
-            pltpu.SemaphoreType.DMA((3,)),
+            pltpu.VMEM((SLOTS, ROWS, N), bf16),
+            pltpu.SemaphoreType.DMA((10,)),
         ],
         name="pack",
         compiler_params=limit(4),
@@ -460,7 +483,9 @@
         tail_ref[layer] = total[N - MARGIN :]
 
 
-def blend_kernel(middle_ref, upper_ref, lower_ref, out_ref):
+def blend_kernel(middle_ref, upper_ref, lower_ref, grad_ref, out_ref, slope_ref):
+    slope_ref[...] = grad_ref[...]
+
     def folded(layer):
         return jnp.concatenate(
             [
@@ -476,7 +501,7 @@
         out_ref[channel] = (folded(channel) / weight)[:, :TILE]
 
 
-def gradient_kernel(
+def gradient_part(
     chan_ref, grad_ref, field_ref, slope_ref, inv_ref, phase_ref, rb_ref, lb_ref, rp_ref, lp_ref,
     sums_ref,
     out_ref,
@@ -537,11 +562,39 @@
     out_ref[...] = total[:, :ZERN]
 
 
+def gradient_kernel(
+    early_ref, chan_ref, done_ref, grad_ref, field_ref, slope_ref, inv_ref, phase_ref,
+    rb_ref, lb_ref, rp_ref, lp_ref, sums_ref,
+    out_ref,
+    *scratch,
+):
+    @pl.when(early_ref[0] == 1)
+    def _():
+        out_ref[...] = done_ref[...]
+
+    @pl.when(early_ref[0] == 0)
+    def _():
+        gradient_part(
+            chan_ref, grad_ref, field_ref, slope_ref, inv_ref, phase_ref,
+            rb_ref, lb_ref, rp_ref, lp_ref, sums_ref, out_ref, *scratch,
+        )
+
+
+GRADIENT_SCRATCH = (
+    ((BLOCKS, SLOTS * 8, 2 * N), f32),
+    ((PAIRS, 4 * N, 2 * N), bf16),
+    ((SLOTS * PUP, 2 * N), bf16),
+    ((SLOTS * PUP, 2 * N), bf16),
+    ((SLOTS * PUP, N), f32),
+    ((SLOTS * DEG_ROWS, N), f32),
+)
+
+
 def limit(mib):
     return pltpu.CompilerParams(vmem_limit_bytes=mib << 20)
 
 
-def objects(width, chan, data, mask, tabs, interpret=False):
+def objects(width, early, chan, data, mask, tabs, interpret=False):
     margin = jax.ShapeDtypeStruct((CHANNELS + 1, MARGIN, N), f32)
     fixed = [tabs[name] for name in TABLES]
     return pl.pallas_call(
@@ -554,9 +607,10 @@
             jax.ShapeDtypeStruct((CHANNELS + 1, N, N), f32),
             margin,
             margin,
+            jax.ShapeDtypeStruct((SLOTS, ZERN), f32),
         ),
-        in_specs=[SM, SM] + [VM] * 6 + [HB] * len(TABLES),
-        out_specs=(VM,) * 7,
+        in_specs=[SM] * 3 + [VM] * 7 + [HB] * len(TABLES),
+        out_specs=(VM,) * 8,
         scratch_shapes=[pltpu.VMEM(table.shape, bf16) for table in fixed]
         + [
             pltpu.SemaphoreType.DMA((len(TABLES),)),
@@ -573,36 +627,30 @@
             pltpu.VMEM((BLOCKS, SLOTS * 16, 2 * N), f32),
             pltpu.VMEM((TWO, 2 * N), f32),
             pltpu.VMEM((SLOTS, 8, N), f32),
-        ],
+        ]
+        + [pltpu.VMEM(*piece) for piece in GRADIENT_SCRATCH],
         interpret=interpret,
         name="objects",
-        compiler_params=limit(16),
+        compiler_params=limit(22),
     )(
-        width, chan, data, mask, tabs["phase"], tabs["left_taper"], tabs["taper"], tabs["weight"],
-        *fixed,
-    )
-
-
-def gradient(chan, grad, field, slope, inverse, tabs, interpret=False):
+        width, early, chan, data, mask, tabs["phase"], tabs["left_taper"], tabs["taper"],
+        tabs["weight"], tabs["sums"], *fixed,
+    )
+
+
+def gradient(early, chan, done, grad, field, slope, inverse, tabs, interpret=False):
     return pl.pallas_call(
         gradient_kernel,
         out_shape=jax.ShapeDtypeStruct((SLOTS, ZERN), f32),
-        in_specs=[SM] + [VM] * 10,
+        in_specs=[SM, SM] + [VM] * 11,
         out_specs=VM,
-        scratch_shapes=[
-            pltpu.VMEM((BLOCKS, SLOTS * 8, 2 * N), f32),
-            pltpu.VMEM((PAIRS, 4 * N, 2 * N), bf16),
-            pltpu.VMEM((SLOTS * PUP, 2 * N), bf16),
-            pltpu.VMEM((SLOTS * PUP, 2 * N), bf16),
-            pltpu.VMEM((SLOTS * PUP, N), f32),
-            pltpu.VMEM((SLOTS * DEG_ROWS, N), f32),
-        ],
+        scratch_shapes=[pltpu.VMEM(*piece) for piece in GRADIENT_SCRATCH],
         interpret=interpret,
         name="gradient",
         compiler_params=limit(16),
     )(
-        chan, grad, field, slope, inverse, tabs["phase"], tabs["right_back"], tabs["left_back"],
-        tabs["right_pupil"], tabs["left_pupil"], tabs["sums"],
+        early, chan, done, grad, field, slope, inverse, tabs["phase"], tabs["right_back"],
+        tabs["left_back"], tabs["right_pupil"], tabs["left_pupil"], tabs["sums"],
     )
 
 
@@ -622,15 +670,18 @@
     )(canvas, left, right)
 
 
-def blend(middle, upper, lower):
+def blend(middle, upper, lower, grad):
     return pl.pallas_call(
         blend_kernel,
-        out_shape=jax.ShapeDtypeStruct((CHANNELS, TILE, TILE), f32),
-        in_specs=[VM] * 3,
-        out_specs=VM,
+        out_shape=(
+            jax.ShapeDtypeStruct((CHANNELS, TILE, TILE), f32),
+            jax.ShapeDtypeStruct((SLOTS, ZERN), f32),
+        ),
+        in_specs=[VM] * 4,
+        out_specs=(VM,) * 2,
         name="blend",
         compiler_params=limit(8),
-    )(middle, upper, lower)
+    )(middle, upper, lower, grad)
 
 
 def shifted(cells, axis, forward):
@@ -646,20 +697,21 @@
     shift = shifts.reshape(SLOTS, 2).T
     data = pack(coef, shift, pixels.reshape(SLOTS, N, N)).reshape(1, SLOTS, 1, ROWS, N)
     data = lax.all_to_all(data, "patch", split_axis=1, concat_axis=0, tiled=True)
-    grad, field, slope, inverse, canvas, head, tail = objects(
-        intersection.reshape(1), chan_map, data.reshape(SLOTS, ROWS, N), pupil_mask, tabs
+    early = ((lax.axis_index("frame") % DEPTH) == 0).astype(jnp.int32).reshape(1)
+    grad, field, slope, inverse, canvas, head, tail, done = objects(
+        intersection.reshape(1), early, chan_map, data.reshape(SLOTS, ROWS, N), pupil_mask, tabs
     )
     left = shifted(tail, "frame", True)
     right = shifted(head, "frame", False)
-    grad = gradient(chan_map, grad, field, slope, inverse, tabs)
+    grad = gradient(early, chan_map, done, grad, field, slope, inverse, tabs)
     grad = lax.all_to_all(
         grad.reshape(SLOTS, 1, 1, ZERN), "patch", split_axis=0, concat_axis=1, tiled=True
     )
     middle, head, tail = fold(canvas, left, right)
     upper = shifted(tail, "patch", True)
     lower = shifted(head, "patch", False)
-    blended = blend(middle, upper, lower)
-    return (blended, grad)
+    blended, grad = blend(middle, upper, lower, grad.reshape(SLOTS, ZERN))
+    return (blended, grad.reshape(coeffs.shape))
 
 
 def solution(mesh):

time: 70.9 us -> 68.1 us (0.961)
  starting transfers between devices: 25 us -> 22.1 us
    pallas_call x1, Pallas kernels: 5.8 us -> 8.71 us  [objects(): pl.pallas_call(object_kernel, out_shape=(jax.ShapeDtypeStruct((BLOCKS, SL...]
    pallas_call x1, Pallas kernels: 3.38 us -> 0.56 us  [gradient(): pl.pallas_call(gradient_kernel, out_shape=jax.ShapeDtypeStruct((SLOTS, ZE...]
    ppermute x2, starting transfers between devices: 5.91 us -> 3.84 us  [shifted(): return lax.ppermute(cells, axis, [(i, i + 1) for i in range(ends)])]
    ppermute x2, starting transfers between devices: 11.3 us -> 10.5 us  [shifted(): return lax.ppermute(cells, axis, [(i + 1, i) for i in range(ends)])]
  transfers between devices with their start and end apart: 5 -> 5, of which waited for: 2 -> 2; matrix products, arithmetic and copies ran while one was open for 0% -> 0% of each run, Pallas kernels for 5% -> 1%
where the time goes in v5:
time: 68.1 us; the launch traced here: 67.1 us
  starting transfers between devices  22.1 us (32%)
  waiting for transfers between devices  18.1 us (27%)
  blocking collectives  13.2 us (19%)
  Pallas kernels  12.1 us (18%)
  between operations  1.54 us (2%)
    all_to_all x1, waiting for transfers between devices, per_device(): lax.all_to_all(data, 'patch', split_axis=1, concat_axis=0, tiled=True)  17.2 us
    all_to_all x1, blocking collectives, per_device(): lax.all_to_all(grad.reshape(SLOTS, 1, 1, ZERN), 'patch', split_axis=0, co...  13.2 us
    ppermute x2, starting transfers between devices, shifted(): return lax.ppermute(cells, axis, [(i + 1, i) for i in range(ends)])  10.5 us
    pallas_call x1, Pallas kernels, objects(): pl.pallas_call(object_kernel, out_shape=(jax.ShapeDtypeStruct((BLOCKS, SL...  8.71 us
    all_to_all x1, starting transfers between devices, per_device(): lax.all_to_all(data, 'patch', split_axis=1, concat_axis=0, tiled=True)  7.8 us
    ppermute x2, starting transfers between devices, shifted(): return lax.ppermute(cells, axis, [(i, i + 1) for i in range(ends)])  3.84 us
    pallas_call x1, Pallas kernels, pack(): pl.pallas_call(pack_kernel, out_shape=jax.ShapeDtypeStruct((SLOTS, ROWS,...  1.97 us
  transfers between devices with their start and end apart: 5, of which 2 were waited for; matrix products, arithmetic and copies ran while one was open for 0% of the time, Pallas kernels for 1%

profile of v5, /device:TPU:7, one launch (start us, length us, event | category | flops | bytes accessed | tf_op | source)
XLA Modules:
  0.0 67.1 jit_solution(12158041221729665274)
XLA Ops:
  0.6 0.0 copy-start.10
  0.6 0.0 copy-start.1
  0.7 0.0 copy-start.2
  0.7 0.0 copy-start
  0.7 0.0 copy-start.3
  0.7 0.0 copy-start.4
  0.7 0.0 copy-start.8
  0.7 0.0 copy-start.12
  0.7 0.0 copy-start.6
  0.7 0.0 copy-start.5
  0.8 0.0 copy-start.7
  0.8 0.0 copy-start.11
  0.8 0.0 copy-start.9
  0.8 2.0 %pack.1 = bf16[16,136,128]{2,1,0:T(8,128)(2,1)} custom-call(f32[16,36]{1,0:T(8,128)} %bitcast.23, s32[2,16]{1,0:T(2,128)} %bitcast.24, bf16[16,128,128]{2,1,0:T(8,128)(2,1)} %bitcast.22), custom_call_target="tpu_custom_call" | custom-call | tf_op jit(solution)/shard_map/pack/pallas_call | solution.py:456
  2.8 7.8 %all-to-all-start = ((bf16[1,16,1,136,128]{4,3,2,0,1:T(8,128)(2,1)}), bf16[1,16,1,136,128]{4,3,2,0,1:T(8,128)(2,1)S(1)}, u32[]{:S(2)}, u32[]{:S(2)}) async-start(bf16[1,16,1,136,128]{4,3,2,0,1:T(8,128)(2,1)} %bitcast.7), calls=%async_computation | async-start | bytes 1114112 | tf_op jit(solution)/shard_map/all_to_all | solution.py:699
  11.2 17.2 %all-to-all-done = bf16[1,16,1,136,128]{4,3,2,0,1:T(8,128)(2,1)S(1)} async-done(((bf16[1,16,1,136,128]{4,3,2,0,1:T(8,128)(2,1)}), bf16[1,16,1,136,128]{4,3,2,0,1:T(8,128)(2,1)S(1)}, u32[]{:S(2)}, u32[]{:S(2)}) %all-to-all-start) | async-done | bytes 557088 | tf_op jit(solution)/shard_map/all_to_all | solution.py:699
  28.4 0.0 copy-done.10
  28.4 0.0 copy-done.1
  28.4 0.0 copy-done.2
  28.5 8.7 %objects.1 = (f32[9,128,256]{2,1,0:T(8,128)S(1)}, f32[8,256,256]{2,1,0:T(8,128)S(1)}, f32[1024,128]{1,0:T(8,128)S(1)}, f32[128,128]{1,0:T(8,128)S(1)}, f32[3,128...) custom-call(s32[1]{0:T(128)} %bitcast.18.width_ref, ...), custom_call_target="tpu_custom_call" | custom-call | tf_op jit(solution)/shard_map/objects/pallas_call | solution.py:600
  37.3 1.9 %collective-permute-start = (f32[3,16,128]{2,1,0:T(8,128)S(1)}, f32[3,16,128]{2,1,0:T(8,128)S(1)}, u32[]{:S(2)}, u32[]{:S(2)}) collective-permute-start(f32[3,16,128]{2,1,0:T(8,128)S(1)} %get-tuple-element.16), channel_id=1, source_target_pairs={{0,16},{16,32},{32,48},{48,64},{64,80},{80,96},{96,112},{112,128},... | collective-permute-start | bytes 73736 | tf_op jit(solution)/shard_map/ppermute | solution.py:690
  39.2 8.1 %collective-permute-start.1 = (f32[3,16,128]{2,1,0:T(8,128)S(1)}, f32[3,16,128]{2,1,0:T(8,128)S(1)}, u32[]{:S(2)}, u32[]{:S(2)}) collective-permute-start(f32[3,16,128]{2,1,0:T(8,128)S(1)} %get-tuple-element.17), channel_id=1, source_target_pairs={{16,0},{32,16},{48,32},{64,48},{80,64},{96,80},{112,96},{128,112},... | collective-permute-start | bytes 73736 | tf_op jit(solution)/shard_map/ppermute | solution.py:691
  47.2 0.0 collective-permute-done.left_ref
  47.3 0.9 %collective-permute-done.1.right_ref = f32[3,16,128]{2,1,0:T(8,128)S(1)} collective-permute-done((f32[3,16,128]{2,1,0:T(8,128)S(1)}, f32[3,16,128]{2,1,0:T(8,128)S(1)}, u32[]{:S(2)}, u32[]{:S(2)}) %collective-permute-start.1) | collective-permute-done | bytes 24608 | tf_op jit(solution)/shard_map/ppermute | solution.py:691
  48.2 0.2 fold.1
  48.4 1.9 %collective-permute-start.2 = (f32[3,16,128]{2,1,0:T(8,128)S(1)}, f32[3,16,128]{2,1,0:T(8,128)S(1)}, u32[]{:S(2)}, u32[]{:S(2)}) collective-permute-start(f32[3,16,128]{2,1,0:T(8,128)S(1)} %get-tuple-element.19), channel_id=1, source_target_pairs={{0,1},{1,2},{2,3},{3,4},{4,5},{5,6},{6,7},{7,8},{8,9},{9,10},{10,1... | collective-permute-start | bytes 73736 | tf_op jit(solution)/shard_map/ppermute | solution.py:690
  50.3 2.4 %collective-permute-start.3 = (f32[3,16,128]{2,1,0:T(8,128)S(1)}, f32[3,16,128]{2,1,0:T(8,128)S(1)}, u32[]{:S(2)}, u32[]{:S(2)}) collective-permute-start(f32[3,16,128]{2,1,0:T(8,128)S(1)} %get-tuple-element.20), channel_id=1, source_target_pairs={{1,0},{2,1},{3,2},{4,3},{5,4},{6,5},{7,6},{8,7},{9,8},{10,9},{11,1... | collective-permute-start | bytes 73736 | tf_op jit(solution)/shard_map/ppermute | solution.py:691
  52.7 0.6 gradient.1
  53.3 13.2 %all_to_all.8 = f32[16,1,1,36]{3,2,1,0:T(1,128)S(1)} all-to-all(f32[16,1,1,36]{3,2,1,0:T(1,128)S(1)} %bitcast.20), channel_id=1, replica_groups=mesh['frame'=32,'patch'=16] {'patch'}, dimensions={0} | all-to-all | bytes 4608 | tf_op jit(solution)/shard_map/all_to_all | solution.py:707
  66.4 0.0 collective-permute-done.2.upper_ref
  66.4 0.0 collective-permute-done.3.lower_ref
  66.4 0.7 blend.1
  (10 shorter events, 0.0 us)
Async XLA Ops:
  0.6 27.8 %copy-start.10 = (bf16[16,192]{1,0:T(8,128)(2,1)S(1)}, bf16[16,192]{1,0:T(8,128)(2,1)}, u32[]{:S(2)}) copy-start(bf16[16,192]{1,0:T(8,128)(2,1)} %constant.52.clone.sums_ref) | copy-start | bytes 18436
  0.6 27.8 %copy-start.1 = (f32[40,1152]{1,0:T(8,128)S(1)}, f32[40,1152]{1,0:T(8,128)}, u32[]{:S(2)}) copy-start(f32[40,1152]{1,0:T(8,128)} %constant.51.clone.phase_ref) | copy-start | bytes 552964
  0.7 27.8 %copy-start.2 = (bf16[128,432]{1,0:T(8,128)(2,1)S(1)}, bf16[128,432]{1,0:T(8,128)(2,1)}, u32[]{:S(2)}) copy-start(bf16[128,432]{1,0:T(8,128)(2,1)} %constant.48.clone.lb_hbm.lb_ref) | copy-start | bytes 331780
  0.7 27.8 %copy-start = (bf16[2,256,256]{2,1,0:T(8,128)(2,1)S(1)}, bf16[2,256,256]{2,1,0:T(8,128)(2,1)}, u32[]{:S(2)}) copy-start(bf16[2,256,256]{2,1,0:T(8,128)(2,1)} %constant.46.clone.rb_hbm.rb_ref) | copy-start | bytes 786436
  0.7 27.8 %copy-start.3 = (bf16[2,256,128]{2,1,0:T(8,128)(2,1)S(1)}, bf16[2,256,128]{2,1,0:T(8,128)(2,1)}, u32[]{:S(2)}) copy-start(bf16[2,256,128]{2,1,0:T(8,128)(2,1)} %constant.43.clone.lp_hbm.lp_ref) | copy-start | bytes 393220
  0.7 27.8 %copy-start.4 = (bf16[2,128,256]{2,1,0:T(8,128)(2,1)S(1)}, bf16[2,128,256]{2,1,0:T(8,128)(2,1)}, u32[]{:S(2)}) copy-start(bf16[2,128,256]{2,1,0:T(8,128)(2,1)} %constant.42.clone.rp_hbm.rp_ref) | copy-start | bytes 393220
  0.7 27.8 %copy-start.8 = (f32[72,128]{1,0:T(8,128)S(1)}, f32[72,128]{1,0:T(8,128)}, u32[]{:S(2)}) copy-start(f32[72,128]{1,0:T(8,128)} %constant.50.clone.weight_ref) | copy-start | bytes 110596
  0.7 27.8 %copy-start.12 = (f32[1,256]{1,0:T(1,128)S(1)}, f32[1,256]{1,0:T(1,128)}, u32[]{:S(2)}) copy-start(f32[1,256]{1,0:T(1,128)} %constant.49.clone.taper_ref) | copy-start | bytes 3076
  0.7 27.8 %copy-start.6 = (bf16[144,256]{1,0:T(8,128)(2,1)S(1)}, bf16[144,256]{1,0:T(8,128)(2,1)}, u32[]{:S(2)}) copy-start(bf16[144,256]{1,0:T(8,128)(2,1)} %constant.47.clone.lt_ref) | copy-start | bytes 221188
  0.7 27.7 %copy-start.5 = (bf16[2,256,256]{2,1,0:T(8,128)(2,1)S(1)}, bf16[2,256,256]{2,1,0:T(8,128)(2,1)}, u32[]{:S(2)}) copy-start(bf16[2,256,256]{2,1,0:T(8,128)(2,1)} %constant.45.clone.rf_hbm) | copy-start | bytes 786436
  0.8 27.7 %copy-start.7 = (bf16[2,144,128]{2,1,0:T(8,128)(2,1)S(1)}, bf16[2,144,128]{2,1,0:T(8,128)(2,1)}, u32[]{:S(2)}) copy-start(bf16[2,144,128]{2,1,0:T(8,128)(2,1)} %constant.44.clone.lh_hbm) | copy-start | bytes 221188
  0.8 27.7 %copy-start.11 = (s32[16]{0:T(128)S(1)}, s32[16]{0:T(128)}, u32[]{:S(2)}) copy-start(s32[16]{0:T(128)} %chan_ref.3) | copy-start | bytes 196
  0.8 27.7 %copy-start.9 = (s32[64,64]{1,0:T(8,128)S(1)}, s32[64,64]{1,0:T(8,128)}, u32[]{:S(2)}) copy-start(s32[64,64]{1,0:T(8,128)} %mask_ref.1) | copy-start | bytes 49156
  2.8 25.7 %all-to-all-start = ((bf16[1,16,1,136,128]{4,3,2,0,1:T(8,128)(2,1)}), bf16[1,16,1,136,128]{4,3,2,0,1:T(8,128)(2,1)S(1)}, u32[]{:S(2)}, u32[]{:S(2)}) async-start(bf16[1,16,1,136,128]{4,3,2,0,1:T(8,128)(2,1)} %bitcast.7), calls=%async_computation | async-start | bytes 1114112 | tf_op jit(solution)/shard_map/all_to_all | solution.py:699
  37.3 10.0 %collective-permute-start = (f32[3,16,128]{2,1,0:T(8,128)S(1)}, f32[3,16,128]{2,1,0:T(8,128)S(1)}, u32[]{:S(2)}, u32[]{:S(2)}) collective-permute-start(f32[3,16,128]{2,1,0:T(8,128)S(1)} %get-tuple-element.16), channel_id=1, source_target_pairs={{0,16},{16,32},{32,48},{48,64},{64,80},{80,96},{96,112},{112,128},... | collective-permute-start | bytes 73736 | tf_op jit(solution)/shard_map/ppermute | solution.py:690
  39.2 9.0 %collective-permute-start.1 = (f32[3,16,128]{2,1,0:T(8,128)S(1)}, f32[3,16,128]{2,1,0:T(8,128)S(1)}, u32[]{:S(2)}, u32[]{:S(2)}) collective-permute-start(f32[3,16,128]{2,1,0:T(8,128)S(1)} %get-tuple-element.17), channel_id=1, source_target_pairs={{16,0},{32,16},{48,32},{64,48},{80,64},{96,80},{112,96},{128,112},... | collective-permute-start | bytes 73736 | tf_op jit(solution)/shard_map/ppermute | solution.py:691
  48.4 18.1 %collective-permute-start.2 = (f32[3,16,128]{2,1,0:T(8,128)S(1)}, f32[3,16,128]{2,1,0:T(8,128)S(1)}, u32[]{:S(2)}, u32[]{:S(2)}) collective-permute-start(f32[3,16,128]{2,1,0:T(8,128)S(1)} %get-tuple-element.19), channel_id=1, source_target_pairs={{0,1},{1,2},{2,3},{3,4},{4,5},{5,6},{6,7},{7,8},{8,9},{9,10},{10,1... | collective-permute-start | bytes 73736 | tf_op jit(solution)/shard_map/ppermute | solution.py:690
  50.3 16.2 %collective-permute-start.3 = (f32[3,16,128]{2,1,0:T(8,128)S(1)}, f32[3,16,128]{2,1,0:T(8,128)S(1)}, u32[]{:S(2)}, u32[]{:S(2)}) collective-permute-start(f32[3,16,128]{2,1,0:T(8,128)S(1)} %get-tuple-element.20), channel_id=1, source_target_pairs={{1,0},{2,1},{3,2},{4,3},{5,4},{6,5},{7,6},{8,7},{9,8},{10,9},{11,1... | collective-permute-start | bytes 73736 | tf_op jit(solution)/shard_map/ppermute | solution.py:691
